TPU v7x, 32 devices: a whole 2x2x4 slice. The times are simulated.
32 devices in a mesh: grp: 2 (over y), row: 8 (over z, x), col: 2 (over core).
Axes of the slice: x: 2, y: 2, z: 4, core: 2. Of those that a mesh axis runs over, the one named last changes fastest.
Arguments:
- features: bfloat16 [128, 128, 256], P(('grp', 'row'), 'col'), parts along dimension 0, may hold values from -6 to 6
- cotangent: bfloat16 [128, 128, 256], P(('grp', 'row'), 'col'), parts along dimension 0, may hold values from -6 to 6
- domain: int32 [128, 128], P(('grp', 'row'), 'col'), parts along dimension 0, may hold values 0 or 1
- qkv_weight: bfloat16 [256, 768], replicated, may hold values from -6 to 6
- proj_weight: bfloat16 [256, 256], replicated, may hold values from -0.375 to 0.375
- norm_gain: float32 [256], replicated, may hold values from 0.5 to 1.5
Outputs:
- updated: bfloat16 [128, 128, 256], P(('grp', 'row'), 'col'), parts along dimension 0
- grad_features: bfloat16 [128, 128, 256], P(('grp', 'row'), 'col'), parts along dimension 0
- grad_qkv: float32 [512, 768], P('grp'), parts along dimension 0
- grad_proj: float32 [512, 256], P('grp'), parts along dimension 0
- grad_gain: float32 [512], P('grp'), parts along dimension 0
There are 2 independent parts, one for each index of `grp`. A program takes and returns all parts, laid end to end along the dimension named above; an argument that names none is the same for every part. Nothing has to cross between parts.
All inputs are finite; a program needn't handle non-finite values. No bound on the sum of `domain` on one device may be relied on, other than what follows from the above.
Results may differ from a plain program's by a relative error of at most 0.013.
Values may be sent and summed in bfloat16 or wider, within the bound.
No kernel may reach another device: no remote copies, remote signals or barrier semaphores. Data moves between devices by JAX's collectives and lax.ppermute only.
A program may use at most 64 MiB of HBM per device.

v0:
```python
import jax
import jax.numpy as jnp
from jax import lax
from jax.sharding import PartitionSpec as P

HEADS = 8
WIN = 8
SHIFT = 4


NORM_EPSILON = 1e-05
MASKED_SCORE = -1e30


def from_behind(array, axis, by):
    peers = lax.axis_size(axis)
    return lax.ppermute(array, axis, [(i, (i + by) % peers) for i in range(peers)])


def layer_norm(values, norm_gain):
    average = jnp.mean(values, -1, keepdims=True)
    centred = values - average
    variance = jnp.mean(centred * centred, -1, keepdims=True)
    return centred * lax.rsqrt(variance + NORM_EPSILON) * norm_gain


def region_of(cell_ids, extent):
    return (cell_ids >= extent - WIN).astype(jnp.int32) + (cell_ids >= extent - SHIFT).astype(
        jnp.int32
    )


def region_labels(row_start, tile_rows, total_rows, col_start, tile_cols, total_cols):
    row_ids = row_start + jnp.arange(tile_rows, dtype=jnp.int32)
    col_ids = col_start + jnp.arange(tile_cols, dtype=jnp.int32)
    return region_of(row_ids, total_rows)[:, None] * 3 + region_of(col_ids, total_cols)[None, :]


def contract_rows(left, right):
    return lax.dot_general(
        left, right, (((0,), (0,)), ((), ())), preferred_element_type=jnp.float32
    )


def contract_cols(left, right):
    return lax.dot_general(
        left, right, (((1,), (1,)), ((), ())), preferred_element_type=jnp.float32
    )


def window_core(projected, labels):
    tile_rows, tile_cols, triple = projected.shape
    channels = triple // 3
    windows = tile_cols // WIN
    head_dim = channels // HEADS
    grouped = (
        projected.reshape(tile_rows, windows, WIN, triple)
        .transpose(1, 0, 2, 3)
        .reshape(windows, tile_rows * WIN, triple)
    )
    grouped_labels = (
        labels.reshape(tile_rows, windows, WIN).transpose(1, 0, 2).reshape(windows, tile_rows * WIN)
    )
    query_part = grouped[:, :, :channels].reshape(windows, -1, HEADS, head_dim)
    key_part = grouped[:, :, channels : 2 * channels].reshape(windows, -1, HEADS, head_dim)
    value_part = grouped[:, :, 2 * channels :].reshape(windows, -1, HEADS, head_dim)
    scores = jnp.einsum("wqhd,wkhd->whqk", query_part, key_part) * head_dim ** (-0.5)
    allowed = (grouped_labels[:, :, None] == grouped_labels[:, None, :])[:, None]
    scores = jnp.where(allowed, scores, MASKED_SCORE)
    peak = lax.stop_gradient(jnp.max(scores, -1, keepdims=True))
    weights = jnp.exp(scores - peak)
    probability = weights / jnp.sum(weights, -1, keepdims=True)
    probability = lax.optimization_barrier(probability.astype(jnp.bfloat16)).astype(jnp.float32)
    context = jnp.einsum("whqk,wkhd->wqhd", probability, value_part)
    context = (
        context.reshape(windows, tile_rows, WIN, channels)
        .transpose(1, 0, 2, 3)
        .reshape(tile_rows, tile_cols, channels)
    )
    return context.astype(jnp.bfloat16)


def forward_block(shifted, labels, qkv_weight, proj_weight):
    tile_rows, tile_cols, channels = shifted.shape
    flat_rows = shifted.reshape(-1, channels)
    projected = jnp.dot(flat_rows, qkv_weight, preferred_element_type=jnp.float32).astype(
        jnp.bfloat16
    )
    projected = projected.reshape(tile_rows, tile_cols, 3 * channels)
    context = window_core(projected.astype(jnp.float32), labels)
    attended = jnp.dot(
        context.reshape(-1, channels), proj_weight, preferred_element_type=jnp.float32
    ).astype(jnp.bfloat16)
    return (projected, context, attended.reshape(shifted.shape))


def backward_block(shifted, labels, projected, context, dattended, qkv_weight, proj_weight):
    channels = shifted.shape[-1]
    grad_rows = dattended.reshape(-1, channels)
    grad_proj = contract_rows(context.reshape(-1, channels), grad_rows)
    dcontext = contract_cols(grad_rows, proj_weight).astype(jnp.bfloat16).reshape(context.shape)

    def core_only(values):
        return window_core(values, labels)

    _, pullback = jax.vjp(core_only, projected.astype(jnp.float32))
    dprojected = pullback(dcontext)[0].astype(jnp.bfloat16).reshape(-1, 3 * channels)
    grad_qkv = contract_rows(shifted.reshape(-1, channels), dprojected)
    dshifted = contract_cols(dprojected, qkv_weight).astype(jnp.bfloat16).reshape(shifted.shape)
    return (grad_qkv, grad_proj, dshifted)


def norm_backward(values, norm_gain, dnormed):

    def apply_norm(inputs):
        return layer_norm(inputs, norm_gain)

    _, pullback = jax.vjp(apply_norm, values)
    upstream = dnormed.astype(jnp.float32)
    grad_values = pullback(upstream)[0]
    standard = layer_norm(values, jnp.ones_like(norm_gain))
    grad_gain = jnp.sum((upstream * standard).reshape(-1, values.shape[-1]), 0)
    return (grad_values, grad_gain)


def roll_ahead(tile):
    upper_rows = from_behind(tile[:SHIFT], "row", -1)
    rolled = jnp.concatenate([tile[SHIFT:], upper_rows], 0)
    left_cols = from_behind(rolled[:, :SHIFT], "col", -1)
    return jnp.concatenate([rolled[:, SHIFT:], left_cols], 1)


def roll_behind(tile):
    lower_rows = from_behind(tile[-SHIFT:], "row", 1)
    rolled = jnp.concatenate([lower_rows, tile[:-SHIFT]], 0)
    right_cols = from_behind(rolled[:, -SHIFT:], "col", 1)
    return jnp.concatenate([right_cols, rolled[:, :-SHIFT]], 1)


def on_device(features, cotangent, domain, qkv_weight, proj_weight, norm_gain):
    tile_rows, tile_cols, channels = features.shape
    values = features.astype(jnp.float32)
    normed = layer_norm(values, norm_gain).astype(jnp.bfloat16)
    masked_grad = cotangent * domain.astype(jnp.bfloat16)[..., None]
    inside = domain.astype(jnp.float32)[..., None]
    labels = region_labels(
        lax.axis_index("row") * tile_rows,
        tile_rows,
        tile_rows * lax.axis_size("row"),
        lax.axis_index("col") * tile_cols,
        tile_cols,
        tile_cols * lax.axis_size("col"),
    )
    shifted = roll_ahead(normed)
    projected, context, attended = forward_block(shifted, labels, qkv_weight, proj_weight)
    updated = (values + inside * roll_behind(attended).astype(jnp.float32)).astype(jnp.bfloat16)
    dattended = roll_ahead(masked_grad)
    part_qkv, part_proj, dshifted = backward_block(
        shifted, labels, projected, context, dattended, qkv_weight, proj_weight
    )
    dnormed = roll_behind(dshifted)
    grad_values, part_gain = norm_backward(values, norm_gain, dnormed)
    grad_features = (cotangent.astype(jnp.float32) + grad_values).astype(jnp.bfloat16)
    chip_sums = (
        lax.psum(part_qkv.astype(jnp.bfloat16), "col").astype(jnp.float32),
        lax.psum(part_proj.astype(jnp.bfloat16), "col").astype(jnp.float32),
        lax.psum(part_gain.astype(jnp.bfloat16), "col").astype(jnp.float32),
    )
    grad_qkv, grad_proj, grad_gain = lax.psum((chip_sums[0], chip_sums[1], chip_sums[2]), "row")
    return (updated, grad_features, grad_qkv, grad_proj, grad_gain)


def solution(mesh):
    return jax.shard_map(
        on_device,
        mesh=mesh,
        in_specs=(
            P(("grp", "row"), "col", None),
            P(("grp", "row"), "col", None),
            P(("grp", "row"), "col"),
            P(),
            P(),
            P(),
        ),
        out_specs=(
            P(("grp", "row"), "col", None),
            P(("grp", "row"), "col", None),
            P("grp", None),
            P("grp", None),
            P("grp"),
        ),
        check_vma=False,
    )
```

profile of v0, /device:TPU:0, one launch (start us, length us, event | category | flops | bytes accessed | tf_op | source)
XLA Modules:
  0.0 150.2 jit_solution(4569476133203946728)
XLA Ops:
  7.2 0.8 fusion.51
  8.0 1.1 broadcast_multiply_fusion
  9.1 6.0 %collective-permute-start.4 = (bf16[4,64,256]{2,1,0:T(8,128)(2,1)S(1)}, bf16[4,64,256]{2,1,0:T(8,128)(2,1)S(1)}, u32[]{:S(2)}, u32[]{:S(2)}) collective-permute-start(bf16[4,64,256]{2,1,0:T(8,128)(2,1)S(1)} %get-tuple-element.22), channel_id=1, source_target_pairs={{0,14},{2,0},{4,2},{6,4},{8,6},{10,8},{12,10},{14,12},{1,15},{3,1}... | collective-permute-start | bytes 393224 | tf_op jit(solution)/shard_map/ppermute | solution.py:17
  15.1 1.1 convert_reduce_fusion
  16.3 1.2 fusion.24
  17.5 1.2 fusion.22
  19.5 0.8 broadcast_compare_fusion
  20.4 3.3 %collective-permute-done = bf16[4,64,256]{2,1,0:T(8,128)(2,1)S(1)} collective-permute-done((bf16[4,64,256]{2,1,0:T(8,128)(2,1)S(1)}, bf16[4,64,256]{2,1,0:T(8,128)(2,1)S(1)}, u32[]{:S(2)}, u32[]{:S(2)}) %collective-permute-start) | collective-permute-done | bytes 131104 | tf_op jit(solution)/shard_map/ppermute | solution.py:17
  28.3 3.7 %fusion.52 = (f32[8,8,64]{2,1,0:T(8,128)}, f32[8,8,64,64]{2,3,1,0:T(8,128)}) fusion(pred[8,64,64]{1,2,0:T(8,128)(4,1)} %broadcast_compare_fusion, bf16[8,64,8,32]{1,3,2,0:T(8,128)(2,1)S(1)} %bitcast.100, bf16[8,64,8,32]{1,3,2,0:T(8,128)(2,1)S(1)} %bitcast.102), kind=kOutput, calls=%fused_computation.94 | convolution fusion | flops 17825856 | bytes 1622016 | tf_op jit(solution)/shard_map/sub | solution.py:71
  32.1 0.8 multiply_divide_fusion
  32.8 2.3 %fusion.6 = (f32[8,8,64]{2,1,0:T(8,128)S(1)}, bf16[8,8,64,64]{2,3,1,0:T(8,128)(2,1)S(1)}) fusion(f32[8,8,64,64]{2,3,1,0:T(8,128)} %get-tuple-element.30, bf16[8,8,64,64]{2,3,1,0:T(8,128)(2,1)S(1)} %convolution_convert_fusion, f32[8,8,64]{2,1,0:T(8,128)S(1)} %multiply_divide_fusion, f32[8,8,64]{2,1,0:T(8,128)} %get-tuple-element.29), kind=kLoop, calls=%fused_computation.8 | loop fusion | flops 1568768 | bytes 2146304 | tf_op jit(solution)/shard_map/transpose(jvp())/reduce_sum | solution.py:72
  35.2 1.2 fusion.9
  37.1 1.6 %fusion.42 = f32[8,8,64,32]{2,3,1,0:T(8,128)} fusion(bf16[8,64,8,32]{1,3,2,0:T(8,128)(2,1)S(1)} %bitcast.103, f32[8,8,64,64]{2,3,1,0:T(8,128)S(1)} %copy-done.2, bf16[8,8,64,64]{2,3,1,0:T(8,128)(2,1)S(1)} %convolution_convert_fusion, f32[8,8,64]{2,1,0:T(8,128)S(1)} %neg.9, f32[8,8,64]{2,1,0:T(8,128)S(1)} %copy-done.16, pred[8,64,64]{1,2,0:T(8,128)(4,1)S(1)} %copy-done.17), kind=kOutput, calls=%fused_computation.86 | convolution fusion | flops 18350080 | bytes 2424832 | tf_op jit(solution)/shard_map/transpose(jvp(wqhd,wkhd->whqk))/dot_general | solution.py:67
  38.7 1.7 %fusion.44 = f32[8,8,64,32]{2,3,1,0:T(8,128)} fusion(bf16[8,64,8,32]{1,3,2,0:T(8,128)(2,1)S(1)} %bitcast.101, f32[8,8,64,64]{2,3,1,0:T(8,128)S(1)} %copy-done.2, bf16[8,8,64,64]{2,3,1,0:T(8,128)(2,1)S(1)} %convolution_convert_fusion, f32[8,8,64]{2,1,0:T(8,128)S(1)} %neg.9, f32[8,8,64]{2,1,0:T(8,128)S(1)} %copy-done.16, pred[8,64,64]{1,2,0:T(8,128)(4,1)S(1)} %copy-done.17), kind=kOutput, calls=%fused_computation.87 | convolution fusion | flops 18350080 | bytes 2424832 | tf_op jit(solution)/shard_map/transpose(jvp(wqhd,wkhd->whqk))/dot_general | solution.py:67
  40.7 0.9 copy-done.4
  42.0 1.6 %copy.52 = f32[8,64,256]{2,1,0:T(8,128)S(1)} copy(f32[8,64,256]{1,2,0:T(8,128)} %bitcast.94) | data formatting | bytes 1048576 | tf_op jit(solution)/shard_map/transpose(jvp())/reshape | solution.py:64
  43.7 1.1 fusion.8
  45.5 0.7 convert_element_type.151
  47.1 0.9 fusion.10
  48.1 9.6 %collective-permute-done.6 = bf16[4,64,256]{2,1,0:T(8,128)(2,1)S(1)} collective-permute-done((bf16[4,64,256]{2,1,0:T(8,128)(2,1)S(1)}, bf16[4,64,256]{2,1,0:T(8,128)(2,1)S(1)}, u32[]{:S(2)}, u32[]{:S(2)}) %collective-permute-start.6) | collective-permute-done | bytes 131104 | tf_op jit(solution)/shard_map/ppermute | solution.py:17
  59.8 2.5 %psum.46 = bf16[256]{0:T(256)(128)(2,1)S(1)} all-reduce(bf16[256]{0:T(256)(128)(2,1)S(1)} %get-tuple-element.5), channel_id=1, replica_groups=mesh['grp'=2,'row'=8,'col'=2] {'col'}, use_global_device_ids=true, to_apply=%region_12.13 | all-reduce | flops 256 | bytes 1024 | tf_op jit(solution)/shard_map/psum | solution.py:167
  62.3 1.2 add_convert_fusion.1
  63.5 5.5 %all-reduce.8.cloned.1.call-done = (bf16[256,768]{1,0:T(8,128)(2,1)}, bf16[256,256]{1,0:T(8,128)(2,1)}) async-done(((bf16[256,768]{1,0:T(8,128)(2,1)}, bf16[256,256]{1,0:T(8,128)(2,1)}), (bf16[256,768]{1,0:T(8,128)(2,1)}, bf16[256,256]{1,0:T(8,128)(2,1)})) %all-reduce.8.cloned.1.call-update) | async-done | bytes 524304 | tf_op jit(solution)/shard_map/psum | solution.py:165
  69.0 74.4 %all-reduce.9 = (f32[256,768]{1,0:T(8,128)}, f32[256,256]{1,0:T(8,128)}, f32[256]{0:T(256)}) all-reduce(bf16[256,768]{1,0:T(8,128)(2,1)} %get-tuple-element.10, bf16[256,256]{1,0:T(8,128)(2,1)} %get-tuple-element.11, bf16[256]{0:T(256)(128)(2,1)S(1)} %psum.46), channel_id=1, replica_groups=mesh['grp'=2,'row'=8,'col'=2] {'row'}, use_global_device_ids=true, to_apply=%region_8.9 | all-reduce | flops 262400 | bytes 1574400 | tf_op jit(solution)/shard_map/psum | solution.py:169
  (98 shorter events, 10.4 us)
Async XLA Ops:
  7.2 17.8 %copy-start = (bf16[256,768]{1,0:T(8,128)(2,1)S(1)}, bf16[256,768]{1,0:T(8,128)(2,1)}, u32[]{:S(2)}) copy-start(bf16[256,768]{1,0:T(8,128)(2,1)} %param.9) | copy-start | bytes 1179652
  7.2 61.8 %all-reduce.8.cloned.1.call-start = ((), (), s32[]{:S(2)}) async-start(), calls=%async_computation | async-start | bytes 1048576 | tf_op jit(solution)/shard_map/psum | solution.py:165
  9.1 14.9 %copy-start.10 = (bf16[256,256]{1,0:T(8,128)(2,1)S(1)}, bf16[256,256]{1,0:T(8,128)(2,1)}, u32[]{:S(2)}) copy-start(bf16[256,256]{1,0:T(8,128)(2,1)} %param.10) | copy-start | bytes 393220
  9.1 11.2 %collective-permute-start.4 = (bf16[4,64,256]{2,1,0:T(8,128)(2,1)S(1)}, bf16[4,64,256]{2,1,0:T(8,128)(2,1)S(1)}, u32[]{:S(2)}, u32[]{:S(2)}) collective-permute-start(bf16[4,64,256]{2,1,0:T(8,128)(2,1)S(1)} %get-tuple-element.22), channel_id=1, source_target_pairs={{0,14},{2,0},{4,2},{6,4},{8,6},{10,8},{12,10},{14,12},{1,15},{3,1}... | collective-permute-start | bytes 393224 | tf_op jit(solution)/shard_map/ppermute | solution.py:17
  18.7 5.0 %collective-permute-start = (bf16[4,64,256]{2,1,0:T(8,128)(2,1)S(1)}, bf16[4,64,256]{2,1,0:T(8,128)(2,1)S(1)}, u32[]{:S(2)}, u32[]{:S(2)}) collective-permute-start(bf16[4,64,256]{2,1,0:T(8,128)(2,1)S(1)} %get-tuple-element.26), channel_id=1, source_target_pairs={{0,14},{2,0},{4,2},{6,4},{8,6},{10,8},{12,10},{14,12},{1,15},{3,1}... | collective-permute-start | bytes 393224 | tf_op jit(solution)/shard_map/ppermute | solution.py:17
  20.3 3.6 %collective-permute-start.5 = (bf16[8,4,256]{2,1,0:T(4,128)(2,1)S(1)}, bf16[8,4,256]{2,1,0:T(4,128)(2,1)S(1)}, u32[]{:S(2)}, u32[]{:S(2)}) collective-permute-start(bf16[8,4,256]{2,1,0:T(4,128)(2,1)S(1)} %pad_maximum_fusion.5), channel_id=1, source_target_pairs={{0,1},{1,0},{2,3},{3,2},{4,5},{5,4},{6,7},{7,6},{8,9},{9,8},{10,11... | collective-permute-start | bytes 49160 | tf_op jit(solution)/shard_map/ppermute | solution.py:17
  23.7 1.2 collective-permute-start.1
  26.1 2.2 %copy-start.14 = (bf16[8,64,256]{1,2,0:T(8,128)(2,1)}, bf16[8,64,256]{1,2,0:T(8,128)(2,1)S(1)}, u32[]{:S(2)}) copy-start(bf16[8,64,256]{1,2,0:T(8,128)(2,1)S(1)} %copy.39) | copy-start | bytes 786436
  26.4 1.9 %copy-start.12 = (bf16[8,64,256]{1,2,0:T(8,128)(2,1)}, bf16[8,64,256]{1,2,0:T(8,128)(2,1)S(1)}, u32[]{:S(2)}) copy-start(bf16[8,64,256]{1,2,0:T(8,128)(2,1)S(1)} %copy.38) | copy-start | bytes 786436
  35.1 1.9 %copy-start.2 = (f32[8,8,64,64]{2,3,1,0:T(8,128)S(1)}, f32[8,8,64,64]{2,3,1,0:T(8,128)}, u32[]{:S(2)}) copy-start(f32[8,8,64,64]{2,3,1,0:T(8,128)} %get-tuple-element.30) | copy-start | bytes 3145732
  35.1 1.9 %copy-start.15 = (bf16[8,64,256]{1,2,0:T(8,128)(2,1)S(1)}, bf16[8,64,256]{1,2,0:T(8,128)(2,1)}, u32[]{:S(2)}) copy-start(bf16[8,64,256]{1,2,0:T(8,128)(2,1)} %copy-done.14) | copy-start | bytes 786436
  35.1 1.9 %copy-start.16 = (f32[8,8,64]{2,1,0:T(8,128)S(1)}, f32[8,8,64]{2,1,0:T(8,128)}, u32[]{:S(2)}) copy-start(f32[8,8,64]{2,1,0:T(8,128)} %get-tuple-element.29) | copy-start | bytes 49156
  35.1 1.9 %copy-start.17 = (pred[8,64,64]{1,2,0:T(8,128)(4,1)S(1)}, pred[8,64,64]{1,2,0:T(8,128)(4,1)}, u32[]{:S(2)}) copy-start(pred[8,64,64]{1,2,0:T(8,128)(4,1)} %broadcast_compare_fusion) | copy-start | bytes 98308
  37.1 1.6 %copy-start.13 = (bf16[8,64,256]{1,2,0:T(8,128)(2,1)S(1)}, bf16[8,64,256]{1,2,0:T(8,128)(2,1)}, u32[]{:S(2)}) copy-start(bf16[8,64,256]{1,2,0:T(8,128)(2,1)} %copy-done.12) | copy-start | bytes 786436
  40.4 1.2 copy-start.4
  42.0 1.7 %copy-start.9 = (bf16[8,64,256]{2,1,0:T(8,128)(2,1)S(1)}, bf16[8,64,256]{2,1,0:T(8,128)(2,1)}, u32[]{:S(2)}) copy-start(bf16[8,64,256]{2,1,0:T(8,128)(2,1)} %copy-done.8) | copy-start | bytes 786436
  44.9 1.3 copy-start.11
  46.5 12.4 %copy-start.1 = (bf16[8,64,256]{2,1,0:T(8,128)(2,1)S(1)}, bf16[8,64,256]{2,1,0:T(8,128)(2,1)}, u32[]{:S(2)}) copy-start(bf16[8,64,256]{2,1,0:T(8,128)(2,1)} %param.6) | copy-start | bytes 786436
  46.5 12.4 %copy-start.18 = (f32[256]{0:T(256)S(1)}, f32[256]{0:T(256)}, u32[]{:S(2)}) copy-start(f32[256]{0:T(256)} %param.11) | copy-start | bytes 3076
  46.5 11.2 %collective-permute-start.2 = (bf16[4,64,256]{2,1,0:T(8,128)(2,1)S(1)}, bf16[4,64,256]{2,1,0:T(8,128)(2,1)S(1)}, u32[]{:S(2)}, u32[]{:S(2)}) collective-permute-start(bf16[4,64,256]{2,1,0:T(8,128)(2,1)S(1)} %bitcast.104), channel_id=1, source_target_pairs={{0,2},{2,4},{4,6},{6,8},{8,10},{10,12},{12,14},{14,0},{1,3},{3,5},... | collective-permute-start | bytes 393224 | tf_op jit(solution)/shard_map/ppermute | solution.py:17
  47.0 15.3 %copy-start.7 = (bf16[8,64,256]{2,1,0:T(8,128)(2,1)S(1)}, bf16[8,64,256]{2,1,0:T(8,128)(2,1)}, u32[]{:S(2)}) copy-start(bf16[8,64,256]{2,1,0:T(8,128)(2,1)} %param.7) | copy-start | bytes 786436
  47.0 10.6 %collective-permute-start.6 = (bf16[4,64,256]{2,1,0:T(8,128)(2,1)S(1)}, bf16[4,64,256]{2,1,0:T(8,128)(2,1)S(1)}, u32[]{:S(2)}, u32[]{:S(2)}) collective-permute-start(bf16[4,64,256]{2,1,0:T(8,128)(2,1)S(1)} %bitcast.105), channel_id=1, source_target_pairs={{0,2},{2,4},{4,6},{6,8},{8,10},{10,12},{12,14},{14,0},{1,3},{3,5},... | collective-permute-start | bytes 393224 | tf_op jit(solution)/shard_map/ppermute | solution.py:17
  57.7 1.2 collective-permute-start.7
  57.8 4.5 %collective-permute-start.3 = (bf16[8,4,256]{2,1,0:T(4,128)(2,1)S(1)}, bf16[8,4,256]{2,1,0:T(4,128)(2,1)S(1)}, u32[]{:S(2)}, u32[]{:S(2)}) collective-permute-start(bf16[8,4,256]{2,1,0:T(4,128)(2,1)S(1)} %pad_maximum_fusion.6), channel_id=1, source_target_pairs={{0,1},{1,0},{2,3},{3,2},{4,5},{5,4},{6,7},{7,6},{8,9},{9,8},{10,11... | collective-permute-start | bytes 49160 | tf_op jit(solution)/shard_map/ppermute | solution.py:17
  (4 other events, 3.9 us)
Sparse Core Ops, SparseCore 0:
  48.2 20.7 all-reduce.7
where the time goes:
time: 151 us; the launch traced here: 150 us
  blocking collectives  76.8 us (51%)
  waiting for transfers between devices  19.6 us (13%)
  between operations  14.6 us (10%)
  matrix products  12.7 us (8%)
  other arithmetic  11.5 us (8%)
  starting transfers between devices  7.53 us (5%)
  local copies, waits for them, and re-layouts  7.28 us (5%)
    psum x1, blocking collectives, on_device(): lax.psum((chip_sums[0], chip_sums[1], chip_sums[2]), 'row')  74.4 us
    ppermute x8, waiting for transfers between devices, from_behind(): lax.ppermute(array, axis, [(i, (i + by) % peers) for i in range(peers)])  14.1 us
    ppermute x8, starting transfers between devices, from_behind(): lax.ppermute(array, axis, [(i, (i + by) % peers) for i in range(peers)])  7.5 us
    psum x1, waiting for transfers between devices, on_device(): lax.psum(part_qkv.astype(jnp.bfloat16), 'col').astype(jnp.float32)  5.47 us
    sub x1, matrix products, window_core(): weights = jnp.exp(scores - peak)  3.75 us
    dot_general x2, matrix products, window_core(): jnp.einsum('wqhd,wkhd->whqk', query_part, key_part) * head_dim ** (-0.5)  3.33 us
  transfers between devices with their start and end apart: 9, of which 5 were waited for; matrix products, arithmetic and copies ran while one was open for 6% of the time, Pallas kernels for 0%

commit v1 on v0

v1 whole, which is shorter than its diff:
```python
import jax
import jax.numpy as jnp
from jax import lax
from jax.experimental import pallas as pl
from jax.experimental.pallas import tpu as pltpu
from jax.sharding import PartitionSpec as P

HEADS = 8
WIN = 8
SHIFT = 4
NORM_EPSILON = 1e-05
MASKED_SCORE = -1e30
LOG2_E = 1.4426950408889634

BF16 = jnp.bfloat16
F32 = jnp.float32


def dot(left, right, left_dim, right_dim):
    return lax.dot_general(
        left, right, (((left_dim,), (right_dim,)), ((), ())), preferred_element_type=F32
    )


def assemble_shifted(buf, own, below, right, corner):
    cols = own.shape[1]
    buf[0:SHIFT, 0:cols, :] = own
    buf[SHIFT:WIN, 0:cols, :] = below[...].astype(F32)
    buf[0:SHIFT, cols : cols + WIN, :] = right[...].astype(F32)
    buf[SHIFT:WIN, cols : cols + WIN, :] = corner[...].astype(F32)


def domain_rows(domain, rows, channels):
    flags = domain[...].astype(F32).astype(BF16)
    row_ids = lax.broadcasted_iota(jnp.int32, (flags.shape[0], channels), 0)
    return [dot(flags, (row_ids == row).astype(F32).astype(BF16), 0, 0) for row in rows]


def block_kernel(
    feat, feat_below, feat_right, feat_corner,
    cot, cot_below, cot_right, cot_corner,
    domain, wqkv, wproj, gain,
    keep, send, ad_keep, ad_send,
    buf, shifted, projected, dattended, dcontext, context, dprojected, grads,
):
    tile_rows, cols, channels = feat.shape
    windows = cols // WIN
    cells = WIN * WIN
    half = channels // 2
    group_heads = HEADS // 2
    head_dim = channels // HEADS

    assemble_shifted(buf, feat[SHIFT:WIN].astype(F32), feat_below, feat_right, feat_corner)
    for w in range(windows):
        x = buf[:, SHIFT + WIN * w : SHIFT + WIN * (w + 1), :].reshape(cells, channels)
        centred = x - jnp.mean(x, -1, keepdims=True)
        variance = jnp.mean(centred * centred, -1, keepdims=True)
        normed = centred * lax.rsqrt(variance + NORM_EPSILON) * gain[...]
        shifted[cells * w : cells * (w + 1), :] = normed.astype(BF16)

    masks = domain_rows(domain, range(SHIFT, WIN), channels)
    own = jnp.stack([cot[SHIFT + i].astype(F32) * masks[i] for i in range(SHIFT)], 0)
    assemble_shifted(buf, own, cot_below, cot_right, cot_corner)
    for w in range(windows):
        x = buf[:, SHIFT + WIN * w : SHIFT + WIN * (w + 1), :].reshape(cells, channels)
        dattended[cells * w : cells * (w + 1), :] = x.astype(BF16)

    step = 128
    for m in range(0, cells * windows, step):
        projected[m : m + step, :] = dot(shifted[m : m + step, :], wqkv[...], 1, 0).astype(BF16)
        dcontext[m : m + step, :] = dot(dattended[m : m + step, :], wproj[...], 1, 1).astype(BF16)

    last_row = lax.axis_index("row") == lax.axis_size("row") - 1
    last_col = lax.axis_index("col") == lax.axis_size("col") - 1
    wide = group_heads * cells
    key_id = lax.broadcasted_iota(jnp.int32, (cells, wide), 0)
    query_id = lax.broadcasted_iota(jnp.int32, (cells, wide), 1)
    row_apart = ((key_id ^ query_id) & (WIN * SHIFT)) != 0
    col_apart = ((key_id ^ query_id) & SHIFT) != 0
    lane = lax.broadcasted_iota(jnp.int32, (cells, half), 1)
    in_head = [lane // head_dim == h for h in range(group_heads)]
    scale = head_dim ** (-0.5)

    def spread(values):
        zero = jnp.zeros_like(values)
        return jnp.concatenate([jnp.where(m, values, zero) for m in in_head], 0)

    def gather(full):
        parts = [full[cells * h : cells * (h + 1)] for h in range(group_heads)]
        out = parts[-1]
        for h in range(group_heads - 2, -1, -1):
            out = jnp.where(in_head[h], parts[h], out)
        return out

    def one_window(base, excluded):
        for g in range(2):
            at = half * g
            rows = pl.ds(base, cells)
            query = projected[rows, at : at + half]
            key = projected[rows, channels + at : channels + at + half]
            value = projected[rows, 2 * channels + at : 2 * channels + at + half]
            dctx = dcontext[rows, at : at + half]
            query_x = spread(query)
            dctx_x = spread(dctx)
            scores = dot(key, query_x, 1, 1)
            scores = jnp.where(excluded, MASKED_SCORE, scores)
            peak = jnp.max(scores, 0, keepdims=True)
            weights = jnp.exp2((scores - peak) * (scale * LOG2_E))
            probability = weights * (1.0 / jnp.sum(weights, 0, keepdims=True))
            prob16 = probability.astype(BF16)
            context[rows, at : at + half] = gather(dot(prob16, value, 0, 0)).astype(BF16)
            dprob = dot(value, dctx_x, 1, 1).astype(BF16).astype(F32)
            mean = jnp.sum(probability * dprob, 0, keepdims=True)
            dscore = (probability * (dprob - mean) * scale).astype(BF16)
            dprojected[rows, at : at + half] = gather(dot(dscore, key, 0, 0)).astype(BF16)
            dprojected[rows, channels + at : channels + at + half] = dot(
                dscore, query_x, 1, 0
            ).astype(BF16)
            dprojected[rows, 2 * channels + at : 2 * channels + at + half] = dot(
                prob16, dctx_x, 1, 0
            ).astype(BF16)

    row_excluded = jnp.logical_and(row_apart, last_row)
    for w in range(windows):
        excluded = row_excluded
        if w == windows - 1:
            excluded = jnp.logical_or(excluded, jnp.logical_and(col_apart, last_col))
        one_window(cells * w, excluded)

    for b in range(3):
        grads[channels * b : channels * (b + 1), :] = dot(
            shifted[...], dprojected[:, channels * b : channels * (b + 1)], 0, 0
        ).astype(BF16)
    grads[3 * channels : 4 * channels, :] = dot(context[...], dattended[...], 0, 0).astype(BF16)
    mine = lax.axis_index("col")
    keep[...] = grads[pl.ds(pl.multiple_of(mine * 2 * channels, 2 * channels), 2 * channels), :]
    send[...] = grads[
        pl.ds(pl.multiple_of((1 - mine) * 2 * channels, 2 * channels), 2 * channels), :
    ]

    def leave(slot):
        ad_keep[slot] = buf[0:SHIFT, 0:cols, :].astype(BF16)
        ad_send[slot] = buf[SHIFT:WIN, 0:cols, :].astype(BF16)

    for w in range(windows):
        rows = slice(cells * w, cells * (w + 1))
        buf[:, WIN * w : WIN * (w + 1), :] = dot(context[rows, :], wproj[...], 1, 0).reshape(
            WIN, WIN, channels
        )
    leave(0)
    for w in range(windows):
        rows = slice(cells * w, cells * (w + 1))
        buf[:, WIN * w : WIN * (w + 1), :] = dot(dprojected[rows, :], wqkv[...], 1, 1).reshape(
            WIN, WIN, channels
        )
    leave(1)


def finish_kernel(feat, cot, domain, gain, ad_keep, ad_rows, ad_cols, updated, grad_features, buf):
    tile_rows, cols, channels = feat.shape
    masks = domain_rows(domain, range(WIN), channels)

    def unshifted(slot):
        buf[:, 0:WIN, :] = ad_cols[slot].astype(F32)
        buf[0:SHIFT, WIN : WIN + cols, :] = ad_rows[slot].astype(F32)
        buf[SHIFT:WIN, WIN : WIN + cols, :] = ad_keep[slot].astype(F32)

    unshifted(0)
    for i in range(WIN):
        back = buf[i, SHIFT : SHIFT + cols, :]
        updated[i] = (feat[i].astype(F32) + masks[i] * back).astype(BF16)
    unshifted(1)
    for i in range(WIN):
        upstream = buf[i, SHIFT : SHIFT + cols, :] * gain[...]
        x = feat[i].astype(F32)
        centred = x - jnp.mean(x, -1, keepdims=True)
        variance = jnp.mean(centred * centred, -1, keepdims=True)
        inverse = lax.rsqrt(variance + NORM_EPSILON)
        standard = centred * inverse
        along = jnp.mean(upstream * standard, -1, keepdims=True)
        flat = jnp.mean(upstream, -1, keepdims=True)
        grad = inverse * (upstream - flat - standard * along)
        grad_features[i] = (cot[i].astype(F32) + grad).astype(BF16)


def sums_kernel(own, row_peer, col_peer, wqkv, gain, grad_qkv, grad_proj, grad_gain, blocks):
    channels = own.shape[0]
    mine_col = lax.axis_index("col")
    mine_row = lax.axis_index("row") % 2
    blocks[2 * mine_col + mine_row] = own[...].astype(F32)
    blocks[2 * mine_col + 1 - mine_row] = row_peer[...].astype(F32)
    other = 2 * (1 - mine_col)
    blocks[other] = col_peer[0:channels, :].astype(F32)
    blocks[other + 1] = col_peer[channels:, :].astype(F32)
    total = jnp.zeros((8, channels), F32)
    ones = jnp.ones((8, channels), BF16)
    for b in range(3):
        part = blocks[b]
        grad_qkv[:, channels * b : channels * (b + 1)] = part
        product = part * wqkv[:, channels * b : channels * (b + 1)].astype(F32)
        high = product.astype(BF16)
        low = (product - high.astype(F32)).astype(BF16)
        total = total + dot(ones, high, 1, 1) + dot(ones, low, 1, 1)
    grad_proj[...] = blocks[3]
    grad_gain[...] = total[0:1, :] / gain[...]


def run(kernel, out_shapes, scratch, *operands):
    return pl.pallas_call(
        kernel,
        out_shape=out_shapes,
        scratch_shapes=scratch,
        compiler_params=pltpu.CompilerParams(vmem_limit_bytes=48 << 20),
    )(*operands)


def ahead(array, axes):
    sizes = [lax.axis_size(a) for a in axes]
    if len(axes) == 1:
        pairs = [(i, (i - 1) % sizes[0]) for i in range(sizes[0])]
    else:
        rows, cols = sizes
        pairs = [
            (r * cols + c, (r - 1) % rows * cols + (c - 1) % cols)
            for r in range(rows)
            for c in range(cols)
        ]
    return lax.ppermute(array, axes if len(axes) > 1 else axes[0], pairs)


def behind(array, axis):
    peers = lax.axis_size(axis)
    return lax.ppermute(array, axis, [(i, (i + 1) % peers) for i in range(peers)])


def swap(array, axis, bit):
    return lax.ppermute(array, axis, [(i, i ^ bit) for i in range(lax.axis_size(axis))])


def add16(left, right):
    return (left.astype(F32) + right.astype(F32)).astype(BF16)


def on_device(features, cotangent, domain, qkv_weight, proj_weight, norm_gain):
    tile_rows, cols, channels = features.shape
    gain = norm_gain.reshape(1, channels)
    tokens = tile_rows * cols

    feat_below = ahead(features[:SHIFT], ("row",))
    feat_right = ahead(features[SHIFT:, :WIN], ("col",))
    feat_corner = ahead(features[:SHIFT, :WIN], ("row", "col"))
    flags = domain.astype(BF16)[..., None]
    cot_below = ahead(cotangent[:SHIFT] * flags[:SHIFT], ("row",))
    cot_right = ahead(cotangent[SHIFT:, :WIN] * flags[SHIFT:, :WIN], ("col",))
    cot_corner = ahead(cotangent[:SHIFT, :WIN] * flags[:SHIFT, :WIN], ("row", "col"))

    def shape(dims, dtype):
        return jax.ShapeDtypeStruct(dims, dtype)

    keep, send, ad_keep, ad_send = run(
        block_kernel,
        (
            shape((2 * channels, channels), BF16),
            shape((2 * channels, channels), BF16),
            shape((2, SHIFT, cols, channels), BF16),
            shape((2, SHIFT, cols, channels), BF16),
        ),
        [
            pltpu.VMEM((WIN, cols + WIN, channels), F32),
            pltpu.VMEM((tokens, channels), BF16),
            pltpu.VMEM((tokens, 3 * channels), BF16),
            pltpu.VMEM((tokens, channels), BF16),
            pltpu.VMEM((tokens, channels), BF16),
            pltpu.VMEM((tokens, channels), BF16),
            pltpu.VMEM((tokens, 3 * channels), BF16),
            pltpu.VMEM((4 * channels, channels), BF16),
        ],
        features, feat_below, feat_right, feat_corner,
        cotangent, cot_below, cot_right, cot_corner,
        domain, qkv_weight, proj_weight, gain,
    )

    summed = add16(keep, swap(send, "col", 1))
    mine_row = lax.axis_index("row") % 2
    mine = lax.dynamic_slice_in_dim(summed, mine_row * channels, channels, 0)
    other = lax.dynamic_slice_in_dim(summed, (1 - mine_row) * channels, channels, 0)
    own = add16(mine, swap(other, "row", 1))
    bit = 2
    while bit < lax.axis_size("row"):
        own = add16(own, swap(own, "row", bit))
        bit *= 2
    row_peer = swap(own, "row", 1)
    pair = jnp.where(
        mine_row == 0,
        jnp.concatenate([own, row_peer], 0),
        jnp.concatenate([row_peer, own], 0),
    )
    col_peer = swap(pair, "col", 1)
    grad_qkv, grad_proj, grad_gain = run(
        sums_kernel,
        (
            shape((channels, 3 * channels), F32),
            shape((channels, channels), F32),
            shape((1, channels), F32),
        ),
        [pltpu.VMEM((4, channels, channels), F32)],
        own, row_peer, col_peer, qkv_weight, gain,
    )

    ad_rows = behind(ad_send, "row")
    edge = jnp.concatenate([ad_rows[:, :, cols - WIN :], ad_keep[:, :, cols - WIN :]], 1)
    ad_cols = behind(edge, "col")
    updated, grad_features = run(
        finish_kernel,
        (shape(features.shape, BF16), shape(features.shape, BF16)),
        [pltpu.VMEM((WIN, cols + WIN, channels), F32)],
        features, cotangent, domain, gain, ad_keep, ad_rows, ad_cols,
    )
    return updated, grad_features, grad_qkv, grad_proj, grad_gain.reshape(channels)


def solution(mesh):
    return jax.shard_map(
        on_device,
        mesh=mesh,
        in_specs=(
            P(("grp", "row"), "col", None),
            P(("grp", "row"), "col", None),
            P(("grp", "row"), "col"),
            P(),
            P(),
            P(),
        ),
        out_specs=(
            P(("grp", "row"), "col", None),
            P(("grp", "row"), "col", None),
            P("grp", None),
            P("grp", None),
            P("grp"),
        ),
        check_vma=False,
    )
```

time: 151 us -> 61.4 us (0.41)
  blocking collectives: 76.8 us -> 0 us
  between operations: 14.6 us -> 0.8 us
  waiting for transfers between devices: 19.6 us -> 33.4 us
  matrix products: 12.7 us -> 0 us
  Pallas kernels: 0 us -> 10.1 us
  other arithmetic: 11.5 us -> 1.94 us
  starting transfers between devices: 7.53 us -> 12.9 us
  local copies, waits for them, and re-layouts: 7.28 us -> 1.99 us
    psum x2 -> x0, blocking collectives: 76.8 us -> none  [the longest x1 74.4 us: on_device(): lax.psum((chip_sums[0], chip_sums[1], chip_sums[2]), 'row')]
    ppermute x8 -> x14, waiting for transfers between devices: 14.1 us -> 33.4 us  [the longest x6 26.8 us: swap(): lax.ppermute(array, axis, [(i, i ^ bit) for i in range(lax.axis_size(axis...]
    pallas_call x0 -> x3, Pallas kernels: none -> 10.1 us  [run(): pl.pallas_call(kernel, out_shape=out_shapes, scratch_shapes=scratch, comp...]
    dot_general x11 -> x0, matrix products: 9 us -> none  [the longest x2 3.33 us: window_core(): jnp.einsum('wqhd,wkhd->whqk', query_part, key_part) * head_dim ** (-0.5)]
    psum x1 -> x0, waiting for transfers between devices: 5.47 us -> none  [on_device(): lax.psum(part_qkv.astype(jnp.bfloat16), 'col').astype(jnp.float32)]
    reduce_sum x5 -> x0, other arithmetic: 5.4 us -> none  [the longest x1 2.28 us: window_core(): probability = weights / jnp.sum(weights, -1, keepdims=True)]
    ppermute x8 -> x14, starting transfers between devices: 7.5 us -> 12.9 us  [the longest x6 8.79 us: ahead(): return lax.ppermute(array, axes if len(axes) > 1 else axes[0], pairs)]
    sub x1 -> x0, matrix products: 3.75 us -> none  [window_core(): weights = jnp.exp(scores - peak)]
  transfers between devices with their start and end apart: 9 -> 14, of which waited for: 5 -> 8; matrix products, arithmetic and copies ran while one was open for 6% -> 2% of each run, Pallas kernels for 0% -> 2%
where the time goes in v1:
time: 61.4 us; the launch traced here: 61.1 us
  waiting for transfers between devices  33.4 us (54%)
  starting transfers between devices  12.9 us (21%)
  Pallas kernels  10.1 us (16%)
  local copies, waits for them, and re-layouts  1.99 us (3%)
  other arithmetic  1.94 us (3%)
  between operations  0.8 us (1%)
    ppermute x6, waiting for transfers between devices, swap(): lax.ppermute(array, axis, [(i, i ^ bit) for i in range(lax.axis_size(axis...  26.8 us
    pallas_call x3, Pallas kernels, run(): pl.pallas_call(kernel, out_shape=out_shapes, scratch_shapes=scratch, comp...  10.1 us
    ppermute x6, starting transfers between devices, ahead(): return lax.ppermute(array, axes if len(axes) > 1 else axes[0], pairs)  8.79 us
    ppermute x6, waiting for transfers between devices, ahead(): return lax.ppermute(array, axes if len(axes) > 1 else axes[0], pairs)  5.63 us
    ppermute x6, starting transfers between devices, swap(): lax.ppermute(array, axis, [(i, i ^ bit) for i in range(lax.axis_size(axis...  2.1 us
    ppermute x2, starting transfers between devices, behind(): lax.ppermute(array, axis, [(i, (i + 1) % peers) for i in range(peers)])  2 us
  transfers between devices with their start and end apart: 14, of which 8 were waited for; matrix products, arithmetic and copies ran while one was open for 2% of the time, Pallas kernels for 2%

profile of v1, /device:TPU:0, one launch (start us, length us, event | category | flops | bytes accessed | tf_op | source)
XLA Modules:
  0.0 61.1 jit_solution(10525932761700411103)
XLA Ops:
  0.6 0.7 %convert_bitcast_fusion = bf16[8,64,1]{1,0,2:T(8,128)(2,1)S(1)} fusion(s32[8,64]{1,0:T(8,128)} %domain.3), kind=kLoop, calls=%fused_computation.13 | loop fusion | flops 512 | bytes 3072 | tf_op jit(solution)/shard_map/broadcast_in_dim | solution.py:252
  1.4 0.8 %slice_multiply_fusion.1 = (bf16[4,8,256]{2,1,0:T(8,128)(2,1)S(1)}, bf16[4,8,256]{2,1,0:T(8,128)(2,1)S(1)}) fusion(bf16[8,64,256]{2,1,0:T(8,128)(2,1)} %cot.3, bf16[4,8]{1,0:T(4,128)(2,1)S(1)} %get-tuple-element.27, bf16[4,8]{1,0:T(4,128)(2,1)S(1)} %get-tuple-element.28), kind=kLoop, calls=%fused_computation.7 | loop fusion | flops 16384 | bytes 65664 | tf_op jit(solution)/shard_map/mul | solution.py:255
  2.2 5.4 %collective-permute-start.5 = (bf16[4,8,256]{2,1,0:T(8,128)(2,1)S(1)}, bf16[4,8,256]{2,1,0:T(8,128)(2,1)S(1)}, u32[]{:S(2)}, u32[]{:S(2)}) collective-permute-start(bf16[4,8,256]{2,1,0:T(8,128)(2,1)S(1)} %get-tuple-element.23), channel_id=1, source_target_pairs={{0,15},{1,14},{2,1},{3,0},{4,3},{5,2},{6,5},{7,4},{8,7},{9,6},{10,... | collective-permute-start | bytes 49160 | tf_op jit(solution)/shard_map/ppermute | solution.py:228
  7.6 0.7 %collective-permute-start.4 = (bf16[4,8,256]{2,1,0:T(8,128)(2,1)S(1)}, bf16[4,8,256]{2,1,0:T(8,128)(2,1)S(1)}, u32[]{:S(2)}, u32[]{:S(2)}) collective-permute-start(bf16[4,8,256]{2,1,0:T(8,128)(2,1)S(1)} %get-tuple-element.24), channel_id=1, source_target_pairs={{0,1},{1,0},{2,3},{3,2},{4,5},{5,4},{6,7},{7,6},{8,9},{9,8},{10,11... | collective-permute-start | bytes 49160 | tf_op jit(solution)/shard_map/ppermute | solution.py:228
  8.3 0.9 %slice.34 = bf16[4,64,256]{2,1,0:T(8,128)(2,1)S(1)} slice(bf16[8,64,256]{2,1,0:T(8,128)(2,1)} %feat.3), slice={[0:4], [0:64], [0:256]} | slice | bytes 262144 | tf_op jit(solution)/shard_map/slice | solution.py:249
  9.2 0.6 collective-permute-start
  9.9 1.4 %collective-permute-start.3 = (bf16[4,64,256]{2,1,0:T(8,128)(2,1)S(1)}, bf16[4,64,256]{2,1,0:T(8,128)(2,1)S(1)}, u32[]{:S(2)}, u32[]{:S(2)}) collective-permute-start(bf16[4,64,256]{2,1,0:T(8,128)(2,1)S(1)} %slice_multiply_fusion), channel_id=1, source_target_pairs={{0,14},{2,0},{4,2},{6,4},{8,6},{10,8},{12,10},{14,12},{1,15},{3,1}... | collective-permute-start | bytes 393224 | tf_op jit(solution)/shard_map/ppermute | solution.py:228
  11.5 0.6 %collective-permute-start.1 = (bf16[4,8,256]{2,1,0:T(8,128)(2,1)S(1)}, bf16[4,8,256]{2,1,0:T(8,128)(2,1)S(1)}, u32[]{:S(2)}, u32[]{:S(2)}) collective-permute-start(bf16[4,8,256]{2,1,0:T(8,128)(2,1)S(1)} %get-tuple-element.26), channel_id=1, source_target_pairs={{0,1},{1,0},{2,3},{3,2},{4,5},{5,4},{6,7},{7,6},{8,9},{9,8},{10,11... | collective-permute-start | bytes 49160 | tf_op jit(solution)/shard_map/ppermute | solution.py:228
  12.1 4.9 %collective-permute-done.2.feat_corner = bf16[4,8,256]{2,1,0:T(8,128)(2,1)S(1)} collective-permute-done((bf16[4,8,256]{2,1,0:T(8,128)(2,1)S(1)}, bf16[4,8,256]{2,1,0:T(8,128)(2,1)S(1)}, u32[]{:S(2)}, u32[]{:S(2)}) %collective-permute-start.2) | collective-permute-done | bytes 16416 | tf_op jit(solution)/shard_map/ppermute | solution.py:228
  17.0 0.7 %collective-permute-done.3.cot_below = bf16[4,64,256]{2,1,0:T(8,128)(2,1)S(1)} collective-permute-done((bf16[4,64,256]{2,1,0:T(8,128)(2,1)S(1)}, bf16[4,64,256]{2,1,0:T(8,128)(2,1)S(1)}, u32[]{:S(2)}, u32[]{:S(2)}) %collective-permute-start.3) | collective-permute-done | bytes 131104 | tf_op jit(solution)/shard_map/ppermute | solution.py:228
  17.7 1.0 %copy-done.2 = bf16[256,768]{1,0:T(8,128)(2,1)S(1)} copy-done((bf16[256,768]{1,0:T(8,128)(2,1)S(1)}, bf16[256,768]{1,0:T(8,128)(2,1)}, u32[]{:S(2)}) %copy-start.2) | copy-done | bytes 393240
  18.7 7.3 %shard_map.101 = (bf16[512,256]{1,0:T(8,128)(2,1)S(1)}, bf16[512,256]{1,0:T(8,128)(2,1)S(1)}, bf16[2,4,64,256]{3,2,1,0:T(8,128)(2,1)S(1)}, bf16[2,4,64,256]{3,2,1,0:T(8,128)(2,1)S(1)}) custom-call(bf16[8,64,256]{2,1,0:T(8,128)(2,1)S(1)} %copy-done, bf16[4,64,256]{2,1,0:T(8,128)(2,1)S(1)} %collective-permute-done.feat_below, ...), custom_call_target="tpu_custom_call" | custom-call | tf_op jit(solution)/shard_map/pallas_call | solution.py:209
  26.3 1.4 %collective-permute-done.8 = bf16[512,256]{1,0:T(8,128)(2,1)S(1)} collective-permute-done((bf16[512,256]{1,0:T(8,128)(2,1)S(1)}, bf16[512,256]{1,0:T(8,128)(2,1)S(1)}, u32[]{:S(2)}, u32[]{:S(2)}) %collective-permute-start.8) | collective-permute-done | bytes 262176 | tf_op jit(solution)/shard_map/ppermute | solution.py:237
  27.9 5.5 %collective-permute-done.9 = bf16[256,256]{1,0:T(8,128)(2,1)S(1)} collective-permute-done((bf16[256,256]{1,0:T(8,128)(2,1)S(1)}, bf16[256,256]{1,0:T(8,128)(2,1)S(1)}, u32[]{:S(2)}, u32[]{:S(2)}) %collective-permute-start.9) | collective-permute-done | bytes 131104 | tf_op jit(solution)/shard_map/ppermute | solution.py:237
  33.5 5.0 %collective-permute-done.10 = bf16[256,256]{1,0:T(8,128)(2,1)S(1)} collective-permute-done((bf16[256,256]{1,0:T(8,128)(2,1)S(1)}, bf16[256,256]{1,0:T(8,128)(2,1)S(1)}, u32[]{:S(2)}, u32[]{:S(2)}) %collective-permute-start.10) | collective-permute-done | bytes 131104 | tf_op jit(solution)/shard_map/ppermute | solution.py:237
  38.5 1.0 %collective-permute-start.11 = (bf16[256,256]{1,0:T(8,128)(2,1)S(1)}, bf16[256,256]{1,0:T(8,128)(2,1)S(1)}, u32[]{:S(2)}, u32[]{:S(2)}) collective-permute-start(bf16[256,256]{1,0:T(8,128)(2,1)S(1)} %add_convert_fusion.2), channel_id=1, source_target_pairs={{0,8},{2,10},{4,12},{6,14},{8,0},{10,2},{12,4},{14,6},{1,9},{3,11}... | collective-permute-start | bytes 393224 | tf_op jit(solution)/shard_map/ppermute | solution.py:237
  39.5 6.3 %collective-permute-done.11 = bf16[256,256]{1,0:T(8,128)(2,1)S(1)} collective-permute-done((bf16[256,256]{1,0:T(8,128)(2,1)S(1)}, bf16[256,256]{1,0:T(8,128)(2,1)S(1)}, u32[]{:S(2)}, u32[]{:S(2)}) %collective-permute-start.11) | collective-permute-done | bytes 131104 | tf_op jit(solution)/shard_map/ppermute | solution.py:237
  45.9 0.6 %collective-permute-start.12 = (bf16[256,256]{1,0:T(8,128)(2,1)S(1)}, bf16[256,256]{1,0:T(8,128)(2,1)S(1)}, u32[]{:S(2)}, u32[]{:S(2)}) collective-permute-start(bf16[256,256]{1,0:T(8,128)(2,1)S(1)} %add_convert_fusion.1.own), channel_id=1, source_target_pairs={{0,2},{2,0},{4,6},{6,4},{8,10},{10,8},{12,14},{14,12},{1,3},{3,1},... | collective-permute-start | bytes 393224 | tf_op jit(solution)/shard_map/ppermute | solution.py:237
  46.5 1.5 %collective-permute-start.6 = (bf16[2,4,64,256]{3,2,1,0:T(8,128)(2,1)S(1)}, bf16[2,4,64,256]{3,2,1,0:T(8,128)(2,1)S(1)}, u32[]{:S(2)}, u32[]{:S(2)}) collective-permute-start(bf16[2,4,64,256]{3,2,1,0:T(8,128)(2,1)S(1)} %get-tuple-element.15), channel_id=1, source_target_pairs={{0,2},{2,4},{4,6},{6,8},{8,10},{10,12},{12,14},{14,0},{1,3},{3,5},... | collective-permute-start | bytes 786440 | tf_op jit(solution)/shard_map/ppermute | solution.py:233
  48.0 8.6 %collective-permute-done.12.row_peer = bf16[256,256]{1,0:T(8,128)(2,1)S(1)} collective-permute-done((bf16[256,256]{1,0:T(8,128)(2,1)S(1)}, bf16[256,256]{1,0:T(8,128)(2,1)S(1)}, u32[]{:S(2)}, u32[]{:S(2)}) %collective-permute-start.12) | collective-permute-done | bytes 131104 | tf_op jit(solution)/shard_map/ppermute | solution.py:237
  56.8 0.5 collective-permute-start.7
  57.4 1.0 %collective-permute-done.7.ad_cols = bf16[2,8,8,256]{3,2,1,0:T(8,128)(2,1)S(1)} collective-permute-done((bf16[2,8,8,256]{3,2,1,0:T(8,128)(2,1)S(1)}, bf16[2,8,8,256]{3,2,1,0:T(8,128)(2,1)S(1)}, u32[]{:S(2)}, u32[]{:S(2)}) %collective-permute-start.7) | collective-permute-done | bytes 65568 | tf_op jit(solution)/shard_map/ppermute | solution.py:233
  58.4 1.5 %shard_map.102 = (bf16[8,64,256]{2,1,0:T(8,128)(2,1)}, bf16[8,64,256]{2,1,0:T(8,128)(2,1)}) custom-call(bf16[8,64,256]{2,1,0:T(8,128)(2,1)S(1)} %copy-done, bf16[8,64,256]{2,1,0:T(8,128)(2,1)S(1)} %copy-done.1, s32[8,64]{1,0:T(8,128)S(1)} %copy-done.5, f32[1,256]{1,0:T(1,128)S(1)} %bitcast.9, bf16[2,4,64,256]{3,2,1,0:T(8,128)(2,1)S(1)} %get-tuple-element.14.ad_keep, ...), custom_call_target="tpu_custom_call" | custom-call | tf_op jit(solution)/shard_map/pallas_call | solution.py:209
  59.9 1.2 %shard_map.103 = (f32[256,768]{1,0:T(8,128)}, f32[256,256]{1,0:T(8,128)}, f32[1,256]{1,0:T(1,128)}) custom-call(bf16[256,256]{1,0:T(8,128)(2,1)S(1)} %add_convert_fusion.1.own, bf16[256,256]{1,0:T(8,128)(2,1)S(1)} %collective-permute-done.12.row_peer, bf16[512,256]{1,0:T(8,128)(2,1)S(1)} %collective-permute-done.13.col_peer, bf16[256,768]{1,0:T(8,128)(2,1)S(1)} %copy-done.3, ...), custom_call_target="tpu_custom_call" | custom-call | tf_op jit(solution)/shard_map/pallas_call | solution.py:209
  (38 shorter events, 1.0 us)
Async XLA Ops:
  0.6 9.2 %copy-start.1 = (bf16[8,64,256]{2,1,0:T(8,128)(2,1)S(1)}, bf16[8,64,256]{2,1,0:T(8,128)(2,1)}, u32[]{:S(2)}) copy-start(bf16[8,64,256]{2,1,0:T(8,128)(2,1)} %cot.3) | copy-start | bytes 786436
  2.2 9.3 %collective-permute-start.5 = (bf16[4,8,256]{2,1,0:T(8,128)(2,1)S(1)}, bf16[4,8,256]{2,1,0:T(8,128)(2,1)S(1)}, u32[]{:S(2)}, u32[]{:S(2)}) collective-permute-start(bf16[4,8,256]{2,1,0:T(8,128)(2,1)S(1)} %get-tuple-element.23), channel_id=1, source_target_pairs={{0,15},{1,14},{2,1},{3,0},{4,3},{5,2},{6,5},{7,4},{8,7},{9,6},{10,... | collective-permute-start | bytes 49160 | tf_op jit(solution)/shard_map/ppermute | solution.py:228
  7.6 2.2 %copy-start.5 = (s32[8,64]{1,0:T(8,128)S(1)}, s32[8,64]{1,0:T(8,128)}, u32[]{:S(2)}) copy-start(s32[8,64]{1,0:T(8,128)} %domain.3) | copy-start | bytes 6148
  7.6 3.8 %copy-start = (bf16[8,64,256]{2,1,0:T(8,128)(2,1)S(1)}, bf16[8,64,256]{2,1,0:T(8,128)(2,1)}, u32[]{:S(2)}) copy-start(bf16[8,64,256]{2,1,0:T(8,128)(2,1)} %feat.3) | copy-start | bytes 786436
  7.6 4.5 %collective-permute-start.4 = (bf16[4,8,256]{2,1,0:T(8,128)(2,1)S(1)}, bf16[4,8,256]{2,1,0:T(8,128)(2,1)S(1)}, u32[]{:S(2)}, u32[]{:S(2)}) collective-permute-start(bf16[4,8,256]{2,1,0:T(8,128)(2,1)S(1)} %get-tuple-element.24), channel_id=1, source_target_pairs={{0,1},{1,0},{2,3},{3,2},{4,5},{5,4},{6,7},{7,6},{8,9},{9,8},{10,11... | collective-permute-start | bytes 49160 | tf_op jit(solution)/shard_map/ppermute | solution.py:228
  9.2 7.8 %collective-permute-start = (bf16[4,64,256]{2,1,0:T(8,128)(2,1)S(1)}, bf16[4,64,256]{2,1,0:T(8,128)(2,1)S(1)}, u32[]{:S(2)}, u32[]{:S(2)}) collective-permute-start(bf16[4,64,256]{2,1,0:T(8,128)(2,1)S(1)} %slice.34), channel_id=1, source_target_pairs={{0,14},{2,0},{4,2},{6,4},{8,6},{10,8},{12,10},{14,12},{1,15},{3,1}... | collective-permute-start | bytes 393224 | tf_op jit(solution)/shard_map/ppermute | solution.py:228
  9.8 7.9 %copy-start.4 = (bf16[256,256]{1,0:T(8,128)(2,1)S(1)}, bf16[256,256]{1,0:T(8,128)(2,1)}, u32[]{:S(2)}) copy-start(bf16[256,256]{1,0:T(8,128)(2,1)} %wproj.1) | copy-start | bytes 393220
  9.9 7.8 %collective-permute-start.3 = (bf16[4,64,256]{2,1,0:T(8,128)(2,1)S(1)}, bf16[4,64,256]{2,1,0:T(8,128)(2,1)S(1)}, u32[]{:S(2)}, u32[]{:S(2)}) collective-permute-start(bf16[4,64,256]{2,1,0:T(8,128)(2,1)S(1)} %slice_multiply_fusion), channel_id=1, source_target_pairs={{0,14},{2,0},{4,2},{6,4},{8,6},{10,8},{12,10},{14,12},{1,15},{3,1}... | collective-permute-start | bytes 393224 | tf_op jit(solution)/shard_map/ppermute | solution.py:228
  11.4 5.6 %collective-permute-start.2 = (bf16[4,8,256]{2,1,0:T(8,128)(2,1)S(1)}, bf16[4,8,256]{2,1,0:T(8,128)(2,1)S(1)}, u32[]{:S(2)}, u32[]{:S(2)}) collective-permute-start(bf16[4,8,256]{2,1,0:T(8,128)(2,1)S(1)} %get-tuple-element.25), channel_id=1, source_target_pairs={{0,15},{1,14},{2,1},{3,0},{4,3},{5,2},{6,5},{7,4},{8,7},{9,6},{10,... | collective-permute-start | bytes 49160 | tf_op jit(solution)/shard_map/ppermute | solution.py:228
  11.5 6.3 %copy-start.6 = (f32[256]{0:T(256)S(1)}, f32[256]{0:T(256)}, u32[]{:S(2)}) copy-start(f32[256]{0:T(256)} %param.11) | copy-start | bytes 3076
  11.5 5.6 %collective-permute-start.1 = (bf16[4,8,256]{2,1,0:T(8,128)(2,1)S(1)}, bf16[4,8,256]{2,1,0:T(8,128)(2,1)S(1)}, u32[]{:S(2)}, u32[]{:S(2)}) collective-permute-start(bf16[4,8,256]{2,1,0:T(8,128)(2,1)S(1)} %get-tuple-element.26), channel_id=1, source_target_pairs={{0,1},{1,0},{2,3},{3,2},{4,5},{5,4},{6,7},{7,6},{8,9},{9,8},{10,11... | collective-permute-start | bytes 49160 | tf_op jit(solution)/shard_map/ppermute | solution.py:228
  17.7 1.0 %copy-start.2 = (bf16[256,768]{1,0:T(8,128)(2,1)S(1)}, bf16[256,768]{1,0:T(8,128)(2,1)}, u32[]{:S(2)}) copy-start(bf16[256,768]{1,0:T(8,128)(2,1)} %wqkv.3) | copy-start | bytes 1179652
  26.1 1.6 %collective-permute-start.8 = (bf16[512,256]{1,0:T(8,128)(2,1)S(1)}, bf16[512,256]{1,0:T(8,128)(2,1)S(1)}, u32[]{:S(2)}, u32[]{:S(2)}) collective-permute-start(bf16[512,256]{1,0:T(8,128)(2,1)S(1)} %get-tuple-element.19), channel_id=1, source_target_pairs={{0,1},{1,0},{2,3},{3,2},{4,5},{5,4},{6,7},{7,6},{8,9},{9,8},{10,11... | collective-permute-start | bytes 786440 | tf_op jit(solution)/shard_map/ppermute | solution.py:237
  27.8 5.6 %collective-permute-start.9 = (bf16[256,256]{1,0:T(8,128)(2,1)S(1)}, bf16[256,256]{1,0:T(8,128)(2,1)S(1)}, u32[]{:S(2)}, u32[]{:S(2)}) collective-permute-start(bf16[256,256]{1,0:T(8,128)(2,1)S(1)} %constant_dynamic-slice_fusion), channel_id=1, source_target_pairs={{0,2},{2,0},{4,6},{6,4},{8,10},{10,8},{12,14},{14,12},{1,3},{3,1},... | collective-permute-start | bytes 393224 | tf_op jit(solution)/shard_map/ppermute | solution.py:237
  33.4 5.0 %collective-permute-start.10 = (bf16[256,256]{1,0:T(8,128)(2,1)S(1)}, bf16[256,256]{1,0:T(8,128)(2,1)S(1)}, u32[]{:S(2)}, u32[]{:S(2)}) collective-permute-start(bf16[256,256]{1,0:T(8,128)(2,1)S(1)} %add_convert_fusion.3), channel_id=1, source_target_pairs={{0,4},{2,6},{4,0},{6,2},{8,12},{10,14},{12,8},{14,10},{1,5},{3,7},... | collective-permute-start | bytes 393224 | tf_op jit(solution)/shard_map/ppermute | solution.py:237
  38.5 7.3 %collective-permute-start.11 = (bf16[256,256]{1,0:T(8,128)(2,1)S(1)}, bf16[256,256]{1,0:T(8,128)(2,1)S(1)}, u32[]{:S(2)}, u32[]{:S(2)}) collective-permute-start(bf16[256,256]{1,0:T(8,128)(2,1)S(1)} %add_convert_fusion.2), channel_id=1, source_target_pairs={{0,8},{2,10},{4,12},{6,14},{8,0},{10,2},{12,4},{14,6},{1,9},{3,11}... | collective-permute-start | bytes 393224 | tf_op jit(solution)/shard_map/ppermute | solution.py:237
  45.9 10.7 %collective-permute-start.12 = (bf16[256,256]{1,0:T(8,128)(2,1)S(1)}, bf16[256,256]{1,0:T(8,128)(2,1)S(1)}, u32[]{:S(2)}, u32[]{:S(2)}) collective-permute-start(bf16[256,256]{1,0:T(8,128)(2,1)S(1)} %add_convert_fusion.1.own), channel_id=1, source_target_pairs={{0,2},{2,0},{4,6},{6,4},{8,10},{10,8},{12,14},{14,12},{1,3},{3,1},... | collective-permute-start | bytes 393224 | tf_op jit(solution)/shard_map/ppermute | solution.py:237
  46.5 10.2 %collective-permute-start.6 = (bf16[2,4,64,256]{3,2,1,0:T(8,128)(2,1)S(1)}, bf16[2,4,64,256]{3,2,1,0:T(8,128)(2,1)S(1)}, u32[]{:S(2)}, u32[]{:S(2)}) collective-permute-start(bf16[2,4,64,256]{3,2,1,0:T(8,128)(2,1)S(1)} %get-tuple-element.15), channel_id=1, source_target_pairs={{0,2},{2,4},{4,6},{6,8},{8,10},{10,12},{12,14},{14,0},{1,3},{3,5},... | collective-permute-start | bytes 786440 | tf_op jit(solution)/shard_map/ppermute | solution.py:233
  56.7 3.2 %collective-permute-start.13 = (bf16[512,256]{1,0:T(8,128)(2,1)S(1)}, bf16[512,256]{1,0:T(8,128)(2,1)S(1)}, u32[]{:S(2)}, u32[]{:S(2)}) collective-permute-start(bf16[512,256]{1,0:T(8,128)(2,1)S(1)} %maximum_select_fusion), channel_id=1, source_target_pairs={{0,1},{1,0},{2,3},{3,2},{4,5},{5,4},{6,7},{7,6},{8,9},{9,8},{10,11... | collective-permute-start | bytes 786440 | tf_op jit(solution)/shard_map/ppermute | solution.py:237
  56.8 3.1 %copy-start.3 = (bf16[256,768]{1,0:T(8,128)(2,1)S(1)}, bf16[256,768]{1,0:T(8,128)(2,1)}, u32[]{:S(2)}) copy-start(bf16[256,768]{1,0:T(8,128)(2,1)} %wqkv.3) | copy-start | bytes 1179652
  56.8 1.5 %collective-permute-start.7 = (bf16[2,8,8,256]{3,2,1,0:T(8,128)(2,1)S(1)}, bf16[2,8,8,256]{3,2,1,0:T(8,128)(2,1)S(1)}, u32[]{:S(2)}, u32[]{:S(2)}) collective-permute-start(bf16[2,8,8,256]{3,2,1,0:T(8,128)(2,1)S(1)} %pad_maximum_fusion), channel_id=1, source_target_pairs={{0,1},{1,0},{2,3},{3,2},{4,5},{5,4},{6,7},{7,6},{8,9},{9,8},{10,11... | collective-permute-start | bytes 196616 | tf_op jit(solution)/shard_map/ppermute | solution.py:233

commit v2 on v1

--- a/solution.py
+++ b/solution.py
@@ -36,11 +36,43 @@
     return [dot(flags, (row_ids == row).astype(F32).astype(BF16), 0, 0) for row in rows]
 
 
+def pack_kernel(
+    feat, cot, domain_hbm, wqkv_hbm, wproj_hbm, gain_hbm,
+    rows_out, right_out, corner_out, held, domain, wqkv, wproj, gain,
+    sems,
+):
+    channels = feat.shape[-1]
+    copies = [
+        pltpu.make_async_copy(source, target, sems.at[i])
+        for i, (source, target) in enumerate((
+            (cot, held),
+            (domain_hbm, domain),
+            (feat.at[0:SHIFT], rows_out.at[0]),
+            (feat.at[SHIFT:WIN, 0:WIN], right_out.at[0]),
+            (feat.at[0:SHIFT, 0:WIN], corner_out.at[0]),
+            (wqkv_hbm, wqkv),
+            (wproj_hbm, wproj),
+            (gain_hbm, gain),
+        ))
+    ]
+    for copy in copies:
+        copy.start()
+    copies[0].wait()
+    copies[1].wait()
+    masks = domain_rows(domain, range(WIN), channels)
+    for i in range(SHIFT):
+        masked = held[i].astype(F32) * masks[i]
+        rows_out[1, i] = masked.astype(BF16)
+        corner_out[1, i] = masked[0:WIN].astype(BF16)
+        edge = held[SHIFT + i, 0:WIN, :].astype(F32) * masks[SHIFT + i][0:WIN]
+        right_out[1, i] = edge.astype(BF16)
+    for copy in copies[2:]:
+        copy.wait()
+
+
 def block_kernel(
-    feat, feat_below, feat_right, feat_corner,
-    cot, cot_below, cot_right, cot_corner,
-    domain, wqkv, wproj, gain,
-    keep, send, ad_keep, ad_send,
+    feat, cot, domain, below, right, corner, wqkv, wproj, gain,
+    keep, send, att_keep, att_send, dn_keep, dn_send,
     buf, shifted, projected, dattended, dcontext, context, dprojected, grads,
 ):
     tile_rows, cols, channels = feat.shape
@@ -50,7 +82,7 @@
     group_heads = HEADS // 2
     head_dim = channels // HEADS
 
-    assemble_shifted(buf, feat[SHIFT:WIN].astype(F32), feat_below, feat_right, feat_corner)
+    assemble_shifted(buf, feat[SHIFT:WIN].astype(F32), below.at[0], right.at[0], corner.at[0])
     for w in range(windows):
         x = buf[:, SHIFT + WIN * w : SHIFT + WIN * (w + 1), :].reshape(cells, channels)
         centred = x - jnp.mean(x, -1, keepdims=True)
@@ -60,7 +92,7 @@
 
     masks = domain_rows(domain, range(SHIFT, WIN), channels)
     own = jnp.stack([cot[SHIFT + i].astype(F32) * masks[i] for i in range(SHIFT)], 0)
-    assemble_shifted(buf, own, cot_below, cot_right, cot_corner)
+    assemble_shifted(buf, own, below.at[1], right.at[1], corner.at[1])
     for w in range(windows):
         x = buf[:, SHIFT + WIN * w : SHIFT + WIN * (w + 1), :].reshape(cells, channels)
         dattended[cells * w : cells * (w + 1), :] = x.astype(BF16)
@@ -138,38 +170,43 @@
         pl.ds(pl.multiple_of((1 - mine) * 2 * channels, 2 * channels), 2 * channels), :
     ]
 
-    def leave(slot):
-        ad_keep[slot] = buf[0:SHIFT, 0:cols, :].astype(BF16)
-        ad_send[slot] = buf[SHIFT:WIN, 0:cols, :].astype(BF16)
+    def leave(stay, go):
+        stay[...] = buf[0:SHIFT, 0:cols, :].astype(BF16)
+        go[...] = buf[SHIFT:WIN, 0:cols, :].astype(BF16)
 
     for w in range(windows):
         rows = slice(cells * w, cells * (w + 1))
         buf[:, WIN * w : WIN * (w + 1), :] = dot(context[rows, :], wproj[...], 1, 0).reshape(
             WIN, WIN, channels
         )
-    leave(0)
+    leave(att_keep, att_send)
     for w in range(windows):
         rows = slice(cells * w, cells * (w + 1))
         buf[:, WIN * w : WIN * (w + 1), :] = dot(dprojected[rows, :], wqkv[...], 1, 1).reshape(
             WIN, WIN, channels
         )
-    leave(1)
-
-
-def finish_kernel(feat, cot, domain, gain, ad_keep, ad_rows, ad_cols, updated, grad_features, buf):
+    leave(dn_keep, dn_send)
+
+
+def finish_kernel(
+    feat, cot, domain, gain, att_keep, att_rows, dn_keep, dn_rows, edges,
+    updated, grad_features,
+    buf,
+):
     tile_rows, cols, channels = feat.shape
     masks = domain_rows(domain, range(WIN), channels)
 
-    def unshifted(slot):
-        buf[:, 0:WIN, :] = ad_cols[slot].astype(F32)
-        buf[0:SHIFT, WIN : WIN + cols, :] = ad_rows[slot].astype(F32)
-        buf[SHIFT:WIN, WIN : WIN + cols, :] = ad_keep[slot].astype(F32)
-
-    unshifted(0)
+    def unshifted(slot, stayed, came):
+        buf[0:SHIFT, 0:WIN, :] = edges[2 * slot].astype(F32)
+        buf[SHIFT:WIN, 0:WIN, :] = edges[2 * slot + 1].astype(F32)
+        buf[0:SHIFT, WIN : WIN + cols, :] = came[...].astype(F32)
+        buf[SHIFT:WIN, WIN : WIN + cols, :] = stayed[...].astype(F32)
+
+    unshifted(0, att_keep, att_rows)
     for i in range(WIN):
         back = buf[i, SHIFT : SHIFT + cols, :]
         updated[i] = (feat[i].astype(F32) + masks[i] * back).astype(BF16)
-    unshifted(1)
+    unshifted(1, dn_keep, dn_rows)
     for i in range(WIN):
         upstream = buf[i, SHIFT : SHIFT + cols, :] * gain[...]
         x = feat[i].astype(F32)
@@ -205,10 +242,19 @@
     grad_gain[...] = total[0:1, :] / gain[...]
 
 
-def run(kernel, out_shapes, scratch, *operands):
+VMEM = pl.BlockSpec(memory_space=pltpu.MemorySpace.VMEM)
+HBM = pl.BlockSpec(memory_space=pltpu.MemorySpace.HBM)
+
+
+def run(kernel, out_shapes, scratch, *operands, unstaged=()):
+    operands = [
+        pltpu.with_memory_space_constraint(a, pltpu.MemorySpace.HBM) if i in unstaged else a
+        for i, a in enumerate(operands)
+    ]
     return pl.pallas_call(
         kernel,
         out_shape=out_shapes,
+        in_specs=[HBM if i in unstaged else VMEM for i in range(len(operands))],
         scratch_shapes=scratch,
         compiler_params=pltpu.CompilerParams(vmem_limit_bytes=48 << 20),
     )(*operands)
@@ -246,24 +292,39 @@
     gain = norm_gain.reshape(1, channels)
     tokens = tile_rows * cols
 
-    feat_below = ahead(features[:SHIFT], ("row",))
-    feat_right = ahead(features[SHIFT:, :WIN], ("col",))
-    feat_corner = ahead(features[:SHIFT, :WIN], ("row", "col"))
-    flags = domain.astype(BF16)[..., None]
-    cot_below = ahead(cotangent[:SHIFT] * flags[:SHIFT], ("row",))
-    cot_right = ahead(cotangent[SHIFT:, :WIN] * flags[SHIFT:, :WIN], ("col",))
-    cot_corner = ahead(cotangent[:SHIFT, :WIN] * flags[:SHIFT, :WIN], ("row", "col"))
-
     def shape(dims, dtype):
         return jax.ShapeDtypeStruct(dims, dtype)
 
-    keep, send, ad_keep, ad_send = run(
+    rows_out, right_out, corner_out, cotangent, domain, qkv_weight, proj_weight, gain = run(
+        pack_kernel,
+        (
+            shape((2, SHIFT, cols, channels), BF16),
+            shape((2, SHIFT, WIN, channels), BF16),
+            shape((2, SHIFT, WIN, channels), BF16),
+            shape(cotangent.shape, cotangent.dtype),
+            shape(domain.shape, domain.dtype),
+            shape(qkv_weight.shape, qkv_weight.dtype),
+            shape(proj_weight.shape, proj_weight.dtype),
+            shape(gain.shape, gain.dtype),
+        ),
+        [pltpu.SemaphoreType.DMA((8,))],
+        features, cotangent, domain, qkv_weight, proj_weight, gain,
+        unstaged=(0, 1, 2, 3, 4, 5),
+    )
+    below = ahead(rows_out, ("row",))
+    right = ahead(right_out, ("col",))
+    corner = ahead(corner_out, ("row", "col"))
+
+    strip = shape((SHIFT, cols, channels), BF16)
+    keep, send, att_keep, att_send, dn_keep, dn_send = run(
         block_kernel,
         (
             shape((2 * channels, channels), BF16),
             shape((2 * channels, channels), BF16),
-            shape((2, SHIFT, cols, channels), BF16),
-            shape((2, SHIFT, cols, channels), BF16),
+            strip,
+            strip,
+            strip,
+            strip,
         ),
         [
             pltpu.VMEM((WIN, cols + WIN, channels), F32),
@@ -275,10 +336,10 @@
             pltpu.VMEM((tokens, 3 * channels), BF16),
             pltpu.VMEM((4 * channels, channels), BF16),
         ],
-        features, feat_below, feat_right, feat_corner,
-        cotangent, cot_below, cot_right, cot_corner,
-        domain, qkv_weight, proj_weight, gain,
-    )
+        features, cotangent, domain, below, right, corner, qkv_weight, proj_weight, gain,
+    )
+    att_rows = behind(att_send, "row")
+    dn_rows = behind(dn_send, "row")
 
     summed = add16(keep, swap(send, "col", 1))
     mine_row = lax.axis_index("row") % 2
@@ -287,14 +348,28 @@
     own = add16(mine, swap(other, "row", 1))
     bit = 2
     while bit < lax.axis_size("row"):
+        if bit == 4:
+            own, att_rows = lax.optimization_barrier((own, att_rows))
         own = add16(own, swap(own, "row", bit))
         bit *= 2
+    own, dn_rows = lax.optimization_barrier((own, dn_rows))
+    edges = jnp.stack(
+        [part[:, cols - WIN :] for part in (att_rows, att_keep, dn_rows, dn_keep)], 0
+    )
+    edges = behind(edges, "col")
     row_peer = swap(own, "row", 1)
     pair = jnp.where(
         mine_row == 0,
         jnp.concatenate([own, row_peer], 0),
         jnp.concatenate([row_peer, own], 0),
     )
+    updated, grad_features = run(
+        finish_kernel,
+        (shape(features.shape, BF16), shape(features.shape, BF16)),
+        [pltpu.VMEM((WIN, cols + WIN, channels), F32)],
+        features, cotangent, domain, gain, att_keep, att_rows, dn_keep, dn_rows, edges,
+    )
+    pair, updated, grad_features = lax.optimization_barrier((pair, updated, grad_features))
     col_peer = swap(pair, "col", 1)
     grad_qkv, grad_proj, grad_gain = run(
         sums_kernel,
@@ -307,15 +382,6 @@
         own, row_peer, col_peer, qkv_weight, gain,
     )
 
-    ad_rows = behind(ad_send, "row")
-    edge = jnp.concatenate([ad_rows[:, :, cols - WIN :], ad_keep[:, :, cols - WIN :]], 1)
-    ad_cols = behind(edge, "col")
-    updated, grad_features = run(
-        finish_kernel,
-        (shape(features.shape, BF16), shape(features.shape, BF16)),
-        [pltpu.VMEM((WIN, cols + WIN, channels), F32)],
-        features, cotangent, domain, gain, ad_keep, ad_rows, ad_cols,
-    )
     return updated, grad_features, grad_qkv, grad_proj, grad_gain.reshape(channels)
 
 

time: 61.4 us -> 53.3 us (0.87)
  waiting for transfers between devices: 33.4 us -> 19.9 us
  starting transfers between devices: 12.9 us -> 20.4 us
  local copies, waits for them, and re-layouts: 1.99 us -> 0.04 us
  other arithmetic: 1.94 us -> 0.3 us
  Pallas kernels: 10.1 us -> 11.4 us
    ppermute x6, waiting for transfers between devices: 26.8 us -> 13 us  [swap(): lax.ppermute(array, axis, [(i, i ^ bit) for i in range(lax.axis_size(axis...]
    ppermute x6, starting transfers between devices: 2.1 us -> 10.7 us  [swap(): lax.ppermute(array, axis, [(i, i ^ bit) for i in range(lax.axis_size(axis...]
    ppermute x6 -> x3, starting transfers between devices: 8.79 us -> 6.68 us  [ahead(): return lax.ppermute(array, axes if len(axes) > 1 else axes[0], pairs)]
    pallas_call x3 -> x4, Pallas kernels: 10.1 us -> 11.4 us  [run(): pl.pallas_call(kernel, out_shape=out_shapes, in_specs=[HBM if i in unstag...]
    ppermute x2 -> x3, starting transfers between devices: 2 us -> 3.07 us  [behind(): lax.ppermute(array, axis, [(i, (i + 1) % peers) for i in range(peers)])]
    unnamed x14 -> x2, local copies, waits for them, and re-layouts: 1.03 us -> 0.01 us
    slice x5 -> x0, local copies, waits for them, and re-layouts: 0.94 us -> none  [the longest x1 0.91 us: on_device(): feat_below = ahead(features[:SHIFT], ('row',))]
    mul x2 -> x0, other arithmetic: 0.91 us -> none  [the longest x1 0.81 us: on_device(): cotangent[:SHIFT, :WIN] * flags[:SHIFT, :WIN]]
  transfers between devices with their start and end apart: 14 -> 12, of which waited for: 8 -> 9; matrix products, arithmetic and copies ran while one was open for 2% -> 0% of each run, Pallas kernels for 2% -> 3%
where the time goes in v2:
time: 53.3 us; the launch traced here: 52.8 us
  starting transfers between devices  20.4 us (38%)
  waiting for transfers between devices  19.9 us (37%)
  Pallas kernels  11.4 us (21%)
  between operations  0.78 us (1%)
    ppermute x6, waiting for transfers between devices, swap(): lax.ppermute(array, axis, [(i, i ^ bit) for i in range(lax.axis_size(axis...  13 us
    pallas_call x4, Pallas kernels, run(): pl.pallas_call(kernel, out_shape=out_shapes, in_specs=[HBM if i in unstag...  11.4 us
    ppermute x6, starting transfers between devices, swap(): lax.ppermute(array, axis, [(i, i ^ bit) for i in range(lax.axis_size(axis...  10.7 us
    ppermute x3, starting transfers between devices, ahead(): return lax.ppermute(array, axes if len(axes) > 1 else axes[0], pairs)  6.68 us
    ppermute x3, waiting for transfers between devices, ahead(): return lax.ppermute(array, axes if len(axes) > 1 else axes[0], pairs)  5.62 us
    ppermute x3, starting transfers between devices, behind(): lax.ppermute(array, axis, [(i, (i + 1) % peers) for i in range(peers)])  3.07 us
    ppermute x3, waiting for transfers between devices, behind(): lax.ppermute(array, axis, [(i, (i + 1) % peers) for i in range(peers)])  1.24 us
  transfers between devices with their start and end apart: 12, of which 9 were waited for; matrix products, arithmetic and copies ran while one was open for 0% of the time, Pallas kernels for 3%

profile of v2, /device:TPU:0, one launch (start us, length us, event | category | flops | bytes accessed | tf_op | source)
XLA Modules:
  0.0 52.8 jit_solution(4102074766166156485)
XLA Ops:
  0.6 1.3 %shard_map.101 = (bf16[2,4,64,256]{3,2,1,0:T(8,128)(2,1)S(1)}, bf16[2,4,8,256]{3,2,1,0:T(8,128)(2,1)S(1)}, bf16[2,4,8,256]{3,2,1,0:T(8,128)(2,1)S(1)}, bf16[8,64...) custom-call(bf16[8,64,256]{2,1,0:T(8,128)(2,1)} %feat.5, ...), custom_call_target="tpu_custom_call" | custom-call | tf_op jit(solution)/shard_map/pallas_call | solution.py:254
  2.0 6.0 %collective-permute-start = (bf16[2,4,64,256]{3,2,1,0:T(8,128)(2,1)S(1)}, bf16[2,4,64,256]{3,2,1,0:T(8,128)(2,1)S(1)}, u32[]{:S(2)}, u32[]{:S(2)}) collective-permute-start(bf16[2,4,64,256]{3,2,1,0:T(8,128)(2,1)S(1)} %get-tuple-element.33), channel_id=1, source_target_pairs={{0,14},{2,0},{4,2},{6,4},{8,6},{10,8},{12,10},{14,12},{1,15},{3,1}... | collective-permute-start | bytes 786440 | tf_op jit(solution)/shard_map/ppermute | solution.py:274
  8.0 0.7 %collective-permute-start.2 = (bf16[2,4,8,256]{3,2,1,0:T(8,128)(2,1)S(1)}, bf16[2,4,8,256]{3,2,1,0:T(8,128)(2,1)S(1)}, u32[]{:S(2)}, u32[]{:S(2)}) collective-permute-start(bf16[2,4,8,256]{3,2,1,0:T(8,128)(2,1)S(1)} %get-tuple-element.35), channel_id=1, source_target_pairs={{0,15},{1,14},{2,1},{3,0},{4,3},{5,2},{6,5},{7,4},{8,7},{9,6},{10,... | collective-permute-start | bytes 98312 | tf_op jit(solution)/shard_map/ppermute | solution.py:274
  8.7 0.6 %collective-permute-done.1.right = bf16[2,4,8,256]{3,2,1,0:T(8,128)(2,1)S(1)} collective-permute-done((bf16[2,4,8,256]{3,2,1,0:T(8,128)(2,1)S(1)}, bf16[2,4,8,256]{3,2,1,0:T(8,128)(2,1)S(1)}, u32[]{:S(2)}, u32[]{:S(2)}) %collective-permute-start.1) | collective-permute-done | bytes 32800 | tf_op jit(solution)/shard_map/ppermute | solution.py:274
  9.2 5.1 %collective-permute-done.2.corner = bf16[2,4,8,256]{3,2,1,0:T(8,128)(2,1)S(1)} collective-permute-done((bf16[2,4,8,256]{3,2,1,0:T(8,128)(2,1)S(1)}, bf16[2,4,8,256]{3,2,1,0:T(8,128)(2,1)S(1)}, u32[]{:S(2)}, u32[]{:S(2)}) %collective-permute-start.2) | collective-permute-done | bytes 32800 | tf_op jit(solution)/shard_map/ppermute | solution.py:274
  14.3 7.3 %shard_map.102 = (bf16[512,256]{1,0:T(8,128)(2,1)S(1)}, bf16[512,256]{1,0:T(8,128)(2,1)S(1)}, bf16[4,64,256]{2,1,0:T(8,128)(2,1)S(1)}, bf16[4,64,256]{2,1,0:T(8,...) custom-call(bf16[8,64,256]{2,1,0:T(8,128)(2,1)S(1)} %copy-done, ...), custom_call_target="tpu_custom_call" | custom-call | tf_op jit(solution)/shard_map/pallas_call | solution.py:254
  21.6 0.1 collective-permute-start.3
  21.7 1.5 %collective-permute-done.3 = bf16[512,256]{1,0:T(8,128)(2,1)S(1)} collective-permute-done((bf16[512,256]{1,0:T(8,128)(2,1)S(1)}, bf16[512,256]{1,0:T(8,128)(2,1)S(1)}, u32[]{:S(2)}, u32[]{:S(2)}) %collective-permute-start.3) | collective-permute-done | bytes 262176 | tf_op jit(solution)/shard_map/ppermute | solution.py:283
  23.2 0.1 add_convert_fusion
  23.4 2.0 %collective-permute-start.6 = (bf16[4,64,256]{2,1,0:T(8,128)(2,1)S(1)}, bf16[4,64,256]{2,1,0:T(8,128)(2,1)S(1)}, u32[]{:S(2)}, u32[]{:S(2)}) collective-permute-start(bf16[4,64,256]{2,1,0:T(8,128)(2,1)S(1)} %get-tuple-element.41), channel_id=1, source_target_pairs={{0,2},{2,4},{4,6},{6,8},{8,10},{10,12},{12,14},{14,0},{1,3},{3,5},... | collective-permute-start | bytes 393224 | tf_op jit(solution)/shard_map/ppermute | solution.py:279
  25.4 1.0 %collective-permute-start.8 = (bf16[4,64,256]{2,1,0:T(8,128)(2,1)S(1)}, bf16[4,64,256]{2,1,0:T(8,128)(2,1)S(1)}, u32[]{:S(2)}, u32[]{:S(2)}) collective-permute-start(bf16[4,64,256]{2,1,0:T(8,128)(2,1)S(1)} %get-tuple-element.43), channel_id=1, source_target_pairs={{0,2},{2,4},{4,6},{6,8},{8,10},{10,12},{12,14},{14,0},{1,3},{3,5},... | collective-permute-start | bytes 393224 | tf_op jit(solution)/shard_map/ppermute | solution.py:279
  26.4 2.5 %collective-permute-done.4 = bf16[256,256]{1,0:T(8,128)(2,1)S(1)} collective-permute-done((bf16[256,256]{1,0:T(8,128)(2,1)S(1)}, bf16[256,256]{1,0:T(8,128)(2,1)S(1)}, u32[]{:S(2)}, u32[]{:S(2)}) %collective-permute-start.4) | collective-permute-done | bytes 131104 | tf_op jit(solution)/shard_map/ppermute | solution.py:283
  29.0 4.9 %collective-permute-start.5 = (bf16[256,256]{1,0:T(8,128)(2,1)S(1)}, bf16[256,256]{1,0:T(8,128)(2,1)S(1)}, u32[]{:S(2)}, u32[]{:S(2)}) collective-permute-start(bf16[256,256]{1,0:T(8,128)(2,1)S(1)} %add_convert_fusion.3), channel_id=1, source_target_pairs={{0,4},{2,6},{4,0},{6,2},{8,12},{10,14},{12,8},{14,10},{1,5},{3,7},... | collective-permute-start | bytes 393224 | tf_op jit(solution)/shard_map/ppermute | solution.py:283
  33.9 4.2 %collective-permute-done.5 = bf16[256,256]{1,0:T(8,128)(2,1)S(1)} collective-permute-done((bf16[256,256]{1,0:T(8,128)(2,1)S(1)}, bf16[256,256]{1,0:T(8,128)(2,1)S(1)}, u32[]{:S(2)}, u32[]{:S(2)}) %collective-permute-start.5) | collective-permute-done | bytes 131104 | tf_op jit(solution)/shard_map/ppermute | solution.py:283
  38.1 3.6 %collective-permute-start.7 = (bf16[256,256]{1,0:T(8,128)(2,1)S(1)}, bf16[256,256]{1,0:T(8,128)(2,1)S(1)}, u32[]{:S(2)}, u32[]{:S(2)}) collective-permute-start(bf16[256,256]{1,0:T(8,128)(2,1)S(1)} %add_convert_fusion.2), channel_id=1, source_target_pairs={{0,8},{2,10},{4,12},{6,14},{8,0},{10,2},{12,4},{14,6},{1,9},{3,11}... | collective-permute-start | bytes 393224 | tf_op jit(solution)/shard_map/ppermute | solution.py:283
  41.7 2.9 %collective-permute-done.7 = bf16[256,256]{1,0:T(8,128)(2,1)S(1)} collective-permute-done((bf16[256,256]{1,0:T(8,128)(2,1)S(1)}, bf16[256,256]{1,0:T(8,128)(2,1)S(1)}, u32[]{:S(2)}, u32[]{:S(2)}) %collective-permute-start.7) | collective-permute-done | bytes 131104 | tf_op jit(solution)/shard_map/ppermute | solution.py:283
  44.7 1.9 %collective-permute-start.9 = (bf16[256,256]{1,0:T(8,128)(2,1)S(1)}, bf16[256,256]{1,0:T(8,128)(2,1)S(1)}, u32[]{:S(2)}, u32[]{:S(2)}) collective-permute-start(bf16[256,256]{1,0:T(8,128)(2,1)S(1)} %add_convert_fusion.1.own), channel_id=1, source_target_pairs={{0,2},{2,0},{4,6},{6,4},{8,10},{10,8},{12,14},{14,12},{1,3},{3,1},... | collective-permute-start | bytes 393224 | tf_op jit(solution)/shard_map/ppermute | solution.py:283
  46.7 0.1 collective-permute-start.10
  46.8 1.2 %collective-permute-done.10.edges = bf16[4,4,8,256]{3,2,1,0:T(8,128)(2,1)S(1)} collective-permute-done((bf16[4,4,8,256]{3,2,1,0:T(8,128)(2,1)S(1)}, bf16[4,4,8,256]{3,2,1,0:T(8,128)(2,1)S(1)}, u32[]{:S(2)}, u32[]{:S(2)}) %collective-permute-start.10) | collective-permute-done | bytes 65568 | tf_op jit(solution)/shard_map/ppermute | solution.py:279
  48.0 1.5 %shard_map.103 = (bf16[8,64,256]{2,1,0:T(8,128)(2,1)}, bf16[8,64,256]{2,1,0:T(8,128)(2,1)}) custom-call(bf16[8,64,256]{2,1,0:T(8,128)(2,1)S(1)} %copy-done, bf16[8,64,256]{2,1,0:T(8,128)(2,1)S(1)} %get-tuple-element.31.cot, s32[8,64]{1,0:T(8,128)S(1)} %get-tuple-element.32.domain, f32[1,256]{1,0:T(1,128)S(1)} %get-tuple-element.38.gain, ...), custom_call_target="tpu_custom_call" | custom-call | tf_op jit(solution)/shard_map/pallas_call | solution.py:254
  49.5 0.4 collective-permute-done.9.row_peer
  49.9 0.1 maximum_select_fusion
  50.1 1.5 %collective-permute-done.11.col_peer = bf16[512,256]{1,0:T(8,128)(2,1)S(1)} collective-permute-done((bf16[512,256]{1,0:T(8,128)(2,1)S(1)}, bf16[512,256]{1,0:T(8,128)(2,1)S(1)}, u32[]{:S(2)}, u32[]{:S(2)}) %collective-permute-start.11) | collective-permute-done | bytes 262176 | tf_op jit(solution)/shard_map/ppermute | solution.py:283
  51.6 1.2 %shard_map.104 = (f32[256,768]{1,0:T(8,128)}, f32[256,256]{1,0:T(8,128)}, f32[1,256]{1,0:T(1,128)}) custom-call(bf16[256,256]{1,0:T(8,128)(2,1)S(1)} %add_convert_fusion.1.own, bf16[256,256]{1,0:T(8,128)(2,1)S(1)} %collective-permute-done.9.row_peer, bf16[512,256]{1,0:T(8,128)(2,1)S(1)} %collective-permute-done.11.col_peer, ...), custom_call_target="tpu_custom_call" | custom-call | tf_op jit(solution)/shard_map/pallas_call | solution.py:254
  (16 shorter events, 0.3 us)
Async XLA Ops:
  0.6 13.6 %copy-start = (bf16[8,64,256]{2,1,0:T(8,128)(2,1)S(1)}, bf16[8,64,256]{2,1,0:T(8,128)(2,1)}, u32[]{:S(2)}) copy-start(bf16[8,64,256]{2,1,0:T(8,128)(2,1)} %feat.5) | copy-start | bytes 786436
  2.0 12.3 %collective-permute-start = (bf16[2,4,64,256]{3,2,1,0:T(8,128)(2,1)S(1)}, bf16[2,4,64,256]{3,2,1,0:T(8,128)(2,1)S(1)}, u32[]{:S(2)}, u32[]{:S(2)}) collective-permute-start(bf16[2,4,64,256]{3,2,1,0:T(8,128)(2,1)S(1)} %get-tuple-element.33), channel_id=1, source_target_pairs={{0,14},{2,0},{4,2},{6,4},{8,6},{10,8},{12,10},{14,12},{1,15},{3,1}... | collective-permute-start | bytes 786440 | tf_op jit(solution)/shard_map/ppermute | solution.py:274
  8.0 1.2 %collective-permute-start.1 = (bf16[2,4,8,256]{3,2,1,0:T(8,128)(2,1)S(1)}, bf16[2,4,8,256]{3,2,1,0:T(8,128)(2,1)S(1)}, u32[]{:S(2)}, u32[]{:S(2)}) collective-permute-start(bf16[2,4,8,256]{3,2,1,0:T(8,128)(2,1)S(1)} %get-tuple-element.34), channel_id=1, source_target_pairs={{0,1},{1,0},{2,3},{3,2},{4,5},{5,4},{6,7},{7,6},{8,9},{9,8},{10,11... | collective-permute-start | bytes 98312 | tf_op jit(solution)/shard_map/ppermute | solution.py:274
  8.0 6.3 %collective-permute-start.2 = (bf16[2,4,8,256]{3,2,1,0:T(8,128)(2,1)S(1)}, bf16[2,4,8,256]{3,2,1,0:T(8,128)(2,1)S(1)}, u32[]{:S(2)}, u32[]{:S(2)}) collective-permute-start(bf16[2,4,8,256]{3,2,1,0:T(8,128)(2,1)S(1)} %get-tuple-element.35), channel_id=1, source_target_pairs={{0,15},{1,14},{2,1},{3,0},{4,3},{5,2},{6,5},{7,4},{8,7},{9,6},{10,... | collective-permute-start | bytes 98312 | tf_op jit(solution)/shard_map/ppermute | solution.py:274
  21.6 1.6 %collective-permute-start.3 = (bf16[512,256]{1,0:T(8,128)(2,1)S(1)}, bf16[512,256]{1,0:T(8,128)(2,1)S(1)}, u32[]{:S(2)}, u32[]{:S(2)}) collective-permute-start(bf16[512,256]{1,0:T(8,128)(2,1)S(1)} %get-tuple-element.40), channel_id=1, source_target_pairs={{0,1},{1,0},{2,3},{3,2},{4,5},{5,4},{6,7},{7,6},{8,9},{9,8},{10,11... | collective-permute-start | bytes 786440 | tf_op jit(solution)/shard_map/ppermute | solution.py:283
  23.3 5.6 %collective-permute-start.4 = (bf16[256,256]{1,0:T(8,128)(2,1)S(1)}, bf16[256,256]{1,0:T(8,128)(2,1)S(1)}, u32[]{:S(2)}, u32[]{:S(2)}) collective-permute-start(bf16[256,256]{1,0:T(8,128)(2,1)S(1)} %constant_dynamic-slice_fusion), channel_id=1, source_target_pairs={{0,2},{2,0},{4,6},{6,4},{8,10},{10,8},{12,14},{14,12},{1,3},{3,1},... | collective-permute-start | bytes 393224 | tf_op jit(solution)/shard_map/ppermute | solution.py:283
  23.4 14.7 %collective-permute-start.6 = (bf16[4,64,256]{2,1,0:T(8,128)(2,1)S(1)}, bf16[4,64,256]{2,1,0:T(8,128)(2,1)S(1)}, u32[]{:S(2)}, u32[]{:S(2)}) collective-permute-start(bf16[4,64,256]{2,1,0:T(8,128)(2,1)S(1)} %get-tuple-element.41), channel_id=1, source_target_pairs={{0,2},{2,4},{4,6},{6,8},{8,10},{10,12},{12,14},{14,0},{1,3},{3,5},... | collective-permute-start | bytes 393224 | tf_op jit(solution)/shard_map/ppermute | solution.py:279
  25.4 19.3 %collective-permute-start.8 = (bf16[4,64,256]{2,1,0:T(8,128)(2,1)S(1)}, bf16[4,64,256]{2,1,0:T(8,128)(2,1)S(1)}, u32[]{:S(2)}, u32[]{:S(2)}) collective-permute-start(bf16[4,64,256]{2,1,0:T(8,128)(2,1)S(1)} %get-tuple-element.43), channel_id=1, source_target_pairs={{0,2},{2,4},{4,6},{6,8},{8,10},{10,12},{12,14},{14,0},{1,3},{3,5},... | collective-permute-start | bytes 393224 | tf_op jit(solution)/shard_map/ppermute | solution.py:279
  29.0 9.1 %collective-permute-start.5 = (bf16[256,256]{1,0:T(8,128)(2,1)S(1)}, bf16[256,256]{1,0:T(8,128)(2,1)S(1)}, u32[]{:S(2)}, u32[]{:S(2)}) collective-permute-start(bf16[256,256]{1,0:T(8,128)(2,1)S(1)} %add_convert_fusion.3), channel_id=1, source_target_pairs={{0,4},{2,6},{4,0},{6,2},{8,12},{10,14},{12,8},{14,10},{1,5},{3,7},... | collective-permute-start | bytes 393224 | tf_op jit(solution)/shard_map/ppermute | solution.py:283
  38.1 6.6 %collective-permute-start.7 = (bf16[256,256]{1,0:T(8,128)(2,1)S(1)}, bf16[256,256]{1,0:T(8,128)(2,1)S(1)}, u32[]{:S(2)}, u32[]{:S(2)}) collective-permute-start(bf16[256,256]{1,0:T(8,128)(2,1)S(1)} %add_convert_fusion.2), channel_id=1, source_target_pairs={{0,8},{2,10},{4,12},{6,14},{8,0},{10,2},{12,4},{14,6},{1,9},{3,11}... | collective-permute-start | bytes 393224 | tf_op jit(solution)/shard_map/ppermute | solution.py:283
  44.7 5.1 %collective-permute-start.9 = (bf16[256,256]{1,0:T(8,128)(2,1)S(1)}, bf16[256,256]{1,0:T(8,128)(2,1)S(1)}, u32[]{:S(2)}, u32[]{:S(2)}) collective-permute-start(bf16[256,256]{1,0:T(8,128)(2,1)S(1)} %add_convert_fusion.1.own), channel_id=1, source_target_pairs={{0,2},{2,0},{4,6},{6,4},{8,10},{10,8},{12,14},{14,12},{1,3},{3,1},... | collective-permute-start | bytes 393224 | tf_op jit(solution)/shard_map/ppermute | solution.py:283
  46.7 1.3 %collective-permute-start.10 = (bf16[4,4,8,256]{3,2,1,0:T(8,128)(2,1)S(1)}, bf16[4,4,8,256]{3,2,1,0:T(8,128)(2,1)S(1)}, u32[]{:S(2)}, u32[]{:S(2)}) collective-permute-start(bf16[4,4,8,256]{3,2,1,0:T(8,128)(2,1)S(1)} %pad_maximum_fusion), channel_id=1, source_target_pairs={{0,1},{1,0},{2,3},{3,2},{4,5},{5,4},{6,7},{7,6},{8,9},{9,8},{10,11... | collective-permute-start | bytes 196616 | tf_op jit(solution)/shard_map/ppermute | solution.py:279
  50.0 1.6 %collective-permute-start.11 = (bf16[512,256]{1,0:T(8,128)(2,1)S(1)}, bf16[512,256]{1,0:T(8,128)(2,1)S(1)}, u32[]{:S(2)}, u32[]{:S(2)}) collective-permute-start(bf16[512,256]{1,0:T(8,128)(2,1)S(1)} %maximum_select_fusion), channel_id=1, source_target_pairs={{0,1},{1,0},{2,3},{3,2},{4,5},{5,4},{6,7},{7,6},{8,9},{9,8},{10,11... | collective-permute-start | bytes 786440 | tf_op jit(solution)/shard_map/ppermute | solution.py:283

commit v3 on v2

--- a/solution.py
+++ b/solution.py
@@ -74,6 +74,7 @@
     feat, cot, domain, below, right, corner, wqkv, wproj, gain,
     keep, send, att_keep, att_send, dn_keep, dn_send,
     buf, shifted, projected, dattended, dcontext, context, dprojected, grads,
+    query_held, dctx_held, scores_held, dchances_held, chances_held, dscore_held,
 ):
     tile_rows, cols, channels = feat.shape
     windows = cols // WIN
@@ -83,12 +84,13 @@
     head_dim = channels // HEADS
 
     assemble_shifted(buf, feat[SHIFT:WIN].astype(F32), below.at[0], right.at[0], corner.at[0])
+    x = buf[:, SHIFT : SHIFT + cols, :]
+    centred = x - jnp.mean(x, -1, keepdims=True)
+    variance = jnp.mean(centred * centred, -1, keepdims=True)
+    normed = centred * lax.rsqrt(variance + NORM_EPSILON) * gain[...].reshape(1, 1, channels)
     for w in range(windows):
-        x = buf[:, SHIFT + WIN * w : SHIFT + WIN * (w + 1), :].reshape(cells, channels)
-        centred = x - jnp.mean(x, -1, keepdims=True)
-        variance = jnp.mean(centred * centred, -1, keepdims=True)
-        normed = centred * lax.rsqrt(variance + NORM_EPSILON) * gain[...]
-        shifted[cells * w : cells * (w + 1), :] = normed.astype(BF16)
+        tile = normed[:, WIN * w : WIN * (w + 1), :].reshape(cells, channels)
+        shifted[cells * w : cells * (w + 1), :] = tile.astype(BF16)
 
     masks = domain_rows(domain, range(SHIFT, WIN), channels)
     own = jnp.stack([cot[SHIFT + i].astype(F32) * masks[i] for i in range(SHIFT)], 0)
@@ -97,10 +99,8 @@
         x = buf[:, SHIFT + WIN * w : SHIFT + WIN * (w + 1), :].reshape(cells, channels)
         dattended[cells * w : cells * (w + 1), :] = x.astype(BF16)
 
-    step = 128
-    for m in range(0, cells * windows, step):
-        projected[m : m + step, :] = dot(shifted[m : m + step, :], wqkv[...], 1, 0).astype(BF16)
-        dcontext[m : m + step, :] = dot(dattended[m : m + step, :], wproj[...], 1, 1).astype(BF16)
+    projected[...] = dot(shifted[...], wqkv[...], 1, 0).astype(BF16)
+    dcontext[...] = dot(dattended[...], wproj[...], 1, 1).astype(BF16)
 
     last_row = lax.axis_index("row") == lax.axis_size("row") - 1
     last_col = lax.axis_index("col") == lax.axis_size("col") - 1
@@ -124,40 +124,47 @@
             out = jnp.where(in_head[h], parts[h], out)
         return out
 
-    def one_window(base, excluded):
-        for g in range(2):
+    row_excluded = jnp.logical_and(row_apart, last_row)
+    groups = [(w, g) for w in range(windows) for g in range(2)]
+    depth = scores_held.shape[0]
+    for first in range(0, len(groups), depth):
+        batch = groups[first : first + depth]
+        for n, (w, g) in enumerate(batch):
+            rows = slice(cells * w, cells * (w + 1))
             at = half * g
-            rows = pl.ds(base, cells)
-            query = projected[rows, at : at + half]
+            query_x = spread(projected[rows, at : at + half])
             key = projected[rows, channels + at : channels + at + half]
             value = projected[rows, 2 * channels + at : 2 * channels + at + half]
-            dctx = dcontext[rows, at : at + half]
-            query_x = spread(query)
-            dctx_x = spread(dctx)
-            scores = dot(key, query_x, 1, 1)
-            scores = jnp.where(excluded, MASKED_SCORE, scores)
+            dctx_x = spread(dcontext[rows, at : at + half])
+            query_held[n] = query_x
+            dctx_held[n] = dctx_x
+            scores_held[n] = dot(key, query_x, 1, 1)
+            dchances_held[n] = dot(value, dctx_x, 1, 1)
+        for n, (w, g) in enumerate(batch):
+            excluded = row_excluded
+            if w == windows - 1:
+                excluded = jnp.logical_or(excluded, jnp.logical_and(col_apart, last_col))
+            scores = jnp.where(excluded, MASKED_SCORE, scores_held[n])
             peak = jnp.max(scores, 0, keepdims=True)
             weights = jnp.exp2((scores - peak) * (scale * LOG2_E))
-            probability = weights * (1.0 / jnp.sum(weights, 0, keepdims=True))
-            prob16 = probability.astype(BF16)
-            context[rows, at : at + half] = gather(dot(prob16, value, 0, 0)).astype(BF16)
-            dprob = dot(value, dctx_x, 1, 1).astype(BF16).astype(F32)
-            mean = jnp.sum(probability * dprob, 0, keepdims=True)
-            dscore = (probability * (dprob - mean) * scale).astype(BF16)
-            dprojected[rows, at : at + half] = gather(dot(dscore, key, 0, 0)).astype(BF16)
+            chances = weights * (1.0 / jnp.sum(weights, 0, keepdims=True))
+            chances_held[n] = chances.astype(BF16)
+            dchances = dchances_held[n].astype(BF16).astype(F32)
+            mean = jnp.sum(chances * dchances, 0, keepdims=True)
+            dscore_held[n] = (chances * (dchances - mean) * scale).astype(BF16)
+        for n, (w, g) in enumerate(batch):
+            rows = slice(cells * w, cells * (w + 1))
+            at = half * g
+            key = projected[rows, channels + at : channels + at + half]
+            value = projected[rows, 2 * channels + at : 2 * channels + at + half]
+            context[rows, at : at + half] = gather(dot(chances_held[n], value, 0, 0)).astype(BF16)
+            dprojected[rows, at : at + half] = gather(dot(dscore_held[n], key, 0, 0)).astype(BF16)
             dprojected[rows, channels + at : channels + at + half] = dot(
-                dscore, query_x, 1, 0
+                dscore_held[n], query_held[n], 1, 0
             ).astype(BF16)
             dprojected[rows, 2 * channels + at : 2 * channels + at + half] = dot(
-                prob16, dctx_x, 1, 0
+                chances_held[n], dctx_held[n], 1, 0
             ).astype(BF16)
-
-    row_excluded = jnp.logical_and(row_apart, last_row)
-    for w in range(windows):
-        excluded = row_excluded
-        if w == windows - 1:
-            excluded = jnp.logical_or(excluded, jnp.logical_and(col_apart, last_col))
-        one_window(cells * w, excluded)
 
     for b in range(3):
         grads[channels * b : channels * (b + 1), :] = dot(
@@ -170,22 +177,16 @@
         pl.ds(pl.multiple_of((1 - mine) * 2 * channels, 2 * channels), 2 * channels), :
     ]
 
-    def leave(stay, go):
-        stay[...] = buf[0:SHIFT, 0:cols, :].astype(BF16)
-        go[...] = buf[SHIFT:WIN, 0:cols, :].astype(BF16)
-
+    full = dot(context[...], wproj[...], 1, 0)
     for w in range(windows):
-        rows = slice(cells * w, cells * (w + 1))
-        buf[:, WIN * w : WIN * (w + 1), :] = dot(context[rows, :], wproj[...], 1, 0).reshape(
-            WIN, WIN, channels
-        )
-    leave(att_keep, att_send)
+        tile = full[cells * w : cells * (w + 1)].reshape(WIN, WIN, channels).astype(BF16)
+        att_keep[:, WIN * w : WIN * (w + 1), :] = tile[0:SHIFT]
+        att_send[:, WIN * w : WIN * (w + 1), :] = tile[SHIFT:WIN]
+    full = dot(dprojected[...], wqkv[...], 1, 1)
     for w in range(windows):
-        rows = slice(cells * w, cells * (w + 1))
-        buf[:, WIN * w : WIN * (w + 1), :] = dot(dprojected[rows, :], wqkv[...], 1, 1).reshape(
-            WIN, WIN, channels
-        )
-    leave(dn_keep, dn_send)
+        tile = full[cells * w : cells * (w + 1)].reshape(WIN, WIN, channels).astype(BF16)
+        dn_keep[:, WIN * w : WIN * (w + 1), :] = tile[0:SHIFT]
+        dn_send[:, WIN * w : WIN * (w + 1), :] = tile[SHIFT:WIN]
 
 
 def finish_kernel(
@@ -335,6 +336,12 @@
             pltpu.VMEM((tokens, channels), BF16),
             pltpu.VMEM((tokens, 3 * channels), BF16),
             pltpu.VMEM((4 * channels, channels), BF16),
+            pltpu.VMEM((8, 4 * WIN * WIN, channels // 2), BF16),
+            pltpu.VMEM((8, 4 * WIN * WIN, channels // 2), BF16),
+            pltpu.VMEM((8, WIN * WIN, 4 * WIN * WIN), F32),
+            pltpu.VMEM((8, WIN * WIN, 4 * WIN * WIN), F32),
+            pltpu.VMEM((8, WIN * WIN, 4 * WIN * WIN), BF16),
+            pltpu.VMEM((8, WIN * WIN, 4 * WIN * WIN), BF16),
         ],
         features, cotangent, domain, below, right, corner, qkv_weight, proj_weight, gain,
     )

time: 53.3 us -> 49.4 us (0.927)
  Pallas kernels: 11.4 us -> 7.5 us
    pallas_call x4, Pallas kernels: 11.4 us -> 7.5 us  [run(): pl.pallas_call(kernel, out_shape=out_shapes, in_specs=[HBM if i in unstag...]
where the time goes in v3:
time: 49.4 us; the launch traced here: 48.9 us
  starting transfers between devices  20.4 us (41%)
  waiting for transfers between devices  19.9 us (40%)
  Pallas kernels  7.5 us (15%)
  between operations  0.78 us (2%)
    ppermute x6, waiting for transfers between devices, swap(): lax.ppermute(array, axis, [(i, i ^ bit) for i in range(lax.axis_size(axis...  13 us
    ppermute x6, starting transfers between devices, swap(): lax.ppermute(array, axis, [(i, i ^ bit) for i in range(lax.axis_size(axis...  10.7 us
    pallas_call x4, Pallas kernels, run(): pl.pallas_call(kernel, out_shape=out_shapes, in_specs=[HBM if i in unstag...  7.5 us
    ppermute x3, starting transfers between devices, ahead(): return lax.ppermute(array, axes if len(axes) > 1 else axes[0], pairs)  6.68 us
    ppermute x3, waiting for transfers between devices, ahead(): return lax.ppermute(array, axes if len(axes) > 1 else axes[0], pairs)  5.62 us
    ppermute x3, starting transfers between devices, behind(): lax.ppermute(array, axis, [(i, (i + 1) % peers) for i in range(peers)])  3.07 us
    ppermute x3, waiting for transfers between devices, behind(): lax.ppermute(array, axis, [(i, (i + 1) % peers) for i in range(peers)])  1.24 us
  transfers between devices with their start and end apart: 12, of which 9 were waited for; matrix products, arithmetic and copies ran while one was open for 0% of the time, Pallas kernels for 3%

profile of v3, /device:TPU:0, one launch (start us, length us, event | category | flops | bytes accessed | tf_op | source)
XLA Modules:
  0.0 48.9 jit_solution(15885882123187365673)
XLA Ops:
  0.6 1.3 %shard_map.101 = (bf16[2,4,64,256]{3,2,1,0:T(8,128)(2,1)S(1)}, bf16[2,4,8,256]{3,2,1,0:T(8,128)(2,1)S(1)}, bf16[2,4,8,256]{3,2,1,0:T(8,128)(2,1)S(1)}, bf16[8,64...) custom-call(bf16[8,64,256]{2,1,0:T(8,128)(2,1)} %feat.5, ...), custom_call_target="tpu_custom_call" | custom-call | tf_op jit(solution)/shard_map/pallas_call | solution.py:255
  2.0 6.0 %collective-permute-start = (bf16[2,4,64,256]{3,2,1,0:T(8,128)(2,1)S(1)}, bf16[2,4,64,256]{3,2,1,0:T(8,128)(2,1)S(1)}, u32[]{:S(2)}, u32[]{:S(2)}) collective-permute-start(bf16[2,4,64,256]{3,2,1,0:T(8,128)(2,1)S(1)} %get-tuple-element.33), channel_id=1, source_target_pairs={{0,14},{2,0},{4,2},{6,4},{8,6},{10,8},{12,10},{14,12},{1,15},{3,1}... | collective-permute-start | bytes 786440 | tf_op jit(solution)/shard_map/ppermute | solution.py:275
  8.0 0.7 %collective-permute-start.2 = (bf16[2,4,8,256]{3,2,1,0:T(8,128)(2,1)S(1)}, bf16[2,4,8,256]{3,2,1,0:T(8,128)(2,1)S(1)}, u32[]{:S(2)}, u32[]{:S(2)}) collective-permute-start(bf16[2,4,8,256]{3,2,1,0:T(8,128)(2,1)S(1)} %get-tuple-element.35), channel_id=1, source_target_pairs={{0,15},{1,14},{2,1},{3,0},{4,3},{5,2},{6,5},{7,4},{8,7},{9,6},{10,... | collective-permute-start | bytes 98312 | tf_op jit(solution)/shard_map/ppermute | solution.py:275
  8.7 0.6 %collective-permute-done.1.right = bf16[2,4,8,256]{3,2,1,0:T(8,128)(2,1)S(1)} collective-permute-done((bf16[2,4,8,256]{3,2,1,0:T(8,128)(2,1)S(1)}, bf16[2,4,8,256]{3,2,1,0:T(8,128)(2,1)S(1)}, u32[]{:S(2)}, u32[]{:S(2)}) %collective-permute-start.1) | collective-permute-done | bytes 32800 | tf_op jit(solution)/shard_map/ppermute | solution.py:275
  9.2 5.1 %collective-permute-done.2.corner = bf16[2,4,8,256]{3,2,1,0:T(8,128)(2,1)S(1)} collective-permute-done((bf16[2,4,8,256]{3,2,1,0:T(8,128)(2,1)S(1)}, bf16[2,4,8,256]{3,2,1,0:T(8,128)(2,1)S(1)}, u32[]{:S(2)}, u32[]{:S(2)}) %collective-permute-start.2) | collective-permute-done | bytes 32800 | tf_op jit(solution)/shard_map/ppermute | solution.py:275
  14.3 3.4 %shard_map.102 = (bf16[512,256]{1,0:T(8,128)(2,1)S(1)}, bf16[512,256]{1,0:T(8,128)(2,1)S(1)}, bf16[4,64,256]{2,1,0:T(8,128)(2,1)S(1)}, bf16[4,64,256]{2,1,0:T(8,...) custom-call(bf16[8,64,256]{2,1,0:T(8,128)(2,1)S(1)} %copy-done, ...), custom_call_target="tpu_custom_call" | custom-call | tf_op jit(solution)/shard_map/pallas_call | solution.py:255
  17.7 0.1 collective-permute-start.3
  17.8 1.5 %collective-permute-done.3 = bf16[512,256]{1,0:T(8,128)(2,1)S(1)} collective-permute-done((bf16[512,256]{1,0:T(8,128)(2,1)S(1)}, bf16[512,256]{1,0:T(8,128)(2,1)S(1)}, u32[]{:S(2)}, u32[]{:S(2)}) %collective-permute-start.3) | collective-permute-done | bytes 262176 | tf_op jit(solution)/shard_map/ppermute | solution.py:284
  19.3 0.1 add_convert_fusion
  19.4 0.1 collective-permute-start.4
  19.5 2.0 %collective-permute-start.6 = (bf16[4,64,256]{2,1,0:T(8,128)(2,1)S(1)}, bf16[4,64,256]{2,1,0:T(8,128)(2,1)S(1)}, u32[]{:S(2)}, u32[]{:S(2)}) collective-permute-start(bf16[4,64,256]{2,1,0:T(8,128)(2,1)S(1)} %get-tuple-element.41), channel_id=1, source_target_pairs={{0,2},{2,4},{4,6},{6,8},{8,10},{10,12},{12,14},{14,0},{1,3},{3,5},... | collective-permute-start | bytes 393224 | tf_op jit(solution)/shard_map/ppermute | solution.py:280
  21.5 1.0 %collective-permute-start.8 = (bf16[4,64,256]{2,1,0:T(8,128)(2,1)S(1)}, bf16[4,64,256]{2,1,0:T(8,128)(2,1)S(1)}, u32[]{:S(2)}, u32[]{:S(2)}) collective-permute-start(bf16[4,64,256]{2,1,0:T(8,128)(2,1)S(1)} %get-tuple-element.43), channel_id=1, source_target_pairs={{0,2},{2,4},{4,6},{6,8},{8,10},{10,12},{12,14},{14,0},{1,3},{3,5},... | collective-permute-start | bytes 393224 | tf_op jit(solution)/shard_map/ppermute | solution.py:280
  22.5 2.5 %collective-permute-done.4 = bf16[256,256]{1,0:T(8,128)(2,1)S(1)} collective-permute-done((bf16[256,256]{1,0:T(8,128)(2,1)S(1)}, bf16[256,256]{1,0:T(8,128)(2,1)S(1)}, u32[]{:S(2)}, u32[]{:S(2)}) %collective-permute-start.4) | collective-permute-done | bytes 131104 | tf_op jit(solution)/shard_map/ppermute | solution.py:284
  25.1 4.9 %collective-permute-start.5 = (bf16[256,256]{1,0:T(8,128)(2,1)S(1)}, bf16[256,256]{1,0:T(8,128)(2,1)S(1)}, u32[]{:S(2)}, u32[]{:S(2)}) collective-permute-start(bf16[256,256]{1,0:T(8,128)(2,1)S(1)} %add_convert_fusion.3), channel_id=1, source_target_pairs={{0,4},{2,6},{4,0},{6,2},{8,12},{10,14},{12,8},{14,10},{1,5},{3,7},... | collective-permute-start | bytes 393224 | tf_op jit(solution)/shard_map/ppermute | solution.py:284
  30.0 4.2 %collective-permute-done.5 = bf16[256,256]{1,0:T(8,128)(2,1)S(1)} collective-permute-done((bf16[256,256]{1,0:T(8,128)(2,1)S(1)}, bf16[256,256]{1,0:T(8,128)(2,1)S(1)}, u32[]{:S(2)}, u32[]{:S(2)}) %collective-permute-start.5) | collective-permute-done | bytes 131104 | tf_op jit(solution)/shard_map/ppermute | solution.py:284
  34.2 3.6 %collective-permute-start.7 = (bf16[256,256]{1,0:T(8,128)(2,1)S(1)}, bf16[256,256]{1,0:T(8,128)(2,1)S(1)}, u32[]{:S(2)}, u32[]{:S(2)}) collective-permute-start(bf16[256,256]{1,0:T(8,128)(2,1)S(1)} %add_convert_fusion.2), channel_id=1, source_target_pairs={{0,8},{2,10},{4,12},{6,14},{8,0},{10,2},{12,4},{14,6},{1,9},{3,11}... | collective-permute-start | bytes 393224 | tf_op jit(solution)/shard_map/ppermute | solution.py:284
  37.8 2.9 %collective-permute-done.7 = bf16[256,256]{1,0:T(8,128)(2,1)S(1)} collective-permute-done((bf16[256,256]{1,0:T(8,128)(2,1)S(1)}, bf16[256,256]{1,0:T(8,128)(2,1)S(1)}, u32[]{:S(2)}, u32[]{:S(2)}) %collective-permute-start.7) | collective-permute-done | bytes 131104 | tf_op jit(solution)/shard_map/ppermute | solution.py:284
  40.8 2.0 %collective-permute-start.9 = (bf16[256,256]{1,0:T(8,128)(2,1)S(1)}, bf16[256,256]{1,0:T(8,128)(2,1)S(1)}, u32[]{:S(2)}, u32[]{:S(2)}) collective-permute-start(bf16[256,256]{1,0:T(8,128)(2,1)S(1)} %add_convert_fusion.1.own), channel_id=1, source_target_pairs={{0,2},{2,0},{4,6},{6,4},{8,10},{10,8},{12,14},{14,12},{1,3},{3,1},... | collective-permute-start | bytes 393224 | tf_op jit(solution)/shard_map/ppermute | solution.py:284
  42.8 1.2 %collective-permute-done.10.edges = bf16[4,4,8,256]{3,2,1,0:T(8,128)(2,1)S(1)} collective-permute-done((bf16[4,4,8,256]{3,2,1,0:T(8,128)(2,1)S(1)}, bf16[4,4,8,256]{3,2,1,0:T(8,128)(2,1)S(1)}, u32[]{:S(2)}, u32[]{:S(2)}) %collective-permute-start.10) | collective-permute-done | bytes 65568 | tf_op jit(solution)/shard_map/ppermute | solution.py:280
  44.1 1.5 %shard_map.103 = (bf16[8,64,256]{2,1,0:T(8,128)(2,1)}, bf16[8,64,256]{2,1,0:T(8,128)(2,1)}) custom-call(bf16[8,64,256]{2,1,0:T(8,128)(2,1)S(1)} %copy-done, bf16[8,64,256]{2,1,0:T(8,128)(2,1)S(1)} %get-tuple-element.31.cot, s32[8,64]{1,0:T(8,128)S(1)} %get-tuple-element.32.domain, f32[1,256]{1,0:T(1,128)S(1)} %get-tuple-element.38.gain, ...), custom_call_target="tpu_custom_call" | custom-call | tf_op jit(solution)/shard_map/pallas_call | solution.py:255
  45.6 0.4 collective-permute-done.9.row_peer
  46.0 0.1 maximum_select_fusion
  46.1 1.5 %collective-permute-done.11.col_peer = bf16[512,256]{1,0:T(8,128)(2,1)S(1)} collective-permute-done((bf16[512,256]{1,0:T(8,128)(2,1)S(1)}, bf16[512,256]{1,0:T(8,128)(2,1)S(1)}, u32[]{:S(2)}, u32[]{:S(2)}) %collective-permute-start.11) | collective-permute-done | bytes 262176 | tf_op jit(solution)/shard_map/ppermute | solution.py:284
  47.7 1.2 %shard_map.104 = (f32[256,768]{1,0:T(8,128)}, f32[256,256]{1,0:T(8,128)}, f32[1,256]{1,0:T(1,128)}) custom-call(bf16[256,256]{1,0:T(8,128)(2,1)S(1)} %add_convert_fusion.1.own, bf16[256,256]{1,0:T(8,128)(2,1)S(1)} %collective-permute-done.9.row_peer, bf16[512,256]{1,0:T(8,128)(2,1)S(1)} %collective-permute-done.11.col_peer, ...), custom_call_target="tpu_custom_call" | custom-call | tf_op jit(solution)/shard_map/pallas_call | solution.py:255
  (16 shorter events, 0.3 us)
Async XLA Ops:
  0.6 13.6 %copy-start = (bf16[8,64,256]{2,1,0:T(8,128)(2,1)S(1)}, bf16[8,64,256]{2,1,0:T(8,128)(2,1)}, u32[]{:S(2)}) copy-start(bf16[8,64,256]{2,1,0:T(8,128)(2,1)} %feat.5) | copy-start | bytes 786436
  2.0 12.3 %collective-permute-start = (bf16[2,4,64,256]{3,2,1,0:T(8,128)(2,1)S(1)}, bf16[2,4,64,256]{3,2,1,0:T(8,128)(2,1)S(1)}, u32[]{:S(2)}, u32[]{:S(2)}) collective-permute-start(bf16[2,4,64,256]{3,2,1,0:T(8,128)(2,1)S(1)} %get-tuple-element.33), channel_id=1, source_target_pairs={{0,14},{2,0},{4,2},{6,4},{8,6},{10,8},{12,10},{14,12},{1,15},{3,1}... | collective-permute-start | bytes 786440 | tf_op jit(solution)/shard_map/ppermute | solution.py:275
  8.0 1.2 %collective-permute-start.1 = (bf16[2,4,8,256]{3,2,1,0:T(8,128)(2,1)S(1)}, bf16[2,4,8,256]{3,2,1,0:T(8,128)(2,1)S(1)}, u32[]{:S(2)}, u32[]{:S(2)}) collective-permute-start(bf16[2,4,8,256]{3,2,1,0:T(8,128)(2,1)S(1)} %get-tuple-element.34), channel_id=1, source_target_pairs={{0,1},{1,0},{2,3},{3,2},{4,5},{5,4},{6,7},{7,6},{8,9},{9,8},{10,11... | collective-permute-start | bytes 98312 | tf_op jit(solution)/shard_map/ppermute | solution.py:275
  8.0 6.3 %collective-permute-start.2 = (bf16[2,4,8,256]{3,2,1,0:T(8,128)(2,1)S(1)}, bf16[2,4,8,256]{3,2,1,0:T(8,128)(2,1)S(1)}, u32[]{:S(2)}, u32[]{:S(2)}) collective-permute-start(bf16[2,4,8,256]{3,2,1,0:T(8,128)(2,1)S(1)} %get-tuple-element.35), channel_id=1, source_target_pairs={{0,15},{1,14},{2,1},{3,0},{4,3},{5,2},{6,5},{7,4},{8,7},{9,6},{10,... | collective-permute-start | bytes 98312 | tf_op jit(solution)/shard_map/ppermute | solution.py:275
  17.7 1.6 %collective-permute-start.3 = (bf16[512,256]{1,0:T(8,128)(2,1)S(1)}, bf16[512,256]{1,0:T(8,128)(2,1)S(1)}, u32[]{:S(2)}, u32[]{:S(2)}) collective-permute-start(bf16[512,256]{1,0:T(8,128)(2,1)S(1)} %get-tuple-element.40), channel_id=1, source_target_pairs={{0,1},{1,0},{2,3},{3,2},{4,5},{5,4},{6,7},{7,6},{8,9},{9,8},{10,11... | collective-permute-start | bytes 786440 | tf_op jit(solution)/shard_map/ppermute | solution.py:284
  19.4 5.6 %collective-permute-start.4 = (bf16[256,256]{1,0:T(8,128)(2,1)S(1)}, bf16[256,256]{1,0:T(8,128)(2,1)S(1)}, u32[]{:S(2)}, u32[]{:S(2)}) collective-permute-start(bf16[256,256]{1,0:T(8,128)(2,1)S(1)} %constant_dynamic-slice_fusion), channel_id=1, source_target_pairs={{0,2},{2,0},{4,6},{6,4},{8,10},{10,8},{12,14},{14,12},{1,3},{3,1},... | collective-permute-start | bytes 393224 | tf_op jit(solution)/shard_map/ppermute | solution.py:284
  19.5 14.7 %collective-permute-start.6 = (bf16[4,64,256]{2,1,0:T(8,128)(2,1)S(1)}, bf16[4,64,256]{2,1,0:T(8,128)(2,1)S(1)}, u32[]{:S(2)}, u32[]{:S(2)}) collective-permute-start(bf16[4,64,256]{2,1,0:T(8,128)(2,1)S(1)} %get-tuple-element.41), channel_id=1, source_target_pairs={{0,2},{2,4},{4,6},{6,8},{8,10},{10,12},{12,14},{14,0},{1,3},{3,5},... | collective-permute-start | bytes 393224 | tf_op jit(solution)/shard_map/ppermute | solution.py:280
  21.5 19.3 %collective-permute-start.8 = (bf16[4,64,256]{2,1,0:T(8,128)(2,1)S(1)}, bf16[4,64,256]{2,1,0:T(8,128)(2,1)S(1)}, u32[]{:S(2)}, u32[]{:S(2)}) collective-permute-start(bf16[4,64,256]{2,1,0:T(8,128)(2,1)S(1)} %get-tuple-element.43), channel_id=1, source_target_pairs={{0,2},{2,4},{4,6},{6,8},{8,10},{10,12},{12,14},{14,0},{1,3},{3,5},... | collective-permute-start | bytes 393224 | tf_op jit(solution)/shard_map/ppermute | solution.py:280
  25.1 9.1 %collective-permute-start.5 = (bf16[256,256]{1,0:T(8,128)(2,1)S(1)}, bf16[256,256]{1,0:T(8,128)(2,1)S(1)}, u32[]{:S(2)}, u32[]{:S(2)}) collective-permute-start(bf16[256,256]{1,0:T(8,128)(2,1)S(1)} %add_convert_fusion.3), channel_id=1, source_target_pairs={{0,4},{2,6},{4,0},{6,2},{8,12},{10,14},{12,8},{14,10},{1,5},{3,7},... | collective-permute-start | bytes 393224 | tf_op jit(solution)/shard_map/ppermute | solution.py:284
  34.2 6.5 %collective-permute-start.7 = (bf16[256,256]{1,0:T(8,128)(2,1)S(1)}, bf16[256,256]{1,0:T(8,128)(2,1)S(1)}, u32[]{:S(2)}, u32[]{:S(2)}) collective-permute-start(bf16[256,256]{1,0:T(8,128)(2,1)S(1)} %add_convert_fusion.2), channel_id=1, source_target_pairs={{0,8},{2,10},{4,12},{6,14},{8,0},{10,2},{12,4},{14,6},{1,9},{3,11}... | collective-permute-start | bytes 393224 | tf_op jit(solution)/shard_map/ppermute | solution.py:284
  40.8 5.2 %collective-permute-start.9 = (bf16[256,256]{1,0:T(8,128)(2,1)S(1)}, bf16[256,256]{1,0:T(8,128)(2,1)S(1)}, u32[]{:S(2)}, u32[]{:S(2)}) collective-permute-start(bf16[256,256]{1,0:T(8,128)(2,1)S(1)} %add_convert_fusion.1.own), channel_id=1, source_target_pairs={{0,2},{2,0},{4,6},{6,4},{8,10},{10,8},{12,14},{14,12},{1,3},{3,1},... | collective-permute-start | bytes 393224 | tf_op jit(solution)/shard_map/ppermute | solution.py:284
  42.8 1.3 %collective-permute-start.10 = (bf16[4,4,8,256]{3,2,1,0:T(8,128)(2,1)S(1)}, bf16[4,4,8,256]{3,2,1,0:T(8,128)(2,1)S(1)}, u32[]{:S(2)}, u32[]{:S(2)}) collective-permute-start(bf16[4,4,8,256]{3,2,1,0:T(8,128)(2,1)S(1)} %pad_maximum_fusion), channel_id=1, source_target_pairs={{0,1},{1,0},{2,3},{3,2},{4,5},{5,4},{6,7},{7,6},{8,9},{9,8},{10,11... | collective-permute-start | bytes 196616 | tf_op jit(solution)/shard_map/ppermute | solution.py:280
  46.1 1.6 %collective-permute-start.11 = (bf16[512,256]{1,0:T(8,128)(2,1)S(1)}, bf16[512,256]{1,0:T(8,128)(2,1)S(1)}, u32[]{:S(2)}, u32[]{:S(2)}) collective-permute-start(bf16[512,256]{1,0:T(8,128)(2,1)S(1)} %maximum_select_fusion), channel_id=1, source_target_pairs={{0,1},{1,0},{2,3},{3,2},{4,5},{5,4},{6,7},{7,6},{8,9},{9,8},{10,11... | collective-permute-start | bytes 786440 | tf_op jit(solution)/shard_map/ppermute | solution.py:284

commit v4 on v3

--- a/solution.py
+++ b/solution.py
@@ -45,8 +45,8 @@
     copies = [
         pltpu.make_async_copy(source, target, sems.at[i])
         for i, (source, target) in enumerate((
+            (domain_hbm, domain),
             (cot, held),
-            (domain_hbm, domain),
             (feat.at[0:SHIFT], rows_out.at[0]),
             (feat.at[SHIFT:WIN, 0:WIN], right_out.at[0]),
             (feat.at[0:SHIFT, 0:WIN], corner_out.at[0]),
@@ -58,8 +58,8 @@
     for copy in copies:
         copy.start()
     copies[0].wait()
+    masks = domain_rows(domain, range(WIN), channels)
     copies[1].wait()
-    masks = domain_rows(domain, range(WIN), channels)
     for i in range(SHIFT):
         masked = held[i].astype(F32) * masks[i]
         rows_out[1, i] = masked.astype(BF16)
@@ -221,25 +221,21 @@
         grad_features[i] = (cot[i].astype(F32) + grad).astype(BF16)
 
 
-def sums_kernel(own, row_peer, col_peer, wqkv, gain, grad_qkv, grad_proj, grad_gain, blocks):
-    channels = own.shape[0]
-    mine_col = lax.axis_index("col")
-    mine_row = lax.axis_index("row") % 2
-    blocks[2 * mine_col + mine_row] = own[...].astype(F32)
-    blocks[2 * mine_col + 1 - mine_row] = row_peer[...].astype(F32)
-    other = 2 * (1 - mine_col)
-    blocks[other] = col_peer[0:channels, :].astype(F32)
-    blocks[other + 1] = col_peer[channels:, :].astype(F32)
+def sums_kernel(half, col_peer, wqkv, gain, grad_qkv, grad_proj, grad_gain, halves):
+    channels = wqkv.shape[0]
+    mine = lax.axis_index("col")
+    halves[mine] = half[...].astype(F32)
+    halves[1 - mine] = col_peer[...].astype(F32)
     total = jnp.zeros((8, channels), F32)
     ones = jnp.ones((8, channels), BF16)
     for b in range(3):
-        part = blocks[b]
+        part = halves[b // 2, channels * (b % 2) : channels * (b % 2 + 1), :]
         grad_qkv[:, channels * b : channels * (b + 1)] = part
         product = part * wqkv[:, channels * b : channels * (b + 1)].astype(F32)
         high = product.astype(BF16)
         low = (product - high.astype(F32)).astype(BF16)
         total = total + dot(ones, high, 1, 1) + dot(ones, low, 1, 1)
-    grad_proj[...] = blocks[3]
+    grad_proj[...] = halves[1, channels:, :]
     grad_gain[...] = total[0:1, :] / gain[...]
 
 
@@ -345,39 +341,42 @@
         ],
         features, cotangent, domain, below, right, corner, qkv_weight, proj_weight, gain,
     )
+    summed = add16(keep, swap(send, "col", 1))
+    place = lax.axis_index("row") % 4
+    chunk = channels // 2
+
+    def piece(step):
+        return lax.dynamic_slice_in_dim(summed, (place ^ step) * chunk, chunk, 0)
+
     att_rows = behind(att_send, "row")
     dn_rows = behind(dn_send, "row")
-
-    summed = add16(keep, swap(send, "col", 1))
-    mine_row = lax.axis_index("row") % 2
-    mine = lax.dynamic_slice_in_dim(summed, mine_row * channels, channels, 0)
-    other = lax.dynamic_slice_in_dim(summed, (1 - mine_row) * channels, channels, 0)
-    own = add16(mine, swap(other, "row", 1))
-    bit = 2
+    received = [swap(piece(step), "row", step) for step in (1, 2, 3)]
+    own = piece(0).astype(F32)
+    for part in received:
+        own = own + part.astype(F32)
+    own = own.astype(BF16)
+    bit = 4
     while bit < lax.axis_size("row"):
-        if bit == 4:
-            own, att_rows = lax.optimization_barrier((own, att_rows))
-        own = add16(own, swap(own, "row", bit))
+        received = swap(own, "row", bit)
+        own = add16(own, received)
         bit *= 2
-    own, dn_rows = lax.optimization_barrier((own, dn_rows))
+    own, att_rows, dn_rows = lax.optimization_barrier((own, att_rows, dn_rows))
     edges = jnp.stack(
         [part[:, cols - WIN :] for part in (att_rows, att_keep, dn_rows, dn_keep)], 0
     )
     edges = behind(edges, "col")
-    row_peer = swap(own, "row", 1)
-    pair = jnp.where(
-        mine_row == 0,
-        jnp.concatenate([own, row_peer], 0),
-        jnp.concatenate([row_peer, own], 0),
-    )
+    half = jnp.zeros((2 * channels, channels), BF16)
+    parts = [own] + [swap(own, "row", step) for step in (1, 2, 3)]
+    for step, part in enumerate(parts):
+        half = lax.dynamic_update_slice_in_dim(half, part, (place ^ step) * chunk, 0)
     updated, grad_features = run(
         finish_kernel,
         (shape(features.shape, BF16), shape(features.shape, BF16)),
         [pltpu.VMEM((WIN, cols + WIN, channels), F32)],
         features, cotangent, domain, gain, att_keep, att_rows, dn_keep, dn_rows, edges,
     )
-    pair, updated, grad_features = lax.optimization_barrier((pair, updated, grad_features))
-    col_peer = swap(pair, "col", 1)
+    half, updated, grad_features = lax.optimization_barrier((half, updated, grad_features))
+    col_peer = swap(half, "col", 1)
     grad_qkv, grad_proj, grad_gain = run(
         sums_kernel,
         (
@@ -385,10 +384,9 @@
             shape((channels, channels), F32),
             shape((1, channels), F32),
         ),
-        [pltpu.VMEM((4, channels, channels), F32)],
-        own, row_peer, col_peer, qkv_weight, gain,
-    )
-
+        [pltpu.VMEM((2, 2 * channels, channels), F32)],
+        half, col_peer, qkv_weight, gain,
+    )
     return updated, grad_features, grad_qkv, grad_proj, grad_gain.reshape(channels)
 
 

time: 49.4 us -> 46.9 us (0.949)
  starting transfers between devices: 20.4 us -> 18.8 us
  waiting for transfers between devices: 19.9 us -> 19.4 us
    ppermute x6 -> x9, waiting for transfers between devices: 13 us -> 8.41 us  [swap(): lax.ppermute(array, axis, [(i, i ^ bit) for i in range(lax.axis_size(axis...]
    ppermute x3, waiting for transfers between devices: 1.24 us -> 5.4 us  [behind(): lax.ppermute(array, axis, [(i, (i + 1) % peers) for i in range(peers)])]
    ppermute x3, starting transfers between devices: 3.07 us -> 1.54 us  [behind(): lax.ppermute(array, axis, [(i, (i + 1) % peers) for i in range(peers)])]
    ppermute x6 -> x9, starting transfers between devices: 10.7 us -> 10.5 us  [swap(): lax.ppermute(array, axis, [(i, i ^ bit) for i in range(lax.axis_size(axis...]
  transfers between devices with their start and end apart: 12 -> 15, of which waited for: 9 -> 12; matrix products, arithmetic and copies ran while one was open for 0% -> 0% of each run, Pallas kernels for 3% -> 3%
where the time goes in v4:
time: 46.9 us; the launch traced here: 46.8 us
  waiting for transfers between devices  19.4 us (41%)
  starting transfers between devices  18.8 us (40%)
  Pallas kernels  7.52 us (16%)
  between operations  0.81 us (2%)
    ppermute x9, starting transfers between devices, swap(): lax.ppermute(array, axis, [(i, i ^ bit) for i in range(lax.axis_size(axis...  10.5 us
    ppermute x9, waiting for transfers between devices, swap(): lax.ppermute(array, axis, [(i, i ^ bit) for i in range(lax.axis_size(axis...  8.41 us
    pallas_call x4, Pallas kernels, run(): pl.pallas_call(kernel, out_shape=out_shapes, in_specs=[HBM if i in unstag...  7.52 us
    ppermute x3, starting transfers between devices, ahead(): return lax.ppermute(array, axes if len(axes) > 1 else axes[0], pairs)  6.68 us
    ppermute x3, waiting for transfers between devices, ahead(): return lax.ppermute(array, axes if len(axes) > 1 else axes[0], pairs)  5.62 us
    ppermute x3, waiting for transfers between devices, behind(): lax.ppermute(array, axis, [(i, (i + 1) % peers) for i in range(peers)])  5.4 us
    ppermute x3, starting transfers between devices, behind(): lax.ppermute(array, axis, [(i, (i + 1) % peers) for i in range(peers)])  1.54 us
  transfers between devices with their start and end apart: 15, of which 12 were waited for; matrix products, arithmetic and copies ran while one was open for 0% of the time, Pallas kernels for 3%

profile of v4, /device:TPU:0, one launch (start us, length us, event | category | flops | bytes accessed | tf_op | source)
XLA Modules:
  0.0 46.8 jit_solution(15656176758421466853)
XLA Ops:
  0.6 1.3 %shard_map.101 = (bf16[2,4,64,256]{3,2,1,0:T(8,128)(2,1)S(1)}, bf16[2,4,8,256]{3,2,1,0:T(8,128)(2,1)S(1)}, bf16[2,4,8,256]{3,2,1,0:T(8,128)(2,1)S(1)}, bf16[8,64...) custom-call(bf16[8,64,256]{2,1,0:T(8,128)(2,1)} %feat.5, ...), custom_call_target="tpu_custom_call" | custom-call | tf_op jit(solution)/shard_map/pallas_call | solution.py:251
  2.0 6.0 %collective-permute-start = (bf16[2,4,64,256]{3,2,1,0:T(8,128)(2,1)S(1)}, bf16[2,4,64,256]{3,2,1,0:T(8,128)(2,1)S(1)}, u32[]{:S(2)}, u32[]{:S(2)}) collective-permute-start(bf16[2,4,64,256]{3,2,1,0:T(8,128)(2,1)S(1)} %get-tuple-element.32), channel_id=1, source_target_pairs={{0,14},{2,0},{4,2},{6,4},{8,6},{10,8},{12,10},{14,12},{1,15},{3,1}... | collective-permute-start | bytes 786440 | tf_op jit(solution)/shard_map/ppermute | solution.py:271
  8.0 0.6 %collective-permute-start.2 = (bf16[2,4,8,256]{3,2,1,0:T(8,128)(2,1)S(1)}, bf16[2,4,8,256]{3,2,1,0:T(8,128)(2,1)S(1)}, u32[]{:S(2)}, u32[]{:S(2)}) collective-permute-start(bf16[2,4,8,256]{3,2,1,0:T(8,128)(2,1)S(1)} %get-tuple-element.34), channel_id=1, source_target_pairs={{0,15},{1,14},{2,1},{3,0},{4,3},{5,2},{6,5},{7,4},{8,7},{9,6},{10,... | collective-permute-start | bytes 98312 | tf_op jit(solution)/shard_map/ppermute | solution.py:271
  8.7 0.6 %collective-permute-done.1.right = bf16[2,4,8,256]{3,2,1,0:T(8,128)(2,1)S(1)} collective-permute-done((bf16[2,4,8,256]{3,2,1,0:T(8,128)(2,1)S(1)}, bf16[2,4,8,256]{3,2,1,0:T(8,128)(2,1)S(1)}, u32[]{:S(2)}, u32[]{:S(2)}) %collective-permute-start.1) | collective-permute-done | bytes 32800 | tf_op jit(solution)/shard_map/ppermute | solution.py:271
  9.2 5.1 %collective-permute-done.2.corner = bf16[2,4,8,256]{3,2,1,0:T(8,128)(2,1)S(1)} collective-permute-done((bf16[2,4,8,256]{3,2,1,0:T(8,128)(2,1)S(1)}, bf16[2,4,8,256]{3,2,1,0:T(8,128)(2,1)S(1)}, u32[]{:S(2)}, u32[]{:S(2)}) %collective-permute-start.2) | collective-permute-done | bytes 32800 | tf_op jit(solution)/shard_map/ppermute | solution.py:271
  14.3 3.4 %shard_map.102 = (bf16[512,256]{1,0:T(8,128)(2,1)S(1)}, bf16[512,256]{1,0:T(8,128)(2,1)S(1)}, bf16[4,64,256]{2,1,0:T(8,128)(2,1)S(1)}, bf16[4,64,256]{2,1,0:T(8,...) custom-call(bf16[8,64,256]{2,1,0:T(8,128)(2,1)S(1)} %copy-done, ...), custom_call_target="tpu_custom_call" | custom-call | tf_op jit(solution)/shard_map/pallas_call | solution.py:251
  17.8 1.5 %collective-permute-done.3 = bf16[512,256]{1,0:T(8,128)(2,1)S(1)} collective-permute-done((bf16[512,256]{1,0:T(8,128)(2,1)S(1)}, bf16[512,256]{1,0:T(8,128)(2,1)S(1)}, u32[]{:S(2)}, u32[]{:S(2)}) %collective-permute-start.3) | collective-permute-done | bytes 262176 | tf_op jit(solution)/shard_map/ppermute | solution.py:280
  19.5 1.1 %collective-permute-start.6 = (bf16[128,256]{1,0:T(8,128)(2,1)S(1)}, bf16[128,256]{1,0:T(8,128)(2,1)S(1)}, u32[]{:S(2)}, u32[]{:S(2)}) collective-permute-start(bf16[128,256]{1,0:T(8,128)(2,1)S(1)} %get-tuple-element.56), channel_id=1, source_target_pairs={{0,6},{2,4},{4,2},{6,0},{8,14},{10,12},{12,10},{14,8},{1,7},{3,5},... | collective-permute-start | bytes 196616 | tf_op jit(solution)/shard_map/ppermute | solution.py:280
  20.6 2.4 %collective-permute-start.5 = (bf16[128,256]{1,0:T(8,128)(2,1)S(1)}, bf16[128,256]{1,0:T(8,128)(2,1)S(1)}, u32[]{:S(2)}, u32[]{:S(2)}) collective-permute-start(bf16[128,256]{1,0:T(8,128)(2,1)S(1)} %get-tuple-element.57), channel_id=1, source_target_pairs={{0,4},{2,6},{4,0},{6,2},{8,12},{10,14},{12,8},{14,10},{1,5},{3,7},... | collective-permute-start | bytes 196616 | tf_op jit(solution)/shard_map/ppermute | solution.py:280
  23.0 1.4 %collective-permute-start.9 = (bf16[4,64,256]{2,1,0:T(8,128)(2,1)S(1)}, bf16[4,64,256]{2,1,0:T(8,128)(2,1)S(1)}, u32[]{:S(2)}, u32[]{:S(2)}) collective-permute-start(bf16[4,64,256]{2,1,0:T(8,128)(2,1)S(1)} %get-tuple-element.41), channel_id=1, source_target_pairs={{0,2},{2,4},{4,6},{6,8},{8,10},{10,12},{12,14},{14,0},{1,3},{3,5},... | collective-permute-start | bytes 393224 | tf_op jit(solution)/shard_map/ppermute | solution.py:276
  24.4 0.6 %collective-permute-done.4 = bf16[128,256]{1,0:T(8,128)(2,1)S(1)} collective-permute-done((bf16[128,256]{1,0:T(8,128)(2,1)S(1)}, bf16[128,256]{1,0:T(8,128)(2,1)S(1)}, u32[]{:S(2)}, u32[]{:S(2)}) %collective-permute-start.4) | collective-permute-done | bytes 65568 | tf_op jit(solution)/shard_map/ppermute | solution.py:280
  25.0 0.3 collective-permute-done.6
  25.3 0.9 %collective-permute-done.5 = bf16[128,256]{1,0:T(8,128)(2,1)S(1)} collective-permute-done((bf16[128,256]{1,0:T(8,128)(2,1)S(1)}, bf16[128,256]{1,0:T(8,128)(2,1)S(1)}, u32[]{:S(2)}, u32[]{:S(2)}) %collective-permute-start.5) | collective-permute-done | bytes 65568 | tf_op jit(solution)/shard_map/ppermute | solution.py:280
  26.2 3.1 %collective-permute-start.7 = (bf16[128,256]{1,0:T(8,128)(2,1)S(1)}, bf16[128,256]{1,0:T(8,128)(2,1)S(1)}, u32[]{:S(2)}, u32[]{:S(2)}) collective-permute-start(bf16[128,256]{1,0:T(8,128)(2,1)S(1)} %add_convert_fusion.2), channel_id=1, source_target_pairs={{0,8},{2,10},{4,12},{6,14},{8,0},{10,2},{12,4},{14,6},{1,9},{3,11}... | collective-permute-start | bytes 196616 | tf_op jit(solution)/shard_map/ppermute | solution.py:280
  29.3 2.2 %collective-permute-done.7 = bf16[128,256]{1,0:T(8,128)(2,1)S(1)} collective-permute-done((bf16[128,256]{1,0:T(8,128)(2,1)S(1)}, bf16[128,256]{1,0:T(8,128)(2,1)S(1)}, u32[]{:S(2)}, u32[]{:S(2)}) %collective-permute-start.7) | collective-permute-done | bytes 65568 | tf_op jit(solution)/shard_map/ppermute | solution.py:280
  31.6 2.1 %collective-permute-done.8.att_rows = bf16[4,64,256]{2,1,0:T(8,128)(2,1)S(1)} collective-permute-done((bf16[4,64,256]{2,1,0:T(8,128)(2,1)S(1)}, bf16[4,64,256]{2,1,0:T(8,128)(2,1)S(1)}, u32[]{:S(2)}, u32[]{:S(2)}) %collective-permute-start.8) | collective-permute-done | bytes 131104 | tf_op jit(solution)/shard_map/ppermute | solution.py:276
  33.7 2.1 %collective-permute-done.9.dn_rows = bf16[4,64,256]{2,1,0:T(8,128)(2,1)S(1)} collective-permute-done((bf16[4,64,256]{2,1,0:T(8,128)(2,1)S(1)}, bf16[4,64,256]{2,1,0:T(8,128)(2,1)S(1)}, u32[]{:S(2)}, u32[]{:S(2)}) %collective-permute-start.9) | collective-permute-done | bytes 131104 | tf_op jit(solution)/shard_map/ppermute | solution.py:276
  35.8 1.4 %collective-permute-start.12 = (bf16[128,256]{1,0:T(8,128)(2,1)S(1)}, bf16[128,256]{1,0:T(8,128)(2,1)S(1)}, u32[]{:S(2)}, u32[]{:S(2)}) collective-permute-start(bf16[128,256]{1,0:T(8,128)(2,1)S(1)} %add_convert_fusion.1), channel_id=1, source_target_pairs={{0,6},{2,4},{4,2},{6,0},{8,14},{10,12},{12,10},{14,8},{1,7},{3,5},... | collective-permute-start | bytes 196616 | tf_op jit(solution)/shard_map/ppermute | solution.py:280
  37.2 2.4 %collective-permute-start.11 = (bf16[128,256]{1,0:T(8,128)(2,1)S(1)}, bf16[128,256]{1,0:T(8,128)(2,1)S(1)}, u32[]{:S(2)}, u32[]{:S(2)}) collective-permute-start(bf16[128,256]{1,0:T(8,128)(2,1)S(1)} %add_convert_fusion.1), channel_id=1, source_target_pairs={{0,4},{2,6},{4,0},{6,2},{8,12},{10,14},{12,8},{14,10},{1,5},{3,7},... | collective-permute-start | bytes 196616 | tf_op jit(solution)/shard_map/ppermute | solution.py:280
  39.7 1.2 %collective-permute-done.13.edges = bf16[4,4,8,256]{3,2,1,0:T(8,128)(2,1)S(1)} collective-permute-done((bf16[4,4,8,256]{3,2,1,0:T(8,128)(2,1)S(1)}, bf16[4,4,8,256]{3,2,1,0:T(8,128)(2,1)S(1)}, u32[]{:S(2)}, u32[]{:S(2)}) %collective-permute-start.13) | collective-permute-done | bytes 65568 | tf_op jit(solution)/shard_map/ppermute | solution.py:276
  40.9 1.5 %shard_map.103 = (bf16[8,64,256]{2,1,0:T(8,128)(2,1)}, bf16[8,64,256]{2,1,0:T(8,128)(2,1)}) custom-call(bf16[8,64,256]{2,1,0:T(8,128)(2,1)S(1)} %copy-done, bf16[8,64,256]{2,1,0:T(8,128)(2,1)S(1)} %get-tuple-element.30.cot, s32[8,64]{1,0:T(8,128)S(1)} %get-tuple-element.31.domain, f32[1,256]{1,0:T(1,128)S(1)} %get-tuple-element.37.gain, ...), custom_call_target="tpu_custom_call" | custom-call | tf_op jit(solution)/shard_map/pallas_call | solution.py:251
  42.5 1.4 %collective-permute-done.10 = bf16[128,256]{1,0:T(8,128)(2,1)S(1)} collective-permute-done((bf16[128,256]{1,0:T(8,128)(2,1)S(1)}, bf16[128,256]{1,0:T(8,128)(2,1)S(1)}, u32[]{:S(2)}, u32[]{:S(2)}) %collective-permute-start.10) | collective-permute-done | bytes 65568 | tf_op jit(solution)/shard_map/ppermute | solution.py:280
  44.0 1.5 %collective-permute-done.14.col_peer = bf16[512,256]{1,0:T(8,128)(2,1)S(1)} collective-permute-done((bf16[512,256]{1,0:T(8,128)(2,1)S(1)}, bf16[512,256]{1,0:T(8,128)(2,1)S(1)}, u32[]{:S(2)}, u32[]{:S(2)}) %collective-permute-start.14) | collective-permute-done | bytes 262176 | tf_op jit(solution)/shard_map/ppermute | solution.py:280
  45.5 1.3 %shard_map.104 = (f32[256,768]{1,0:T(8,128)}, f32[256,256]{1,0:T(8,128)}, f32[1,256]{1,0:T(1,128)}) custom-call(bf16[512,256]{1,0:T(8,128)(2,1)S(1)} %constant_dynamic-update-slice_fusion.half, bf16[512,256]{1,0:T(8,128)(2,1)S(1)} %collective-permute-done.14.col_peer, bf16[256,768]{1,0:T(8,128)(2,1)S(1)} %get-tuple-element.35.wqkv, ...), custom_call_target="tpu_custom_call" | custom-call | tf_op jit(solution)/shard_map/pallas_call | solution.py:251
  (24 shorter events, 0.6 us)
Async XLA Ops:
  0.6 13.6 %copy-start = (bf16[8,64,256]{2,1,0:T(8,128)(2,1)S(1)}, bf16[8,64,256]{2,1,0:T(8,128)(2,1)}, u32[]{:S(2)}) copy-start(bf16[8,64,256]{2,1,0:T(8,128)(2,1)} %feat.5) | copy-start | bytes 786436
  2.0 12.3 %collective-permute-start = (bf16[2,4,64,256]{3,2,1,0:T(8,128)(2,1)S(1)}, bf16[2,4,64,256]{3,2,1,0:T(8,128)(2,1)S(1)}, u32[]{:S(2)}, u32[]{:S(2)}) collective-permute-start(bf16[2,4,64,256]{3,2,1,0:T(8,128)(2,1)S(1)} %get-tuple-element.32), channel_id=1, source_target_pairs={{0,14},{2,0},{4,2},{6,4},{8,6},{10,8},{12,10},{14,12},{1,15},{3,1}... | collective-permute-start | bytes 786440 | tf_op jit(solution)/shard_map/ppermute | solution.py:271
  8.0 1.2 %collective-permute-start.1 = (bf16[2,4,8,256]{3,2,1,0:T(8,128)(2,1)S(1)}, bf16[2,4,8,256]{3,2,1,0:T(8,128)(2,1)S(1)}, u32[]{:S(2)}, u32[]{:S(2)}) collective-permute-start(bf16[2,4,8,256]{3,2,1,0:T(8,128)(2,1)S(1)} %get-tuple-element.33), channel_id=1, source_target_pairs={{0,1},{1,0},{2,3},{3,2},{4,5},{5,4},{6,7},{7,6},{8,9},{9,8},{10,11... | collective-permute-start | bytes 98312 | tf_op jit(solution)/shard_map/ppermute | solution.py:271
  8.0 6.3 %collective-permute-start.2 = (bf16[2,4,8,256]{3,2,1,0:T(8,128)(2,1)S(1)}, bf16[2,4,8,256]{3,2,1,0:T(8,128)(2,1)S(1)}, u32[]{:S(2)}, u32[]{:S(2)}) collective-permute-start(bf16[2,4,8,256]{3,2,1,0:T(8,128)(2,1)S(1)} %get-tuple-element.34), channel_id=1, source_target_pairs={{0,15},{1,14},{2,1},{3,0},{4,3},{5,2},{6,5},{7,4},{8,7},{9,6},{10,... | collective-permute-start | bytes 98312 | tf_op jit(solution)/shard_map/ppermute | solution.py:271
  17.7 1.6 %collective-permute-start.3 = (bf16[512,256]{1,0:T(8,128)(2,1)S(1)}, bf16[512,256]{1,0:T(8,128)(2,1)S(1)}, u32[]{:S(2)}, u32[]{:S(2)}) collective-permute-start(bf16[512,256]{1,0:T(8,128)(2,1)S(1)} %get-tuple-element.39), channel_id=1, source_target_pairs={{0,1},{1,0},{2,3},{3,2},{4,5},{5,4},{6,7},{7,6},{8,9},{9,8},{10,11... | collective-permute-start | bytes 786440 | tf_op jit(solution)/shard_map/ppermute | solution.py:280
  19.4 5.6 %collective-permute-start.4 = (bf16[128,256]{1,0:T(8,128)(2,1)S(1)}, bf16[128,256]{1,0:T(8,128)(2,1)S(1)}, u32[]{:S(2)}, u32[]{:S(2)}) collective-permute-start(bf16[128,256]{1,0:T(8,128)(2,1)S(1)} %get-tuple-element.55), channel_id=1, source_target_pairs={{0,2},{2,0},{4,6},{6,4},{8,10},{10,8},{12,14},{14,12},{1,3},{3,1},... | collective-permute-start | bytes 196616 | tf_op jit(solution)/shard_map/ppermute | solution.py:280
  19.5 5.8 %collective-permute-start.6 = (bf16[128,256]{1,0:T(8,128)(2,1)S(1)}, bf16[128,256]{1,0:T(8,128)(2,1)S(1)}, u32[]{:S(2)}, u32[]{:S(2)}) collective-permute-start(bf16[128,256]{1,0:T(8,128)(2,1)S(1)} %get-tuple-element.56), channel_id=1, source_target_pairs={{0,6},{2,4},{4,2},{6,0},{8,14},{10,12},{12,10},{14,8},{1,7},{3,5},... | collective-permute-start | bytes 196616 | tf_op jit(solution)/shard_map/ppermute | solution.py:280
  20.6 5.6 %collective-permute-start.5 = (bf16[128,256]{1,0:T(8,128)(2,1)S(1)}, bf16[128,256]{1,0:T(8,128)(2,1)S(1)}, u32[]{:S(2)}, u32[]{:S(2)}) collective-permute-start(bf16[128,256]{1,0:T(8,128)(2,1)S(1)} %get-tuple-element.57), channel_id=1, source_target_pairs={{0,4},{2,6},{4,0},{6,2},{8,12},{10,14},{12,8},{14,10},{1,5},{3,7},... | collective-permute-start | bytes 196616 | tf_op jit(solution)/shard_map/ppermute | solution.py:280
  23.0 10.7 %collective-permute-start.8 = (bf16[4,64,256]{2,1,0:T(8,128)(2,1)S(1)}, bf16[4,64,256]{2,1,0:T(8,128)(2,1)S(1)}, u32[]{:S(2)}, u32[]{:S(2)}) collective-permute-start(bf16[4,64,256]{2,1,0:T(8,128)(2,1)S(1)} %get-tuple-element.40), channel_id=1, source_target_pairs={{0,2},{2,4},{4,6},{6,8},{8,10},{10,12},{12,14},{14,0},{1,3},{3,5},... | collective-permute-start | bytes 393224 | tf_op jit(solution)/shard_map/ppermute | solution.py:276
  23.0 12.8 %collective-permute-start.9 = (bf16[4,64,256]{2,1,0:T(8,128)(2,1)S(1)}, bf16[4,64,256]{2,1,0:T(8,128)(2,1)S(1)}, u32[]{:S(2)}, u32[]{:S(2)}) collective-permute-start(bf16[4,64,256]{2,1,0:T(8,128)(2,1)S(1)} %get-tuple-element.41), channel_id=1, source_target_pairs={{0,2},{2,4},{4,6},{6,8},{8,10},{10,12},{12,14},{14,0},{1,3},{3,5},... | collective-permute-start | bytes 393224 | tf_op jit(solution)/shard_map/ppermute | solution.py:276
  26.2 5.3 %collective-permute-start.7 = (bf16[128,256]{1,0:T(8,128)(2,1)S(1)}, bf16[128,256]{1,0:T(8,128)(2,1)S(1)}, u32[]{:S(2)}, u32[]{:S(2)}) collective-permute-start(bf16[128,256]{1,0:T(8,128)(2,1)S(1)} %add_convert_fusion.2), channel_id=1, source_target_pairs={{0,8},{2,10},{4,12},{6,14},{8,0},{10,2},{12,4},{14,6},{1,9},{3,11}... | collective-permute-start | bytes 196616 | tf_op jit(solution)/shard_map/ppermute | solution.py:280
  35.8 8.1 %collective-permute-start.12 = (bf16[128,256]{1,0:T(8,128)(2,1)S(1)}, bf16[128,256]{1,0:T(8,128)(2,1)S(1)}, u32[]{:S(2)}, u32[]{:S(2)}) collective-permute-start(bf16[128,256]{1,0:T(8,128)(2,1)S(1)} %add_convert_fusion.1), channel_id=1, source_target_pairs={{0,6},{2,4},{4,2},{6,0},{8,14},{10,12},{12,10},{14,8},{1,7},{3,5},... | collective-permute-start | bytes 196616 | tf_op jit(solution)/shard_map/ppermute | solution.py:280
  37.2 6.7 %collective-permute-start.11 = (bf16[128,256]{1,0:T(8,128)(2,1)S(1)}, bf16[128,256]{1,0:T(8,128)(2,1)S(1)}, u32[]{:S(2)}, u32[]{:S(2)}) collective-permute-start(bf16[128,256]{1,0:T(8,128)(2,1)S(1)} %add_convert_fusion.1), channel_id=1, source_target_pairs={{0,4},{2,6},{4,0},{6,2},{8,12},{10,14},{12,8},{14,10},{1,5},{3,7},... | collective-permute-start | bytes 196616 | tf_op jit(solution)/shard_map/ppermute | solution.py:280
  39.6 4.3 %collective-permute-start.10 = (bf16[128,256]{1,0:T(8,128)(2,1)S(1)}, bf16[128,256]{1,0:T(8,128)(2,1)S(1)}, u32[]{:S(2)}, u32[]{:S(2)}) collective-permute-start(bf16[128,256]{1,0:T(8,128)(2,1)S(1)} %add_convert_fusion.1), channel_id=1, source_target_pairs={{0,2},{2,0},{4,6},{6,4},{8,10},{10,8},{12,14},{14,12},{1,3},{3,1},... | collective-permute-start | bytes 196616 | tf_op jit(solution)/shard_map/ppermute | solution.py:280
  39.6 1.3 %collective-permute-start.13 = (bf16[4,4,8,256]{3,2,1,0:T(8,128)(2,1)S(1)}, bf16[4,4,8,256]{3,2,1,0:T(8,128)(2,1)S(1)}, u32[]{:S(2)}, u32[]{:S(2)}) collective-permute-start(bf16[4,4,8,256]{3,2,1,0:T(8,128)(2,1)S(1)} %pad_maximum_fusion), channel_id=1, source_target_pairs={{0,1},{1,0},{2,3},{3,2},{4,5},{5,4},{6,7},{7,6},{8,9},{9,8},{10,11... | collective-permute-start | bytes 196616 | tf_op jit(solution)/shard_map/ppermute | solution.py:276
  43.9 1.6 %collective-permute-start.14 = (bf16[512,256]{1,0:T(8,128)(2,1)S(1)}, bf16[512,256]{1,0:T(8,128)(2,1)S(1)}, u32[]{:S(2)}, u32[]{:S(2)}) collective-permute-start(bf16[512,256]{1,0:T(8,128)(2,1)S(1)} %constant_dynamic-update-slice_fusion.half), channel_id=1, source_target_pairs={{0,1},{1,0},{2,3},{3,2},{4,5},{5,4},{6,7},{7,6},{8,9},{9,8},{10,11... | collective-permute-start | bytes 786440 | tf_op jit(solution)/shard_map/ppermute | solution.py:280

commit v5 on v4

--- a/solution.py
+++ b/solution.py
@@ -72,7 +72,7 @@
 
 def block_kernel(
     feat, cot, domain, below, right, corner, wqkv, wproj, gain,
-    keep, send, att_keep, att_send, dn_keep, dn_send,
+    keep, send, att_keep, dn_keep, both_send,
     buf, shifted, projected, dattended, dcontext, context, dprojected, grads,
     query_held, dctx_held, scores_held, dchances_held, chances_held, dscore_held,
 ):
@@ -181,16 +181,16 @@
     for w in range(windows):
         tile = full[cells * w : cells * (w + 1)].reshape(WIN, WIN, channels).astype(BF16)
         att_keep[:, WIN * w : WIN * (w + 1), :] = tile[0:SHIFT]
-        att_send[:, WIN * w : WIN * (w + 1), :] = tile[SHIFT:WIN]
+        both_send[0, :, WIN * w : WIN * (w + 1), :] = tile[SHIFT:WIN]
     full = dot(dprojected[...], wqkv[...], 1, 1)
     for w in range(windows):
         tile = full[cells * w : cells * (w + 1)].reshape(WIN, WIN, channels).astype(BF16)
         dn_keep[:, WIN * w : WIN * (w + 1), :] = tile[0:SHIFT]
-        dn_send[:, WIN * w : WIN * (w + 1), :] = tile[SHIFT:WIN]
+        both_send[1, :, WIN * w : WIN * (w + 1), :] = tile[SHIFT:WIN]
 
 
 def finish_kernel(
-    feat, cot, domain, gain, att_keep, att_rows, dn_keep, dn_rows, edges,
+    feat, cot, domain, gain, att_keep, dn_keep, both_rows, edges,
     updated, grad_features,
     buf,
 ):
@@ -203,11 +203,11 @@
         buf[0:SHIFT, WIN : WIN + cols, :] = came[...].astype(F32)
         buf[SHIFT:WIN, WIN : WIN + cols, :] = stayed[...].astype(F32)
 
-    unshifted(0, att_keep, att_rows)
+    unshifted(0, att_keep, both_rows.at[0])
     for i in range(WIN):
         back = buf[i, SHIFT : SHIFT + cols, :]
         updated[i] = (feat[i].astype(F32) + masks[i] * back).astype(BF16)
-    unshifted(1, dn_keep, dn_rows)
+    unshifted(1, dn_keep, both_rows.at[1])
     for i in range(WIN):
         upstream = buf[i, SHIFT : SHIFT + cols, :] * gain[...]
         x = feat[i].astype(F32)
@@ -313,15 +313,14 @@
     corner = ahead(corner_out, ("row", "col"))
 
     strip = shape((SHIFT, cols, channels), BF16)
-    keep, send, att_keep, att_send, dn_keep, dn_send = run(
+    keep, send, att_keep, dn_keep, both_send = run(
         block_kernel,
         (
             shape((2 * channels, channels), BF16),
             shape((2 * channels, channels), BF16),
             strip,
             strip,
-            strip,
-            strip,
+            shape((2, SHIFT, cols, channels), BF16),
         ),
         [
             pltpu.VMEM((WIN, cols + WIN, channels), F32),
@@ -348,21 +347,20 @@
     def piece(step):
         return lax.dynamic_slice_in_dim(summed, (place ^ step) * chunk, chunk, 0)
 
-    att_rows = behind(att_send, "row")
-    dn_rows = behind(dn_send, "row")
+    both_rows = behind(both_send, "row")
     received = [swap(piece(step), "row", step) for step in (1, 2, 3)]
     own = piece(0).astype(F32)
     for part in received:
         own = own + part.astype(F32)
     own = own.astype(BF16)
+    own, both_rows = lax.optimization_barrier((own, both_rows))
     bit = 4
     while bit < lax.axis_size("row"):
         received = swap(own, "row", bit)
         own = add16(own, received)
         bit *= 2
-    own, att_rows, dn_rows = lax.optimization_barrier((own, att_rows, dn_rows))
     edges = jnp.stack(
-        [part[:, cols - WIN :] for part in (att_rows, att_keep, dn_rows, dn_keep)], 0
+        [part[:, cols - WIN :] for part in (both_rows[0], att_keep, both_rows[1], dn_keep)], 0
     )
     edges = behind(edges, "col")
     half = jnp.zeros((2 * channels, channels), BF16)
@@ -373,7 +371,7 @@
         finish_kernel,
         (shape(features.shape, BF16), shape(features.shape, BF16)),
         [pltpu.VMEM((WIN, cols + WIN, channels), F32)],
-        features, cotangent, domain, gain, att_keep, att_rows, dn_keep, dn_rows, edges,
+        features, cotangent, domain, gain, att_keep, dn_keep, both_rows, edges,
     )
     half, updated, grad_features = lax.optimization_barrier((half, updated, grad_features))
     col_peer = swap(half, "col", 1)

time: 46.9 us -> 46.3 us (0.987)
  starting transfers between devices: 18.8 us -> 15 us
  waiting for transfers between devices: 19.4 us -> 22.6 us
    ppermute x9, waiting for transfers between devices: 8.41 us -> 17 us  [swap(): lax.ppermute(array, axis, [(i, i ^ bit) for i in range(lax.axis_size(axis...]
    ppermute x3 -> x2, waiting for transfers between devices: 5.4 us -> 0.01 us  [behind(): lax.ppermute(array, axis, [(i, (i + 1) % peers) for i in range(peers)])]
    ppermute x9, starting transfers between devices: 10.5 us -> 8.14 us  [swap(): lax.ppermute(array, axis, [(i, i ^ bit) for i in range(lax.axis_size(axis...]
    ppermute x3 -> x2, starting transfers between devices: 1.54 us -> 0.19 us  [behind(): lax.ppermute(array, axis, [(i, (i + 1) % peers) for i in range(peers)])]
  transfers between devices with their start and end apart: 15 -> 14, of which waited for: 12 -> 9; matrix products, arithmetic and copies ran while one was open for 0% -> 1% of each run, Pallas kernels for 3% -> 3%
where the time goes in v5:
time: 46.3 us; the launch traced here: 46.2 us
  waiting for transfers between devices  22.6 us (49%)
  starting transfers between devices  15 us (32%)
  Pallas kernels  7.52 us (16%)
  between operations  0.8 us (2%)
    ppermute x9, waiting for transfers between devices, swap(): lax.ppermute(array, axis, [(i, i ^ bit) for i in range(lax.axis_size(axis...  17 us
    ppermute x9, starting transfers between devices, swap(): lax.ppermute(array, axis, [(i, i ^ bit) for i in range(lax.axis_size(axis...  8.14 us
    pallas_call x4, Pallas kernels, run(): pl.pallas_call(kernel, out_shape=out_shapes, in_specs=[HBM if i in unstag...  7.52 us
    ppermute x3, starting transfers between devices, ahead(): return lax.ppermute(array, axes if len(axes) > 1 else axes[0], pairs)  6.68 us
    ppermute x3, waiting for transfers between devices, ahead(): return lax.ppermute(array, axes if len(axes) > 1 else axes[0], pairs)  5.62 us
  transfers between devices with their start and end apart: 14, of which 9 were waited for; matrix products, arithmetic and copies ran while one was open for 1% of the time, Pallas kernels for 3%

profile of v5, /device:TPU:0, one launch (start us, length us, event | category | flops | bytes accessed | tf_op | source)
XLA Modules:
  0.0 46.2 jit_solution(15526468500921916175)
XLA Ops:
  0.6 1.3 %shard_map.101 = (bf16[2,4,64,256]{3,2,1,0:T(8,128)(2,1)S(1)}, bf16[2,4,8,256]{3,2,1,0:T(8,128)(2,1)S(1)}, bf16[2,4,8,256]{3,2,1,0:T(8,128)(2,1)S(1)}, bf16[8,64...) custom-call(bf16[8,64,256]{2,1,0:T(8,128)(2,1)} %feat.5, ...), custom_call_target="tpu_custom_call" | custom-call | tf_op jit(solution)/shard_map/pallas_call | solution.py:251
  2.0 6.0 %collective-permute-start = (bf16[2,4,64,256]{3,2,1,0:T(8,128)(2,1)S(1)}, bf16[2,4,64,256]{3,2,1,0:T(8,128)(2,1)S(1)}, u32[]{:S(2)}, u32[]{:S(2)}) collective-permute-start(bf16[2,4,64,256]{3,2,1,0:T(8,128)(2,1)S(1)} %get-tuple-element.30), channel_id=1, source_target_pairs={{0,14},{2,0},{4,2},{6,4},{8,6},{10,8},{12,10},{14,12},{1,15},{3,1}... | collective-permute-start | bytes 786440 | tf_op jit(solution)/shard_map/ppermute | solution.py:271
  8.0 0.6 %collective-permute-start.2 = (bf16[2,4,8,256]{3,2,1,0:T(8,128)(2,1)S(1)}, bf16[2,4,8,256]{3,2,1,0:T(8,128)(2,1)S(1)}, u32[]{:S(2)}, u32[]{:S(2)}) collective-permute-start(bf16[2,4,8,256]{3,2,1,0:T(8,128)(2,1)S(1)} %get-tuple-element.32), channel_id=1, source_target_pairs={{0,15},{1,14},{2,1},{3,0},{4,3},{5,2},{6,5},{7,4},{8,7},{9,6},{10,... | collective-permute-start | bytes 98312 | tf_op jit(solution)/shard_map/ppermute | solution.py:271
  8.7 0.6 %collective-permute-done.1.right = bf16[2,4,8,256]{3,2,1,0:T(8,128)(2,1)S(1)} collective-permute-done((bf16[2,4,8,256]{3,2,1,0:T(8,128)(2,1)S(1)}, bf16[2,4,8,256]{3,2,1,0:T(8,128)(2,1)S(1)}, u32[]{:S(2)}, u32[]{:S(2)}) %collective-permute-start.1) | collective-permute-done | bytes 32800 | tf_op jit(solution)/shard_map/ppermute | solution.py:271
  9.2 5.1 %collective-permute-done.2.corner = bf16[2,4,8,256]{3,2,1,0:T(8,128)(2,1)S(1)} collective-permute-done((bf16[2,4,8,256]{3,2,1,0:T(8,128)(2,1)S(1)}, bf16[2,4,8,256]{3,2,1,0:T(8,128)(2,1)S(1)}, u32[]{:S(2)}, u32[]{:S(2)}) %collective-permute-start.2) | collective-permute-done | bytes 32800 | tf_op jit(solution)/shard_map/ppermute | solution.py:271
  14.3 3.4 %shard_map.102 = (bf16[512,256]{1,0:T(8,128)(2,1)S(1)}, bf16[512,256]{1,0:T(8,128)(2,1)S(1)}, bf16[4,64,256]{2,1,0:T(8,128)(2,1)S(1)}, bf16[4,64,256]{2,1,0:T(8,128)(2,1)S(1)}, bf16[2,4,64,256]{3,2,1,0:T(8,128)(2,1)S(1)}) custom-call(bf16[8,64,256]{2,1,0:T(8,128)(2,1)S(1)} %copy-done, bf16[8,64,256]{2,1,0:T(8,128)(2,1)S(1)} %get-tuple-element.28.cot, ...), custom_call_target="tpu_custom_call" | custom-call | tf_op jit(solution)/shard_map/pallas_call | solution.py:251
  17.7 0.1 collective-permute-start.3
  17.8 0.1 collective-permute-start.7
  17.9 1.4 %collective-permute-done.3 = bf16[512,256]{1,0:T(8,128)(2,1)S(1)} collective-permute-done((bf16[512,256]{1,0:T(8,128)(2,1)S(1)}, bf16[512,256]{1,0:T(8,128)(2,1)S(1)}, u32[]{:S(2)}, u32[]{:S(2)}) %collective-permute-start.3) | collective-permute-done | bytes 262176 | tf_op jit(solution)/shard_map/ppermute | solution.py:280
  19.3 0.1 add_convert_fusion
  19.5 1.7 %collective-permute-start.6 = (bf16[128,256]{1,0:T(8,128)(2,1)S(1)}, bf16[128,256]{1,0:T(8,128)(2,1)S(1)}, u32[]{:S(2)}, u32[]{:S(2)}) collective-permute-start(bf16[128,256]{1,0:T(8,128)(2,1)S(1)} %get-tuple-element.56), channel_id=1, source_target_pairs={{0,6},{2,4},{4,2},{6,0},{8,14},{10,12},{12,10},{14,8},{1,7},{3,5},... | collective-permute-start | bytes 196616 | tf_op jit(solution)/shard_map/ppermute | solution.py:280
  21.1 1.8 %collective-permute-start.5 = (bf16[128,256]{1,0:T(8,128)(2,1)S(1)}, bf16[128,256]{1,0:T(8,128)(2,1)S(1)}, u32[]{:S(2)}, u32[]{:S(2)}) collective-permute-start(bf16[128,256]{1,0:T(8,128)(2,1)S(1)} %get-tuple-element.57), channel_id=1, source_target_pairs={{0,4},{2,6},{4,0},{6,2},{8,12},{10,14},{12,8},{14,10},{1,5},{3,7},... | collective-permute-start | bytes 196616 | tf_op jit(solution)/shard_map/ppermute | solution.py:280
  23.0 7.6 %collective-permute-done.4 = bf16[128,256]{1,0:T(8,128)(2,1)S(1)} collective-permute-done((bf16[128,256]{1,0:T(8,128)(2,1)S(1)}, bf16[128,256]{1,0:T(8,128)(2,1)S(1)}, u32[]{:S(2)}, u32[]{:S(2)}) %collective-permute-start.4) | collective-permute-done | bytes 65568 | tf_op jit(solution)/shard_map/ppermute | solution.py:280
  30.6 0.4 collective-permute-done.6
  31.0 0.9 %collective-permute-start.8 = (bf16[128,256]{1,0:T(8,128)(2,1)S(1)}, bf16[128,256]{1,0:T(8,128)(2,1)S(1)}, u32[]{:S(2)}, u32[]{:S(2)}) collective-permute-start(bf16[128,256]{1,0:T(8,128)(2,1)S(1)} %add_convert_fusion.2), channel_id=1, source_target_pairs={{0,8},{2,10},{4,12},{6,14},{8,0},{10,2},{12,4},{14,6},{1,9},{3,11}... | collective-permute-start | bytes 196616 | tf_op jit(solution)/shard_map/ppermute | solution.py:280
  32.1 4.2 %collective-permute-done.8 = bf16[128,256]{1,0:T(8,128)(2,1)S(1)} collective-permute-done((bf16[128,256]{1,0:T(8,128)(2,1)S(1)}, bf16[128,256]{1,0:T(8,128)(2,1)S(1)}, u32[]{:S(2)}, u32[]{:S(2)}) %collective-permute-start.8) | collective-permute-done | bytes 65568 | tf_op jit(solution)/shard_map/ppermute | solution.py:280
  36.3 1.8 %collective-permute-start.9 = (bf16[128,256]{1,0:T(8,128)(2,1)S(1)}, bf16[128,256]{1,0:T(8,128)(2,1)S(1)}, u32[]{:S(2)}, u32[]{:S(2)}) collective-permute-start(bf16[128,256]{1,0:T(8,128)(2,1)S(1)} %get-tuple-element.52), channel_id=1, source_target_pairs={{0,2},{2,0},{4,6},{6,4},{8,10},{10,8},{12,14},{14,12},{1,3},{3,1},... | collective-permute-start | bytes 196616 | tf_op jit(solution)/shard_map/ppermute | solution.py:280
  38.1 1.7 %collective-permute-start.11 = (bf16[128,256]{1,0:T(8,128)(2,1)S(1)}, bf16[128,256]{1,0:T(8,128)(2,1)S(1)}, u32[]{:S(2)}, u32[]{:S(2)}) collective-permute-start(bf16[128,256]{1,0:T(8,128)(2,1)S(1)} %get-tuple-element.52), channel_id=1, source_target_pairs={{0,6},{2,4},{4,2},{6,0},{8,14},{10,12},{12,10},{14,8},{1,7},{3,5},... | collective-permute-start | bytes 196616 | tf_op jit(solution)/shard_map/ppermute | solution.py:280
  39.9 1.5 %shard_map.103 = (bf16[8,64,256]{2,1,0:T(8,128)(2,1)}, bf16[8,64,256]{2,1,0:T(8,128)(2,1)}) custom-call(bf16[8,64,256]{2,1,0:T(8,128)(2,1)S(1)} %copy-done, bf16[8,64,256]{2,1,0:T(8,128)(2,1)S(1)} %get-tuple-element.28.cot, s32[8,64]{1,0:T(8,128)S(1)} %get-tuple-element.29.domain, f32[1,256]{1,0:T(1,128)S(1)} %get-tuple-element.35.gain, ...), custom_call_target="tpu_custom_call" | custom-call | tf_op jit(solution)/shard_map/pallas_call | solution.py:251
  41.4 1.0 %collective-permute-done.10 = bf16[128,256]{1,0:T(8,128)(2,1)S(1)} collective-permute-done((bf16[128,256]{1,0:T(8,128)(2,1)S(1)}, bf16[128,256]{1,0:T(8,128)(2,1)S(1)}, u32[]{:S(2)}, u32[]{:S(2)}) %collective-permute-start.10) | collective-permute-done | bytes 65568 | tf_op jit(solution)/shard_map/ppermute | solution.py:280
  42.4 0.9 %collective-permute-done.11 = bf16[128,256]{1,0:T(8,128)(2,1)S(1)} collective-permute-done((bf16[128,256]{1,0:T(8,128)(2,1)S(1)}, bf16[128,256]{1,0:T(8,128)(2,1)S(1)}, u32[]{:S(2)}, u32[]{:S(2)}) %collective-permute-start.11) | collective-permute-done | bytes 65568 | tf_op jit(solution)/shard_map/ppermute | solution.py:280
  43.3 0.1 collective-permute-start.13
  43.4 1.5 %collective-permute-done.13.col_peer = bf16[512,256]{1,0:T(8,128)(2,1)S(1)} collective-permute-done((bf16[512,256]{1,0:T(8,128)(2,1)S(1)}, bf16[512,256]{1,0:T(8,128)(2,1)S(1)}, u32[]{:S(2)}, u32[]{:S(2)}) %collective-permute-start.13) | collective-permute-done | bytes 262176 | tf_op jit(solution)/shard_map/ppermute | solution.py:280
  44.9 1.3 %shard_map.104 = (f32[256,768]{1,0:T(8,128)}, f32[256,256]{1,0:T(8,128)}, f32[1,256]{1,0:T(1,128)}) custom-call(bf16[512,256]{1,0:T(8,128)(2,1)S(1)} %constant_dynamic-update-slice_fusion.half, bf16[512,256]{1,0:T(8,128)(2,1)S(1)} %collective-permute-done.13.col_peer, bf16[256,768]{1,0:T(8,128)(2,1)S(1)} %get-tuple-element.33.wqkv, ...), custom_call_target="tpu_custom_call" | custom-call | tf_op jit(solution)/shard_map/pallas_call | solution.py:251
  (22 shorter events, 0.3 us)
Async XLA Ops:
  0.6 13.6 %copy-start = (bf16[8,64,256]{2,1,0:T(8,128)(2,1)S(1)}, bf16[8,64,256]{2,1,0:T(8,128)(2,1)}, u32[]{:S(2)}) copy-start(bf16[8,64,256]{2,1,0:T(8,128)(2,1)} %feat.5) | copy-start | bytes 786436
  2.0 12.3 %collective-permute-start = (bf16[2,4,64,256]{3,2,1,0:T(8,128)(2,1)S(1)}, bf16[2,4,64,256]{3,2,1,0:T(8,128)(2,1)S(1)}, u32[]{:S(2)}, u32[]{:S(2)}) collective-permute-start(bf16[2,4,64,256]{3,2,1,0:T(8,128)(2,1)S(1)} %get-tuple-element.30), channel_id=1, source_target_pairs={{0,14},{2,0},{4,2},{6,4},{8,6},{10,8},{12,10},{14,12},{1,15},{3,1}... | collective-permute-start | bytes 786440 | tf_op jit(solution)/shard_map/ppermute | solution.py:271
  8.0 1.2 %collective-permute-start.1 = (bf16[2,4,8,256]{3,2,1,0:T(8,128)(2,1)S(1)}, bf16[2,4,8,256]{3,2,1,0:T(8,128)(2,1)S(1)}, u32[]{:S(2)}, u32[]{:S(2)}) collective-permute-start(bf16[2,4,8,256]{3,2,1,0:T(8,128)(2,1)S(1)} %get-tuple-element.31), channel_id=1, source_target_pairs={{0,1},{1,0},{2,3},{3,2},{4,5},{5,4},{6,7},{7,6},{8,9},{9,8},{10,11... | collective-permute-start | bytes 98312 | tf_op jit(solution)/shard_map/ppermute | solution.py:271
  8.0 6.3 %collective-permute-start.2 = (bf16[2,4,8,256]{3,2,1,0:T(8,128)(2,1)S(1)}, bf16[2,4,8,256]{3,2,1,0:T(8,128)(2,1)S(1)}, u32[]{:S(2)}, u32[]{:S(2)}) collective-permute-start(bf16[2,4,8,256]{3,2,1,0:T(8,128)(2,1)S(1)} %get-tuple-element.32), channel_id=1, source_target_pairs={{0,15},{1,14},{2,1},{3,0},{4,3},{5,2},{6,5},{7,4},{8,7},{9,6},{10,... | collective-permute-start | bytes 98312 | tf_op jit(solution)/shard_map/ppermute | solution.py:271
  17.7 1.6 %collective-permute-start.3 = (bf16[512,256]{1,0:T(8,128)(2,1)S(1)}, bf16[512,256]{1,0:T(8,128)(2,1)S(1)}, u32[]{:S(2)}, u32[]{:S(2)}) collective-permute-start(bf16[512,256]{1,0:T(8,128)(2,1)S(1)} %get-tuple-element.37), channel_id=1, source_target_pairs={{0,1},{1,0},{2,3},{3,2},{4,5},{5,4},{6,7},{7,6},{8,9},{9,8},{10,11... | collective-permute-start | bytes 786440 | tf_op jit(solution)/shard_map/ppermute | solution.py:280
  17.8 13.2 %collective-permute-start.7 = (bf16[2,4,64,256]{3,2,1,0:T(8,128)(2,1)S(1)}, bf16[2,4,64,256]{3,2,1,0:T(8,128)(2,1)S(1)}, u32[]{:S(2)}, u32[]{:S(2)}) collective-permute-start(bf16[2,4,64,256]{3,2,1,0:T(8,128)(2,1)S(1)} %get-tuple-element.38), channel_id=1, source_target_pairs={{0,2},{2,4},{4,6},{6,8},{8,10},{10,12},{12,14},{14,0},{1,3},{3,5},... | collective-permute-start | bytes 786440 | tf_op jit(solution)/shard_map/ppermute | solution.py:276
  19.4 11.1 %collective-permute-start.4 = (bf16[128,256]{1,0:T(8,128)(2,1)S(1)}, bf16[128,256]{1,0:T(8,128)(2,1)S(1)}, u32[]{:S(2)}, u32[]{:S(2)}) collective-permute-start(bf16[128,256]{1,0:T(8,128)(2,1)S(1)} %get-tuple-element.55), channel_id=1, source_target_pairs={{0,2},{2,0},{4,6},{6,4},{8,10},{10,8},{12,14},{14,12},{1,3},{3,1},... | collective-permute-start | bytes 196616 | tf_op jit(solution)/shard_map/ppermute | solution.py:280
  19.5 11.5 %collective-permute-start.6 = (bf16[128,256]{1,0:T(8,128)(2,1)S(1)}, bf16[128,256]{1,0:T(8,128)(2,1)S(1)}, u32[]{:S(2)}, u32[]{:S(2)}) collective-permute-start(bf16[128,256]{1,0:T(8,128)(2,1)S(1)} %get-tuple-element.56), channel_id=1, source_target_pairs={{0,6},{2,4},{4,2},{6,0},{8,14},{10,12},{12,10},{14,8},{1,7},{3,5},... | collective-permute-start | bytes 196616 | tf_op jit(solution)/shard_map/ppermute | solution.py:280
  21.1 9.8 %collective-permute-start.5 = (bf16[128,256]{1,0:T(8,128)(2,1)S(1)}, bf16[128,256]{1,0:T(8,128)(2,1)S(1)}, u32[]{:S(2)}, u32[]{:S(2)}) collective-permute-start(bf16[128,256]{1,0:T(8,128)(2,1)S(1)} %get-tuple-element.57), channel_id=1, source_target_pairs={{0,4},{2,6},{4,0},{6,2},{8,12},{10,14},{12,8},{14,10},{1,5},{3,7},... | collective-permute-start | bytes 196616 | tf_op jit(solution)/shard_map/ppermute | solution.py:280
  31.0 5.2 %collective-permute-start.8 = (bf16[128,256]{1,0:T(8,128)(2,1)S(1)}, bf16[128,256]{1,0:T(8,128)(2,1)S(1)}, u32[]{:S(2)}, u32[]{:S(2)}) collective-permute-start(bf16[128,256]{1,0:T(8,128)(2,1)S(1)} %add_convert_fusion.2), channel_id=1, source_target_pairs={{0,8},{2,10},{4,12},{6,14},{8,0},{10,2},{12,4},{14,6},{1,9},{3,11}... | collective-permute-start | bytes 196616 | tf_op jit(solution)/shard_map/ppermute | solution.py:280
  32.0 7.9 %collective-permute-start.12 = (bf16[4,4,8,256]{3,2,1,0:T(8,128)(2,1)S(1)}, bf16[4,4,8,256]{3,2,1,0:T(8,128)(2,1)S(1)}, u32[]{:S(2)}, u32[]{:S(2)}) collective-permute-start(bf16[4,4,8,256]{3,2,1,0:T(8,128)(2,1)S(1)} %pad_maximum_fusion), channel_id=1, source_target_pairs={{0,1},{1,0},{2,3},{3,2},{4,5},{5,4},{6,7},{7,6},{8,9},{9,8},{10,11... | collective-permute-start | bytes 196616 | tf_op jit(solution)/shard_map/ppermute | solution.py:276
  36.3 5.1 %collective-permute-start.9 = (bf16[128,256]{1,0:T(8,128)(2,1)S(1)}, bf16[128,256]{1,0:T(8,128)(2,1)S(1)}, u32[]{:S(2)}, u32[]{:S(2)}) collective-permute-start(bf16[128,256]{1,0:T(8,128)(2,1)S(1)} %get-tuple-element.52), channel_id=1, source_target_pairs={{0,2},{2,0},{4,6},{6,4},{8,10},{10,8},{12,14},{14,12},{1,3},{3,1},... | collective-permute-start | bytes 196616 | tf_op jit(solution)/shard_map/ppermute | solution.py:280
  38.1 4.3 %collective-permute-start.10 = (bf16[128,256]{1,0:T(8,128)(2,1)S(1)}, bf16[128,256]{1,0:T(8,128)(2,1)S(1)}, u32[]{:S(2)}, u32[]{:S(2)}) collective-permute-start(bf16[128,256]{1,0:T(8,128)(2,1)S(1)} %get-tuple-element.52), channel_id=1, source_target_pairs={{0,4},{2,6},{4,0},{6,2},{8,12},{10,14},{12,8},{14,10},{1,5},{3,7},... | collective-permute-start | bytes 196616 | tf_op jit(solution)/shard_map/ppermute | solution.py:280
  38.1 5.2 %collective-permute-start.11 = (bf16[128,256]{1,0:T(8,128)(2,1)S(1)}, bf16[128,256]{1,0:T(8,128)(2,1)S(1)}, u32[]{:S(2)}, u32[]{:S(2)}) collective-permute-start(bf16[128,256]{1,0:T(8,128)(2,1)S(1)} %get-tuple-element.52), channel_id=1, source_target_pairs={{0,6},{2,4},{4,2},{6,0},{8,14},{10,12},{12,10},{14,8},{1,7},{3,5},... | collective-permute-start | bytes 196616 | tf_op jit(solution)/shard_map/ppermute | solution.py:280
  43.3 1.6 %collective-permute-start.13 = (bf16[512,256]{1,0:T(8,128)(2,1)S(1)}, bf16[512,256]{1,0:T(8,128)(2,1)S(1)}, u32[]{:S(2)}, u32[]{:S(2)}) collective-permute-start(bf16[512,256]{1,0:T(8,128)(2,1)S(1)} %constant_dynamic-update-slice_fusion.half), channel_id=1, source_target_pairs={{0,1},{1,0},{2,3},{3,2},{4,5},{5,4},{6,7},{7,6},{8,9},{9,8},{10,11... | collective-permute-start | bytes 786440 | tf_op jit(solution)/shard_map/ppermute | solution.py:280

commit v6 on v5

--- a/solution.py
+++ b/solution.py
@@ -37,8 +37,8 @@
 
 
 def pack_kernel(
-    feat, cot, domain_hbm, wqkv_hbm, wproj_hbm, gain_hbm,
-    rows_out, right_out, corner_out, held, domain, wqkv, wproj, gain,
+    feat, cot, domain_hbm,
+    rows_out, right_out, corner_out, held, domain,
     sems,
 ):
     channels = feat.shape[-1]
@@ -50,9 +50,6 @@
             (feat.at[0:SHIFT], rows_out.at[0]),
             (feat.at[SHIFT:WIN, 0:WIN], right_out.at[0]),
             (feat.at[0:SHIFT, 0:WIN], corner_out.at[0]),
-            (wqkv_hbm, wqkv),
-            (wproj_hbm, wproj),
-            (gain_hbm, gain),
         ))
     ]
     for copy in copies:
@@ -67,6 +64,15 @@
         edge = held[SHIFT + i, 0:WIN, :].astype(F32) * masks[SHIFT + i][0:WIN]
         right_out[1, i] = edge.astype(BF16)
     for copy in copies[2:]:
+        copy.wait()
+
+
+def fetch_kernel(wqkv_hbm, wproj_hbm, gain_hbm, wqkv, wproj, gain, sems):
+    pairs = ((wqkv_hbm, wqkv), (wproj_hbm, wproj), (gain_hbm, gain))
+    copies = [pltpu.make_async_copy(a, b, sems.at[i]) for i, (a, b) in enumerate(pairs)]
+    for copy in copies:
+        copy.start()
+    for copy in copies:
         copy.wait()
 
 
@@ -292,7 +298,7 @@
     def shape(dims, dtype):
         return jax.ShapeDtypeStruct(dims, dtype)
 
-    rows_out, right_out, corner_out, cotangent, domain, qkv_weight, proj_weight, gain = run(
+    rows_out, right_out, corner_out, cotangent, domain = run(
         pack_kernel,
         (
             shape((2, SHIFT, cols, channels), BF16),
@@ -300,13 +306,24 @@
             shape((2, SHIFT, WIN, channels), BF16),
             shape(cotangent.shape, cotangent.dtype),
             shape(domain.shape, domain.dtype),
+        ),
+        [pltpu.SemaphoreType.DMA((5,))],
+        features, cotangent, domain,
+        unstaged=(0, 1, 2),
+    )
+    qkv_weight, proj_weight, gain, right_out = lax.optimization_barrier(
+        (qkv_weight, proj_weight, gain, right_out)
+    )
+    qkv_weight, proj_weight, gain = run(
+        fetch_kernel,
+        (
             shape(qkv_weight.shape, qkv_weight.dtype),
             shape(proj_weight.shape, proj_weight.dtype),
             shape(gain.shape, gain.dtype),
         ),
-        [pltpu.SemaphoreType.DMA((8,))],
-        features, cotangent, domain, qkv_weight, proj_weight, gain,
-        unstaged=(0, 1, 2, 3, 4, 5),
+        [pltpu.SemaphoreType.DMA((3,))],
+        qkv_weight, proj_weight, gain,
+        unstaged=(0, 1, 2),
     )
     below = ahead(rows_out, ("row",))
     right = ahead(right_out, ("col",))

time: 46.3 us -> 46.1 us (level)
  waiting for transfers between devices: 22.6 us -> 21.5 us
  Pallas kernels: 7.52 us -> 8.29 us
    ppermute x3, waiting for transfers between devices: 5.62 us -> 4.55 us  [ahead(): return lax.ppermute(array, axes if len(axes) > 1 else axes[0], pairs)]
    pallas_call x4 -> x5, Pallas kernels: 7.52 us -> 8.29 us  [run(): pl.pallas_call(kernel, out_shape=out_shapes, in_specs=[HBM if i in unstag...]
  transfers between devices with their start and end apart: 14 -> 14, of which waited for: 9 -> 8; matrix products, arithmetic and copies ran while one was open for 1% -> 1% of each run, Pallas kernels for 3% -> 6%
where the time goes in v6:
time: 46.1 us; the launch traced here: 45.9 us
  waiting for transfers between devices  21.5 us (47%)
  starting transfers between devices  15 us (33%)
  Pallas kernels  8.29 us (18%)
  between operations  0.81 us (2%)
    ppermute x9, waiting for transfers between devices, swap(): lax.ppermute(array, axis, [(i, i ^ bit) for i in range(lax.axis_size(axis...  17 us
    pallas_call x5, Pallas kernels, run(): pl.pallas_call(kernel, out_shape=out_shapes, in_specs=[HBM if i in unstag...  8.29 us
    ppermute x9, starting transfers between devices, swap(): lax.ppermute(array, axis, [(i, i ^ bit) for i in range(lax.axis_size(axis...  8.14 us
    ppermute x3, starting transfers between devices, ahead(): return lax.ppermute(array, axes if len(axes) > 1 else axes[0], pairs)  6.68 us
    ppermute x3, waiting for transfers between devices, ahead(): return lax.ppermute(array, axes if len(axes) > 1 else axes[0], pairs)  4.55 us
  transfers between devices with their start and end apart: 14, of which 8 were waited for; matrix products, arithmetic and copies ran while one was open for 1% of the time, Pallas kernels for 6%

profile of v6, /device:TPU:0, one launch (start us, length us, event | category | flops | bytes accessed | tf_op | source)
XLA Modules:
  0.0 45.9 jit_solution(15788040090073277150)
XLA Ops:
  0.6 1.0 %shard_map.101 = (bf16[2,4,64,256]{3,2,1,0:T(8,128)(2,1)S(1)}, bf16[2,4,8,256]{3,2,1,0:T(8,128)(2,1)S(1)}, bf16[2,4,8,256]{3,2,1,0:T(8,128)(2,1)S(1)}, bf16[8,64,256]{2,1,0:T(8,128)(2,1)S(1)}, s32[8,64]{1,0:T(8,128)S(1)}) custom-call(bf16[8,64,256]{2,1,0:T(8,128)(2,1)} %feat.5, bf16[8,64,256]{2,1,0:T(8,128)(2,1)} %cot.1, s32[8,64]{1,0:T(8,128)} %domain_hbm.1), custom_call_target="tpu_custom_call" | custom-call | tf_op jit(solution)/shard_map/pallas_call | solution.py:257
  1.7 6.0 %collective-permute-start = (bf16[2,4,64,256]{3,2,1,0:T(8,128)(2,1)S(1)}, bf16[2,4,64,256]{3,2,1,0:T(8,128)(2,1)S(1)}, u32[]{:S(2)}, u32[]{:S(2)}) collective-permute-start(bf16[2,4,64,256]{3,2,1,0:T(8,128)(2,1)S(1)} %get-tuple-element.34), channel_id=1, source_target_pairs={{0,14},{2,0},{4,2},{6,4},{8,6},{10,8},{12,10},{14,12},{1,15},{3,1}... | collective-permute-start | bytes 786440 | tf_op jit(solution)/shard_map/ppermute | solution.py:277
  7.7 0.6 %collective-permute-start.2 = (bf16[2,4,8,256]{3,2,1,0:T(8,128)(2,1)S(1)}, bf16[2,4,8,256]{3,2,1,0:T(8,128)(2,1)S(1)}, u32[]{:S(2)}, u32[]{:S(2)}) collective-permute-start(bf16[2,4,8,256]{3,2,1,0:T(8,128)(2,1)S(1)} %get-tuple-element.37), channel_id=1, source_target_pairs={{0,15},{1,14},{2,1},{3,0},{4,3},{5,2},{6,5},{7,4},{8,7},{9,6},{10,... | collective-permute-start | bytes 98312 | tf_op jit(solution)/shard_map/ppermute | solution.py:277
  8.4 1.0 %shard_map.102 = (bf16[256,768]{1,0:T(8,128)(2,1)S(1)}, bf16[256,256]{1,0:T(8,128)(2,1)S(1)}, f32[1,256]{1,0:T(1,128)S(1)}) custom-call(bf16[256,768]{1,0:T(8,128)(2,1)} %wqkv_hbm, bf16[256,256]{1,0:T(8,128)(2,1)} %wproj_hbm, f32[1,256]{1,0:T(1,128)} %bitcast.14), custom_call_target="tpu_custom_call" | custom-call | tf_op jit(solution)/shard_map/pallas_call | solution.py:257
  9.4 4.5 %collective-permute-done.2.corner = bf16[2,4,8,256]{3,2,1,0:T(8,128)(2,1)S(1)} collective-permute-done((bf16[2,4,8,256]{3,2,1,0:T(8,128)(2,1)S(1)}, bf16[2,4,8,256]{3,2,1,0:T(8,128)(2,1)S(1)}, u32[]{:S(2)}, u32[]{:S(2)}) %collective-permute-start.2) | collective-permute-done | bytes 32800 | tf_op jit(solution)/shard_map/ppermute | solution.py:277
  14.0 3.4 %shard_map.103 = (bf16[512,256]{1,0:T(8,128)(2,1)S(1)}, bf16[512,256]{1,0:T(8,128)(2,1)S(1)}, bf16[4,64,256]{2,1,0:T(8,128)(2,1)S(1)}, bf16[4,64,256]{2,1,0:T(8,128)(2,1)S(1)}, bf16[2,4,64,256]{3,2,1,0:T(8,128)(2,1)S(1)}) custom-call(bf16[8,64,256]{2,1,0:T(8,128)(2,1)S(1)} %copy-done, bf16[8,64,256]{2,1,0:T(8,128)(2,1)S(1)} %get-tuple-element.32.cot, ...), custom_call_target="tpu_custom_call" | custom-call | tf_op jit(solution)/shard_map/pallas_call | solution.py:257
  17.4 0.1 collective-permute-start.3
  17.5 0.1 collective-permute-start.7
  17.6 1.4 %collective-permute-done.3 = bf16[512,256]{1,0:T(8,128)(2,1)S(1)} collective-permute-done((bf16[512,256]{1,0:T(8,128)(2,1)S(1)}, bf16[512,256]{1,0:T(8,128)(2,1)S(1)}, u32[]{:S(2)}, u32[]{:S(2)}) %collective-permute-start.3) | collective-permute-done | bytes 262176 | tf_op jit(solution)/shard_map/ppermute | solution.py:286
  19.0 0.1 add_convert_fusion
  19.2 1.7 %collective-permute-start.6 = (bf16[128,256]{1,0:T(8,128)(2,1)S(1)}, bf16[128,256]{1,0:T(8,128)(2,1)S(1)}, u32[]{:S(2)}, u32[]{:S(2)}) collective-permute-start(bf16[128,256]{1,0:T(8,128)(2,1)S(1)} %get-tuple-element.64), channel_id=1, source_target_pairs={{0,6},{2,4},{4,2},{6,0},{8,14},{10,12},{12,10},{14,8},{1,7},{3,5},... | collective-permute-start | bytes 196616 | tf_op jit(solution)/shard_map/ppermute | solution.py:286
  20.9 1.8 %collective-permute-start.5 = (bf16[128,256]{1,0:T(8,128)(2,1)S(1)}, bf16[128,256]{1,0:T(8,128)(2,1)S(1)}, u32[]{:S(2)}, u32[]{:S(2)}) collective-permute-start(bf16[128,256]{1,0:T(8,128)(2,1)S(1)} %get-tuple-element.65), channel_id=1, source_target_pairs={{0,4},{2,6},{4,0},{6,2},{8,12},{10,14},{12,8},{14,10},{1,5},{3,7},... | collective-permute-start | bytes 196616 | tf_op jit(solution)/shard_map/ppermute | solution.py:286
  22.7 7.6 %collective-permute-done.4 = bf16[128,256]{1,0:T(8,128)(2,1)S(1)} collective-permute-done((bf16[128,256]{1,0:T(8,128)(2,1)S(1)}, bf16[128,256]{1,0:T(8,128)(2,1)S(1)}, u32[]{:S(2)}, u32[]{:S(2)}) %collective-permute-start.4) | collective-permute-done | bytes 65568 | tf_op jit(solution)/shard_map/ppermute | solution.py:286
  30.3 0.4 collective-permute-done.6
  30.7 0.9 %collective-permute-start.8 = (bf16[128,256]{1,0:T(8,128)(2,1)S(1)}, bf16[128,256]{1,0:T(8,128)(2,1)S(1)}, u32[]{:S(2)}, u32[]{:S(2)}) collective-permute-start(bf16[128,256]{1,0:T(8,128)(2,1)S(1)} %add_convert_fusion.2), channel_id=1, source_target_pairs={{0,8},{2,10},{4,12},{6,14},{8,0},{10,2},{12,4},{14,6},{1,9},{3,11}... | collective-permute-start | bytes 196616 | tf_op jit(solution)/shard_map/ppermute | solution.py:286
  31.8 4.2 %collective-permute-done.8 = bf16[128,256]{1,0:T(8,128)(2,1)S(1)} collective-permute-done((bf16[128,256]{1,0:T(8,128)(2,1)S(1)}, bf16[128,256]{1,0:T(8,128)(2,1)S(1)}, u32[]{:S(2)}, u32[]{:S(2)}) %collective-permute-start.8) | collective-permute-done | bytes 65568 | tf_op jit(solution)/shard_map/ppermute | solution.py:286
  36.0 1.8 %collective-permute-start.9 = (bf16[128,256]{1,0:T(8,128)(2,1)S(1)}, bf16[128,256]{1,0:T(8,128)(2,1)S(1)}, u32[]{:S(2)}, u32[]{:S(2)}) collective-permute-start(bf16[128,256]{1,0:T(8,128)(2,1)S(1)} %get-tuple-element.60), channel_id=1, source_target_pairs={{0,2},{2,0},{4,6},{6,4},{8,10},{10,8},{12,14},{14,12},{1,3},{3,1},... | collective-permute-start | bytes 196616 | tf_op jit(solution)/shard_map/ppermute | solution.py:286
  37.8 1.7 %collective-permute-start.11 = (bf16[128,256]{1,0:T(8,128)(2,1)S(1)}, bf16[128,256]{1,0:T(8,128)(2,1)S(1)}, u32[]{:S(2)}, u32[]{:S(2)}) collective-permute-start(bf16[128,256]{1,0:T(8,128)(2,1)S(1)} %get-tuple-element.60), channel_id=1, source_target_pairs={{0,6},{2,4},{4,2},{6,0},{8,14},{10,12},{12,10},{14,8},{1,7},{3,5},... | collective-permute-start | bytes 196616 | tf_op jit(solution)/shard_map/ppermute | solution.py:286
  39.6 1.5 %shard_map.104 = (bf16[8,64,256]{2,1,0:T(8,128)(2,1)}, bf16[8,64,256]{2,1,0:T(8,128)(2,1)}) custom-call(bf16[8,64,256]{2,1,0:T(8,128)(2,1)S(1)} %copy-done, bf16[8,64,256]{2,1,0:T(8,128)(2,1)S(1)} %get-tuple-element.32.cot, s32[8,64]{1,0:T(8,128)S(1)} %get-tuple-element.33.domain, f32[1,256]{1,0:T(1,128)S(1)} %get-tuple-element.43.gain, ...), custom_call_target="tpu_custom_call" | custom-call | tf_op jit(solution)/shard_map/pallas_call | solution.py:257
  41.1 1.0 %collective-permute-done.10 = bf16[128,256]{1,0:T(8,128)(2,1)S(1)} collective-permute-done((bf16[128,256]{1,0:T(8,128)(2,1)S(1)}, bf16[128,256]{1,0:T(8,128)(2,1)S(1)}, u32[]{:S(2)}, u32[]{:S(2)}) %collective-permute-start.10) | collective-permute-done | bytes 65568 | tf_op jit(solution)/shard_map/ppermute | solution.py:286
  42.1 0.9 %collective-permute-done.11 = bf16[128,256]{1,0:T(8,128)(2,1)S(1)} collective-permute-done((bf16[128,256]{1,0:T(8,128)(2,1)S(1)}, bf16[128,256]{1,0:T(8,128)(2,1)S(1)}, u32[]{:S(2)}, u32[]{:S(2)}) %collective-permute-start.11) | collective-permute-done | bytes 65568 | tf_op jit(solution)/shard_map/ppermute | solution.py:286
  43.0 0.1 collective-permute-start.13
  43.1 1.5 %collective-permute-done.13.col_peer = bf16[512,256]{1,0:T(8,128)(2,1)S(1)} collective-permute-done((bf16[512,256]{1,0:T(8,128)(2,1)S(1)}, bf16[512,256]{1,0:T(8,128)(2,1)S(1)}, u32[]{:S(2)}, u32[]{:S(2)}) %collective-permute-start.13) | collective-permute-done | bytes 262176 | tf_op jit(solution)/shard_map/ppermute | solution.py:286
  44.6 1.3 %shard_map.105 = (f32[256,768]{1,0:T(8,128)}, f32[256,256]{1,0:T(8,128)}, f32[1,256]{1,0:T(1,128)}) custom-call(bf16[512,256]{1,0:T(8,128)(2,1)S(1)} %constant_dynamic-update-slice_fusion.half, bf16[512,256]{1,0:T(8,128)(2,1)S(1)} %collective-permute-done.13.col_peer, bf16[256,768]{1,0:T(8,128)(2,1)S(1)} %get-tuple-element.41.wqkv, ...), custom_call_target="tpu_custom_call" | custom-call | tf_op jit(solution)/shard_map/pallas_call | solution.py:257
  (23 shorter events, 0.3 us)
Async XLA Ops:
  1.7 12.3 %collective-permute-start = (bf16[2,4,64,256]{3,2,1,0:T(8,128)(2,1)S(1)}, bf16[2,4,64,256]{3,2,1,0:T(8,128)(2,1)S(1)}, u32[]{:S(2)}, u32[]{:S(2)}) collective-permute-start(bf16[2,4,64,256]{3,2,1,0:T(8,128)(2,1)S(1)} %get-tuple-element.34), channel_id=1, source_target_pairs={{0,14},{2,0},{4,2},{6,4},{8,6},{10,8},{12,10},{14,12},{1,15},{3,1}... | collective-permute-start | bytes 786440 | tf_op jit(solution)/shard_map/ppermute | solution.py:277
  7.7 1.7 %collective-permute-start.1 = (bf16[2,4,8,256]{3,2,1,0:T(8,128)(2,1)S(1)}, bf16[2,4,8,256]{3,2,1,0:T(8,128)(2,1)S(1)}, u32[]{:S(2)}, u32[]{:S(2)}) collective-permute-start(bf16[2,4,8,256]{3,2,1,0:T(8,128)(2,1)S(1)} %get-tuple-element.36), channel_id=1, source_target_pairs={{0,1},{1,0},{2,3},{3,2},{4,5},{5,4},{6,7},{7,6},{8,9},{9,8},{10,11... | collective-permute-start | bytes 98312 | tf_op jit(solution)/shard_map/ppermute | solution.py:277
  7.7 6.3 %copy-start = (bf16[8,64,256]{2,1,0:T(8,128)(2,1)S(1)}, bf16[8,64,256]{2,1,0:T(8,128)(2,1)}, u32[]{:S(2)}) copy-start(bf16[8,64,256]{2,1,0:T(8,128)(2,1)} %feat.5) | copy-start | bytes 786436
  7.7 6.3 %collective-permute-start.2 = (bf16[2,4,8,256]{3,2,1,0:T(8,128)(2,1)S(1)}, bf16[2,4,8,256]{3,2,1,0:T(8,128)(2,1)S(1)}, u32[]{:S(2)}, u32[]{:S(2)}) collective-permute-start(bf16[2,4,8,256]{3,2,1,0:T(8,128)(2,1)S(1)} %get-tuple-element.37), channel_id=1, source_target_pairs={{0,15},{1,14},{2,1},{3,0},{4,3},{5,2},{6,5},{7,4},{8,7},{9,6},{10,... | collective-permute-start | bytes 98312 | tf_op jit(solution)/shard_map/ppermute | solution.py:277
  17.4 1.6 %collective-permute-start.3 = (bf16[512,256]{1,0:T(8,128)(2,1)S(1)}, bf16[512,256]{1,0:T(8,128)(2,1)S(1)}, u32[]{:S(2)}, u32[]{:S(2)}) collective-permute-start(bf16[512,256]{1,0:T(8,128)(2,1)S(1)} %get-tuple-element.45), channel_id=1, source_target_pairs={{0,1},{1,0},{2,3},{3,2},{4,5},{5,4},{6,7},{7,6},{8,9},{9,8},{10,11... | collective-permute-start | bytes 786440 | tf_op jit(solution)/shard_map/ppermute | solution.py:286
  17.5 13.2 %collective-permute-start.7 = (bf16[2,4,64,256]{3,2,1,0:T(8,128)(2,1)S(1)}, bf16[2,4,64,256]{3,2,1,0:T(8,128)(2,1)S(1)}, u32[]{:S(2)}, u32[]{:S(2)}) collective-permute-start(bf16[2,4,64,256]{3,2,1,0:T(8,128)(2,1)S(1)} %get-tuple-element.46), channel_id=1, source_target_pairs={{0,2},{2,4},{4,6},{6,8},{8,10},{10,12},{12,14},{14,0},{1,3},{3,5},... | collective-permute-start | bytes 786440 | tf_op jit(solution)/shard_map/ppermute | solution.py:282
  19.1 11.2 %collective-permute-start.4 = (bf16[128,256]{1,0:T(8,128)(2,1)S(1)}, bf16[128,256]{1,0:T(8,128)(2,1)S(1)}, u32[]{:S(2)}, u32[]{:S(2)}) collective-permute-start(bf16[128,256]{1,0:T(8,128)(2,1)S(1)} %get-tuple-element.63), channel_id=1, source_target_pairs={{0,2},{2,0},{4,6},{6,4},{8,10},{10,8},{12,14},{14,12},{1,3},{3,1},... | collective-permute-start | bytes 196616 | tf_op jit(solution)/shard_map/ppermute | solution.py:286
  19.2 11.5 %collective-permute-start.6 = (bf16[128,256]{1,0:T(8,128)(2,1)S(1)}, bf16[128,256]{1,0:T(8,128)(2,1)S(1)}, u32[]{:S(2)}, u32[]{:S(2)}) collective-permute-start(bf16[128,256]{1,0:T(8,128)(2,1)S(1)} %get-tuple-element.64), channel_id=1, source_target_pairs={{0,6},{2,4},{4,2},{6,0},{8,14},{10,12},{12,10},{14,8},{1,7},{3,5},... | collective-permute-start | bytes 196616 | tf_op jit(solution)/shard_map/ppermute | solution.py:286
  20.9 9.8 %collective-permute-start.5 = (bf16[128,256]{1,0:T(8,128)(2,1)S(1)}, bf16[128,256]{1,0:T(8,128)(2,1)S(1)}, u32[]{:S(2)}, u32[]{:S(2)}) collective-permute-start(bf16[128,256]{1,0:T(8,128)(2,1)S(1)} %get-tuple-element.65), channel_id=1, source_target_pairs={{0,4},{2,6},{4,0},{6,2},{8,12},{10,14},{12,8},{14,10},{1,5},{3,7},... | collective-permute-start | bytes 196616 | tf_op jit(solution)/shard_map/ppermute | solution.py:286
  30.7 5.2 %collective-permute-start.8 = (bf16[128,256]{1,0:T(8,128)(2,1)S(1)}, bf16[128,256]{1,0:T(8,128)(2,1)S(1)}, u32[]{:S(2)}, u32[]{:S(2)}) collective-permute-start(bf16[128,256]{1,0:T(8,128)(2,1)S(1)} %add_convert_fusion.2), channel_id=1, source_target_pairs={{0,8},{2,10},{4,12},{6,14},{8,0},{10,2},{12,4},{14,6},{1,9},{3,11}... | collective-permute-start | bytes 196616 | tf_op jit(solution)/shard_map/ppermute | solution.py:286
  31.7 7.9 %collective-permute-start.12 = (bf16[4,4,8,256]{3,2,1,0:T(8,128)(2,1)S(1)}, bf16[4,4,8,256]{3,2,1,0:T(8,128)(2,1)S(1)}, u32[]{:S(2)}, u32[]{:S(2)}) collective-permute-start(bf16[4,4,8,256]{3,2,1,0:T(8,128)(2,1)S(1)} %pad_maximum_fusion), channel_id=1, source_target_pairs={{0,1},{1,0},{2,3},{3,2},{4,5},{5,4},{6,7},{7,6},{8,9},{9,8},{10,11... | collective-permute-start | bytes 196616 | tf_op jit(solution)/shard_map/ppermute | solution.py:282
  36.0 5.1 %collective-permute-start.9 = (bf16[128,256]{1,0:T(8,128)(2,1)S(1)}, bf16[128,256]{1,0:T(8,128)(2,1)S(1)}, u32[]{:S(2)}, u32[]{:S(2)}) collective-permute-start(bf16[128,256]{1,0:T(8,128)(2,1)S(1)} %get-tuple-element.60), channel_id=1, source_target_pairs={{0,2},{2,0},{4,6},{6,4},{8,10},{10,8},{12,14},{14,12},{1,3},{3,1},... | collective-permute-start | bytes 196616 | tf_op jit(solution)/shard_map/ppermute | solution.py:286
  37.8 4.3 %collective-permute-start.10 = (bf16[128,256]{1,0:T(8,128)(2,1)S(1)}, bf16[128,256]{1,0:T(8,128)(2,1)S(1)}, u32[]{:S(2)}, u32[]{:S(2)}) collective-permute-start(bf16[128,256]{1,0:T(8,128)(2,1)S(1)} %get-tuple-element.60), channel_id=1, source_target_pairs={{0,4},{2,6},{4,0},{6,2},{8,12},{10,14},{12,8},{14,10},{1,5},{3,7},... | collective-permute-start | bytes 196616 | tf_op jit(solution)/shard_map/ppermute | solution.py:286
  37.8 5.2 %collective-permute-start.11 = (bf16[128,256]{1,0:T(8,128)(2,1)S(1)}, bf16[128,256]{1,0:T(8,128)(2,1)S(1)}, u32[]{:S(2)}, u32[]{:S(2)}) collective-permute-start(bf16[128,256]{1,0:T(8,128)(2,1)S(1)} %get-tuple-element.60), channel_id=1, source_target_pairs={{0,6},{2,4},{4,2},{6,0},{8,14},{10,12},{12,10},{14,8},{1,7},{3,5},... | collective-permute-start | bytes 196616 | tf_op jit(solution)/shard_map/ppermute | solution.py:286
  43.0 1.6 %collective-permute-start.13 = (bf16[512,256]{1,0:T(8,128)(2,1)S(1)}, bf16[512,256]{1,0:T(8,128)(2,1)S(1)}, u32[]{:S(2)}, u32[]{:S(2)}) collective-permute-start(bf16[512,256]{1,0:T(8,128)(2,1)S(1)} %constant_dynamic-update-slice_fusion.half), channel_id=1, source_target_pairs={{0,1},{1,0},{2,3},{3,2},{4,5},{5,4},{6,7},{7,6},{8,9},{9,8},{10,11... | collective-permute-start | bytes 786440 | tf_op jit(solution)/shard_map/ppermute | solution.py:286

commit v7 on v6

--- a/solution.py
+++ b/solution.py
@@ -78,8 +78,8 @@
 
 def block_kernel(
     feat, cot, domain, below, right, corner, wqkv, wproj, gain,
-    keep, send, att_keep, dn_keep, both_send,
-    buf, shifted, projected, dattended, dcontext, context, dprojected, grads,
+    keep, send, context, dprojected,
+    buf, shifted, projected, dattended, dcontext, grads,
     query_held, dctx_held, scores_held, dchances_held, chances_held, dscore_held,
 ):
     tile_rows, cols, channels = feat.shape
@@ -183,6 +183,11 @@
         pl.ds(pl.multiple_of((1 - mine) * 2 * channels, 2 * channels), 2 * channels), :
     ]
 
+
+def results_kernel(context, dprojected, wproj, wqkv, att_keep, dn_keep, both_send):
+    channels = wproj.shape[0]
+    cells = WIN * WIN
+    windows = context.shape[0] // cells
     full = dot(context[...], wproj[...], 1, 0)
     for w in range(windows):
         tile = full[cells * w : cells * (w + 1)].reshape(WIN, WIN, channels).astype(BF16)
@@ -330,14 +335,13 @@
     corner = ahead(corner_out, ("row", "col"))
 
     strip = shape((SHIFT, cols, channels), BF16)
-    keep, send, att_keep, dn_keep, both_send = run(
+    keep, send, context, dprojected = run(
         block_kernel,
         (
             shape((2 * channels, channels), BF16),
             shape((2 * channels, channels), BF16),
-            strip,
-            strip,
-            shape((2, SHIFT, cols, channels), BF16),
+            shape((tokens, channels), BF16),
+            shape((tokens, 3 * channels), BF16),
         ),
         [
             pltpu.VMEM((WIN, cols + WIN, channels), F32),
@@ -345,8 +349,6 @@
             pltpu.VMEM((tokens, 3 * channels), BF16),
             pltpu.VMEM((tokens, channels), BF16),
             pltpu.VMEM((tokens, channels), BF16),
-            pltpu.VMEM((tokens, channels), BF16),
-            pltpu.VMEM((tokens, 3 * channels), BF16),
             pltpu.VMEM((4 * channels, channels), BF16),
             pltpu.VMEM((8, 4 * WIN * WIN, channels // 2), BF16),
             pltpu.VMEM((8, 4 * WIN * WIN, channels // 2), BF16),
@@ -357,6 +359,14 @@
         ],
         features, cotangent, domain, below, right, corner, qkv_weight, proj_weight, gain,
     )
+    strip = shape((SHIFT, cols, channels), BF16)
+    att_keep, dn_keep, both_send = run(
+        results_kernel,
+        (strip, strip, shape((2, SHIFT, cols, channels), BF16)),
+        [],
+        context, dprojected, proj_weight, qkv_weight,
+    )
+
     summed = add16(keep, swap(send, "col", 1))
     place = lax.axis_index("row") % 4
     chunk = channels // 2
@@ -370,12 +380,12 @@
     for part in received:
         own = own + part.astype(F32)
     own = own.astype(BF16)
-    own, both_rows = lax.optimization_barrier((own, both_rows))
     bit = 4
     while bit < lax.axis_size("row"):
         received = swap(own, "row", bit)
         own = add16(own, received)
         bit *= 2
+    own, both_rows = lax.optimization_barrier((own, both_rows))
     edges = jnp.stack(
         [part[:, cols - WIN :] for part in (both_rows[0], att_keep, both_rows[1], dn_keep)], 0
     )

time: 46.1 us -> 45.6 us (0.989)
  waiting for transfers between devices: 21.5 us -> 15.8 us
  starting transfers between devices: 15 us -> 20.2 us
    ppermute x9, waiting for transfers between devices: 17 us -> 8.64 us  [swap(): lax.ppermute(array, axis, [(i, i ^ bit) for i in range(lax.axis_size(axis...]
    ppermute x9, starting transfers between devices: 8.14 us -> 13.3 us  [swap(): lax.ppermute(array, axis, [(i, i ^ bit) for i in range(lax.axis_size(axis...]
    ppermute x2, waiting for transfers between devices: 0.01 us -> 2.64 us  [behind(): lax.ppermute(array, axis, [(i, (i + 1) % peers) for i in range(peers)])]
    pallas_call x5 -> x6, Pallas kernels: 8.29 us -> 8.24 us  [run(): pl.pallas_call(kernel, out_shape=out_shapes, in_specs=[HBM if i in unstag...]
  transfers between devices with their start and end apart: 14 -> 14, of which waited for: 8 -> 10; matrix products, arithmetic and copies ran while one was open for 1% -> 0% of each run, Pallas kernels for 6% -> 7%
where the time goes in v7:
time: 45.6 us; the launch traced here: 45.4 us
  starting transfers between devices  20.2 us (44%)
  waiting for transfers between devices  15.8 us (35%)
  Pallas kernels  8.24 us (18%)
  between operations  0.82 us (2%)
    ppermute x9, starting transfers between devices, swap(): lax.ppermute(array, axis, [(i, i ^ bit) for i in range(lax.axis_size(axis...  13.3 us
    ppermute x9, waiting for transfers between devices, swap(): lax.ppermute(array, axis, [(i, i ^ bit) for i in range(lax.axis_size(axis...  8.64 us
    pallas_call x6, Pallas kernels, run(): pl.pallas_call(kernel, out_shape=out_shapes, in_specs=[HBM if i in unstag...  8.24 us
    ppermute x3, starting transfers between devices, ahead(): return lax.ppermute(array, axes if len(axes) > 1 else axes[0], pairs)  6.68 us
    ppermute x3, waiting for transfers between devices, ahead(): return lax.ppermute(array, axes if len(axes) > 1 else axes[0], pairs)  4.55 us
    ppermute x2, waiting for transfers between devices, behind(): lax.ppermute(array, axis, [(i, (i + 1) % peers) for i in range(peers)])  2.64 us
  transfers between devices with their start and end apart: 14, of which 10 were waited for; matrix products, arithmetic and copies ran while one was open for 0% of the time, Pallas kernels for 7%

profile of v7, /device:TPU:0, one launch (start us, length us, event | category | flops | bytes accessed | tf_op | source)
XLA Modules:
  0.0 45.4 jit_solution(14895507241640856272)
XLA Ops:
  0.6 1.0 %shard_map.101 = (bf16[2,4,64,256]{3,2,1,0:T(8,128)(2,1)S(1)}, bf16[2,4,8,256]{3,2,1,0:T(8,128)(2,1)S(1)}, bf16[2,4,8,256]{3,2,1,0:T(8,128)(2,1)S(1)}, bf16[8,64,256]{2,1,0:T(8,128)(2,1)S(1)}, s32[8,64]{1,0:T(8,128)S(1)}) custom-call(bf16[8,64,256]{2,1,0:T(8,128)(2,1)} %feat.5, bf16[8,64,256]{2,1,0:T(8,128)(2,1)} %cot.1, s32[8,64]{1,0:T(8,128)} %domain_hbm.1), custom_call_target="tpu_custom_call" | custom-call | tf_op jit(solution)/shard_map/pallas_call | solution.py:262
  1.7 6.0 %collective-permute-start = (bf16[2,4,64,256]{3,2,1,0:T(8,128)(2,1)S(1)}, bf16[2,4,64,256]{3,2,1,0:T(8,128)(2,1)S(1)}, u32[]{:S(2)}, u32[]{:S(2)}) collective-permute-start(bf16[2,4,64,256]{3,2,1,0:T(8,128)(2,1)S(1)} %get-tuple-element.36), channel_id=1, source_target_pairs={{0,14},{2,0},{4,2},{6,4},{8,6},{10,8},{12,10},{14,12},{1,15},{3,1}... | collective-permute-start | bytes 786440 | tf_op jit(solution)/shard_map/ppermute | solution.py:282
  7.7 0.6 %collective-permute-start.2 = (bf16[2,4,8,256]{3,2,1,0:T(8,128)(2,1)S(1)}, bf16[2,4,8,256]{3,2,1,0:T(8,128)(2,1)S(1)}, u32[]{:S(2)}, u32[]{:S(2)}) collective-permute-start(bf16[2,4,8,256]{3,2,1,0:T(8,128)(2,1)S(1)} %get-tuple-element.39), channel_id=1, source_target_pairs={{0,15},{1,14},{2,1},{3,0},{4,3},{5,2},{6,5},{7,4},{8,7},{9,6},{10,... | collective-permute-start | bytes 98312 | tf_op jit(solution)/shard_map/ppermute | solution.py:282
  8.4 1.0 %shard_map.102 = (bf16[256,768]{1,0:T(8,128)(2,1)S(1)}, bf16[256,256]{1,0:T(8,128)(2,1)S(1)}, f32[1,256]{1,0:T(1,128)S(1)}) custom-call(bf16[256,768]{1,0:T(8,128)(2,1)} %wqkv_hbm, bf16[256,256]{1,0:T(8,128)(2,1)} %wproj_hbm, f32[1,256]{1,0:T(1,128)} %bitcast.14), custom_call_target="tpu_custom_call" | custom-call | tf_op jit(solution)/shard_map/pallas_call | solution.py:262
  9.4 4.5 %collective-permute-done.2.corner = bf16[2,4,8,256]{3,2,1,0:T(8,128)(2,1)S(1)} collective-permute-done((bf16[2,4,8,256]{3,2,1,0:T(8,128)(2,1)S(1)}, bf16[2,4,8,256]{3,2,1,0:T(8,128)(2,1)S(1)}, u32[]{:S(2)}, u32[]{:S(2)}) %collective-permute-start.2) | collective-permute-done | bytes 32800 | tf_op jit(solution)/shard_map/ppermute | solution.py:282
  14.0 2.9 %shard_map.103 = (bf16[512,256]{1,0:T(8,128)(2,1)S(1)}, bf16[512,256]{1,0:T(8,128)(2,1)S(1)}, bf16[512,256]{1,0:T(8,128)(2,1)S(1)}, bf16[512,768]{1,0:T(8,128)(2,1)S(1)}) custom-call(bf16[8,64,256]{2,1,0:T(8,128)(2,1)S(1)} %copy-done, bf16[8,64,256]{2,1,0:T(8,128)(2,1)S(1)} %get-tuple-element.34.cot, s32[8,64]{1,0:T(8,128)S(1)} %get-tuple-element.35.domain, ...), custom_call_target="tpu_custom_call" | custom-call | tf_op jit(solution)/shard_map/pallas_call | solution.py:262
  17.0 1.5 %collective-permute-done.3 = bf16[512,256]{1,0:T(8,128)(2,1)S(1)} collective-permute-done((bf16[512,256]{1,0:T(8,128)(2,1)S(1)}, bf16[512,256]{1,0:T(8,128)(2,1)S(1)}, u32[]{:S(2)}, u32[]{:S(2)}) %collective-permute-start.3) | collective-permute-done | bytes 262176 | tf_op jit(solution)/shard_map/ppermute | solution.py:291
  18.7 1.5 %collective-permute-start.5 = (bf16[128,256]{1,0:T(8,128)(2,1)S(1)}, bf16[128,256]{1,0:T(8,128)(2,1)S(1)}, u32[]{:S(2)}, u32[]{:S(2)}) collective-permute-start(bf16[128,256]{1,0:T(8,128)(2,1)S(1)} %get-tuple-element.67), channel_id=1, source_target_pairs={{0,4},{2,6},{4,0},{6,2},{8,12},{10,14},{12,8},{14,10},{1,5},{3,7},... | collective-permute-start | bytes 196616 | tf_op jit(solution)/shard_map/ppermute | solution.py:291
  20.2 1.9 %collective-permute-start.6 = (bf16[128,256]{1,0:T(8,128)(2,1)S(1)}, bf16[128,256]{1,0:T(8,128)(2,1)S(1)}, u32[]{:S(2)}, u32[]{:S(2)}) collective-permute-start(bf16[128,256]{1,0:T(8,128)(2,1)S(1)} %get-tuple-element.66), channel_id=1, source_target_pairs={{0,6},{2,4},{4,2},{6,0},{8,14},{10,12},{12,10},{14,8},{1,7},{3,5},... | collective-permute-start | bytes 196616 | tf_op jit(solution)/shard_map/ppermute | solution.py:291
  22.2 0.4 shard_map.104
  22.6 0.1 collective-permute-start.8
  22.8 0.2 collective-permute-done.4
  23.0 0.5 %collective-permute-done.5 = bf16[128,256]{1,0:T(8,128)(2,1)S(1)} collective-permute-done((bf16[128,256]{1,0:T(8,128)(2,1)S(1)}, bf16[128,256]{1,0:T(8,128)(2,1)S(1)}, u32[]{:S(2)}, u32[]{:S(2)}) %collective-permute-start.5) | collective-permute-done | bytes 65568 | tf_op jit(solution)/shard_map/ppermute | solution.py:291
  23.5 2.0 %collective-permute-done.6 = bf16[128,256]{1,0:T(8,128)(2,1)S(1)} collective-permute-done((bf16[128,256]{1,0:T(8,128)(2,1)S(1)}, bf16[128,256]{1,0:T(8,128)(2,1)S(1)}, u32[]{:S(2)}, u32[]{:S(2)}) %collective-permute-start.6) | collective-permute-done | bytes 65568 | tf_op jit(solution)/shard_map/ppermute | solution.py:291
  25.5 5.8 %collective-permute-start.7 = (bf16[128,256]{1,0:T(8,128)(2,1)S(1)}, bf16[128,256]{1,0:T(8,128)(2,1)S(1)}, u32[]{:S(2)}, u32[]{:S(2)}) collective-permute-start(bf16[128,256]{1,0:T(8,128)(2,1)S(1)} %add_convert_fusion.2), channel_id=1, source_target_pairs={{0,8},{2,10},{4,12},{6,14},{8,0},{10,2},{12,4},{14,6},{1,9},{3,11}... | collective-permute-start | bytes 196616 | tf_op jit(solution)/shard_map/ppermute | solution.py:291
  31.3 2.2 %collective-permute-done.7 = bf16[128,256]{1,0:T(8,128)(2,1)S(1)} collective-permute-done((bf16[128,256]{1,0:T(8,128)(2,1)S(1)}, bf16[128,256]{1,0:T(8,128)(2,1)S(1)}, u32[]{:S(2)}, u32[]{:S(2)}) %collective-permute-start.7) | collective-permute-done | bytes 65568 | tf_op jit(solution)/shard_map/ppermute | solution.py:291
  33.6 1.4 %collective-permute-done.8.both_rows = bf16[2,4,64,256]{3,2,1,0:T(8,128)(2,1)S(1)} collective-permute-done((bf16[2,4,64,256]{3,2,1,0:T(8,128)(2,1)S(1)}, bf16[2,4,64,256]{3,2,1,0:T(8,128)(2,1)S(1)}, u32[]{:S(2)}, u32[]{:S(2)}) %collective-permute-start.8) | collective-permute-done | bytes 262176 | tf_op jit(solution)/shard_map/ppermute | solution.py:287
  35.0 2.3 %collective-permute-start.9 = (bf16[128,256]{1,0:T(8,128)(2,1)S(1)}, bf16[128,256]{1,0:T(8,128)(2,1)S(1)}, u32[]{:S(2)}, u32[]{:S(2)}) collective-permute-start(bf16[128,256]{1,0:T(8,128)(2,1)S(1)} %add_convert_fusion.1), channel_id=1, source_target_pairs={{0,2},{2,0},{4,6},{6,4},{8,10},{10,8},{12,14},{14,12},{1,3},{3,1},... | collective-permute-start | bytes 196616 | tf_op jit(solution)/shard_map/ppermute | solution.py:291
  37.3 1.5 %collective-permute-start.11 = (bf16[128,256]{1,0:T(8,128)(2,1)S(1)}, bf16[128,256]{1,0:T(8,128)(2,1)S(1)}, u32[]{:S(2)}, u32[]{:S(2)}) collective-permute-start(bf16[128,256]{1,0:T(8,128)(2,1)S(1)} %add_convert_fusion.1), channel_id=1, source_target_pairs={{0,6},{2,4},{4,2},{6,0},{8,14},{10,12},{12,10},{14,8},{1,7},{3,5},... | collective-permute-start | bytes 196616 | tf_op jit(solution)/shard_map/ppermute | solution.py:291
  39.0 1.2 %collective-permute-done.12.edges = bf16[4,4,8,256]{3,2,1,0:T(8,128)(2,1)S(1)} collective-permute-done((bf16[4,4,8,256]{3,2,1,0:T(8,128)(2,1)S(1)}, bf16[4,4,8,256]{3,2,1,0:T(8,128)(2,1)S(1)}, u32[]{:S(2)}, u32[]{:S(2)}) %collective-permute-start.12) | collective-permute-done | bytes 65568 | tf_op jit(solution)/shard_map/ppermute | solution.py:287
  40.2 1.5 %shard_map.105 = (bf16[8,64,256]{2,1,0:T(8,128)(2,1)}, bf16[8,64,256]{2,1,0:T(8,128)(2,1)}) custom-call(bf16[8,64,256]{2,1,0:T(8,128)(2,1)S(1)} %copy-done, bf16[8,64,256]{2,1,0:T(8,128)(2,1)S(1)} %get-tuple-element.34.cot, s32[8,64]{1,0:T(8,128)S(1)} %get-tuple-element.35.domain, f32[1,256]{1,0:T(1,128)S(1)} %get-tuple-element.45.gain, ...), custom_call_target="tpu_custom_call" | custom-call | tf_op jit(solution)/shard_map/pallas_call | solution.py:262
  41.8 0.7 %collective-permute-done.11 = bf16[128,256]{1,0:T(8,128)(2,1)S(1)} collective-permute-done((bf16[128,256]{1,0:T(8,128)(2,1)S(1)}, bf16[128,256]{1,0:T(8,128)(2,1)S(1)}, u32[]{:S(2)}, u32[]{:S(2)}) %collective-permute-start.11) | collective-permute-done | bytes 65568 | tf_op jit(solution)/shard_map/ppermute | solution.py:291
  42.6 1.5 %collective-permute-done.13.col_peer = bf16[512,256]{1,0:T(8,128)(2,1)S(1)} collective-permute-done((bf16[512,256]{1,0:T(8,128)(2,1)S(1)}, bf16[512,256]{1,0:T(8,128)(2,1)S(1)}, u32[]{:S(2)}, u32[]{:S(2)}) %collective-permute-start.13) | collective-permute-done | bytes 262176 | tf_op jit(solution)/shard_map/ppermute | solution.py:291
  44.1 1.3 %shard_map.106 = (f32[256,768]{1,0:T(8,128)}, f32[256,256]{1,0:T(8,128)}, f32[1,256]{1,0:T(1,128)}) custom-call(bf16[512,256]{1,0:T(8,128)(2,1)S(1)} %constant_dynamic-update-slice_fusion.half, bf16[512,256]{1,0:T(8,128)(2,1)S(1)} %collective-permute-done.13.col_peer, bf16[256,768]{1,0:T(8,128)(2,1)S(1)} %get-tuple-element.43.wqkv, ...), custom_call_target="tpu_custom_call" | custom-call | tf_op jit(solution)/shard_map/pallas_call | solution.py:262
  (25 shorter events, 0.6 us)
Async XLA Ops:
  1.7 12.3 %collective-permute-start = (bf16[2,4,64,256]{3,2,1,0:T(8,128)(2,1)S(1)}, bf16[2,4,64,256]{3,2,1,0:T(8,128)(2,1)S(1)}, u32[]{:S(2)}, u32[]{:S(2)}) collective-permute-start(bf16[2,4,64,256]{3,2,1,0:T(8,128)(2,1)S(1)} %get-tuple-element.36), channel_id=1, source_target_pairs={{0,14},{2,0},{4,2},{6,4},{8,6},{10,8},{12,10},{14,12},{1,15},{3,1}... | collective-permute-start | bytes 786440 | tf_op jit(solution)/shard_map/ppermute | solution.py:282
  7.7 1.7 %collective-permute-start.1 = (bf16[2,4,8,256]{3,2,1,0:T(8,128)(2,1)S(1)}, bf16[2,4,8,256]{3,2,1,0:T(8,128)(2,1)S(1)}, u32[]{:S(2)}, u32[]{:S(2)}) collective-permute-start(bf16[2,4,8,256]{3,2,1,0:T(8,128)(2,1)S(1)} %get-tuple-element.38), channel_id=1, source_target_pairs={{0,1},{1,0},{2,3},{3,2},{4,5},{5,4},{6,7},{7,6},{8,9},{9,8},{10,11... | collective-permute-start | bytes 98312 | tf_op jit(solution)/shard_map/ppermute | solution.py:282
  7.7 6.3 %copy-start = (bf16[8,64,256]{2,1,0:T(8,128)(2,1)S(1)}, bf16[8,64,256]{2,1,0:T(8,128)(2,1)}, u32[]{:S(2)}) copy-start(bf16[8,64,256]{2,1,0:T(8,128)(2,1)} %feat.5) | copy-start | bytes 786436
  7.7 6.3 %collective-permute-start.2 = (bf16[2,4,8,256]{3,2,1,0:T(8,128)(2,1)S(1)}, bf16[2,4,8,256]{3,2,1,0:T(8,128)(2,1)S(1)}, u32[]{:S(2)}, u32[]{:S(2)}) collective-permute-start(bf16[2,4,8,256]{3,2,1,0:T(8,128)(2,1)S(1)} %get-tuple-element.39), channel_id=1, source_target_pairs={{0,15},{1,14},{2,1},{3,0},{4,3},{5,2},{6,5},{7,4},{8,7},{9,6},{10,... | collective-permute-start | bytes 98312 | tf_op jit(solution)/shard_map/ppermute | solution.py:282
  16.9 1.6 %collective-permute-start.3 = (bf16[512,256]{1,0:T(8,128)(2,1)S(1)}, bf16[512,256]{1,0:T(8,128)(2,1)S(1)}, u32[]{:S(2)}, u32[]{:S(2)}) collective-permute-start(bf16[512,256]{1,0:T(8,128)(2,1)S(1)} %get-tuple-element.47), channel_id=1, source_target_pairs={{0,1},{1,0},{2,3},{3,2},{4,5},{5,4},{6,7},{7,6},{8,9},{9,8},{10,11... | collective-permute-start | bytes 786440 | tf_op jit(solution)/shard_map/ppermute | solution.py:291
  18.6 4.3 %collective-permute-start.4 = (bf16[128,256]{1,0:T(8,128)(2,1)S(1)}, bf16[128,256]{1,0:T(8,128)(2,1)S(1)}, u32[]{:S(2)}, u32[]{:S(2)}) collective-permute-start(bf16[128,256]{1,0:T(8,128)(2,1)S(1)} %get-tuple-element.65), channel_id=1, source_target_pairs={{0,2},{2,0},{4,6},{6,4},{8,10},{10,8},{12,14},{14,12},{1,3},{3,1},... | collective-permute-start | bytes 196616 | tf_op jit(solution)/shard_map/ppermute | solution.py:291
  18.7 4.8 %collective-permute-start.5 = (bf16[128,256]{1,0:T(8,128)(2,1)S(1)}, bf16[128,256]{1,0:T(8,128)(2,1)S(1)}, u32[]{:S(2)}, u32[]{:S(2)}) collective-permute-start(bf16[128,256]{1,0:T(8,128)(2,1)S(1)} %get-tuple-element.67), channel_id=1, source_target_pairs={{0,4},{2,6},{4,0},{6,2},{8,12},{10,14},{12,8},{14,10},{1,5},{3,7},... | collective-permute-start | bytes 196616 | tf_op jit(solution)/shard_map/ppermute | solution.py:291
  20.2 5.2 %collective-permute-start.6 = (bf16[128,256]{1,0:T(8,128)(2,1)S(1)}, bf16[128,256]{1,0:T(8,128)(2,1)S(1)}, u32[]{:S(2)}, u32[]{:S(2)}) collective-permute-start(bf16[128,256]{1,0:T(8,128)(2,1)S(1)} %get-tuple-element.66), channel_id=1, source_target_pairs={{0,6},{2,4},{4,2},{6,0},{8,14},{10,12},{12,10},{14,8},{1,7},{3,5},... | collective-permute-start | bytes 196616 | tf_op jit(solution)/shard_map/ppermute | solution.py:291
  22.6 12.4 %collective-permute-start.8 = (bf16[2,4,64,256]{3,2,1,0:T(8,128)(2,1)S(1)}, bf16[2,4,64,256]{3,2,1,0:T(8,128)(2,1)S(1)}, u32[]{:S(2)}, u32[]{:S(2)}) collective-permute-start(bf16[2,4,64,256]{3,2,1,0:T(8,128)(2,1)S(1)} %get-tuple-element.50), channel_id=1, source_target_pairs={{0,2},{2,4},{4,6},{6,8},{8,10},{10,12},{12,14},{14,0},{1,3},{3,5},... | collective-permute-start | bytes 786440 | tf_op jit(solution)/shard_map/ppermute | solution.py:287
  25.5 8.0 %collective-permute-start.7 = (bf16[128,256]{1,0:T(8,128)(2,1)S(1)}, bf16[128,256]{1,0:T(8,128)(2,1)S(1)}, u32[]{:S(2)}, u32[]{:S(2)}) collective-permute-start(bf16[128,256]{1,0:T(8,128)(2,1)S(1)} %add_convert_fusion.2), channel_id=1, source_target_pairs={{0,8},{2,10},{4,12},{6,14},{8,0},{10,2},{12,4},{14,6},{1,9},{3,11}... | collective-permute-start | bytes 196616 | tf_op jit(solution)/shard_map/ppermute | solution.py:291
  35.0 6.8 %collective-permute-start.9 = (bf16[128,256]{1,0:T(8,128)(2,1)S(1)}, bf16[128,256]{1,0:T(8,128)(2,1)S(1)}, u32[]{:S(2)}, u32[]{:S(2)}) collective-permute-start(bf16[128,256]{1,0:T(8,128)(2,1)S(1)} %add_convert_fusion.1), channel_id=1, source_target_pairs={{0,2},{2,0},{4,6},{6,4},{8,10},{10,8},{12,14},{14,12},{1,3},{3,1},... | collective-permute-start | bytes 196616 | tf_op jit(solution)/shard_map/ppermute | solution.py:291
  37.3 4.5 %collective-permute-start.10 = (bf16[128,256]{1,0:T(8,128)(2,1)S(1)}, bf16[128,256]{1,0:T(8,128)(2,1)S(1)}, u32[]{:S(2)}, u32[]{:S(2)}) collective-permute-start(bf16[128,256]{1,0:T(8,128)(2,1)S(1)} %add_convert_fusion.1), channel_id=1, source_target_pairs={{0,4},{2,6},{4,0},{6,2},{8,12},{10,14},{12,8},{14,10},{1,5},{3,7},... | collective-permute-start | bytes 196616 | tf_op jit(solution)/shard_map/ppermute | solution.py:291
  37.3 5.2 %collective-permute-start.11 = (bf16[128,256]{1,0:T(8,128)(2,1)S(1)}, bf16[128,256]{1,0:T(8,128)(2,1)S(1)}, u32[]{:S(2)}, u32[]{:S(2)}) collective-permute-start(bf16[128,256]{1,0:T(8,128)(2,1)S(1)} %add_convert_fusion.1), channel_id=1, source_target_pairs={{0,6},{2,4},{4,2},{6,0},{8,14},{10,12},{12,10},{14,8},{1,7},{3,5},... | collective-permute-start | bytes 196616 | tf_op jit(solution)/shard_map/ppermute | solution.py:291
  38.9 1.3 %collective-permute-start.12 = (bf16[4,4,8,256]{3,2,1,0:T(8,128)(2,1)S(1)}, bf16[4,4,8,256]{3,2,1,0:T(8,128)(2,1)S(1)}, u32[]{:S(2)}, u32[]{:S(2)}) collective-permute-start(bf16[4,4,8,256]{3,2,1,0:T(8,128)(2,1)S(1)} %pad_maximum_fusion), channel_id=1, source_target_pairs={{0,1},{1,0},{2,3},{3,2},{4,5},{5,4},{6,7},{7,6},{8,9},{9,8},{10,11... | collective-permute-start | bytes 196616 | tf_op jit(solution)/shard_map/ppermute | solution.py:287
  42.5 1.6 %collective-permute-start.13 = (bf16[512,256]{1,0:T(8,128)(2,1)S(1)}, bf16[512,256]{1,0:T(8,128)(2,1)S(1)}, u32[]{:S(2)}, u32[]{:S(2)}) collective-permute-start(bf16[512,256]{1,0:T(8,128)(2,1)S(1)} %constant_dynamic-update-slice_fusion.half), channel_id=1, source_target_pairs={{0,1},{1,0},{2,3},{3,2},{4,5},{5,4},{6,7},{7,6},{8,9},{9,8},{10,11... | collective-permute-start | bytes 786440 | tf_op jit(solution)/shard_map/ppermute | solution.py:291
